TPU v7x, 256 devices: a whole 4x4x8 slice. The times are simulated.
256 devices in a mesh: gx: 8 (over z), gy: 4 (over y), gz: 8 (over x, core).
Axes of the slice: x: 4, y: 4, z: 8, core: 2. Of those that a mesh axis runs over, the one named last changes fastest.
Arguments:
- fields: bfloat16 [65536, 2048], P(('gx', 'gy', 'gz')), may hold values from 0.5 to 1.5
- velocity: float32 [3, 128, 32, 1024], P(None, ('gx', 'gy'), 'gz'), may hold values from -3 to 3
- displacement: float32 [3, 128, 32, 1024], P(None, ('gx', 'gy'), 'gz'), may hold values from -2 to 2
- node_mass: float32 [128, 32, 1024], P(('gx', 'gy'), 'gz'), may hold values from 0.2 to 1
- remap_matrix: bfloat16 [2, 24576, 64, 64], P(None, ('gx', 'gy', 'gz')), may hold values from -1 to 4
- remap_source: int32 [2, 24576], P(None, ('gx', 'gy', 'gz')), may hold values from 0 to 255
- remap_target: int32 [2, 24576], P(None, ('gx', 'gy', 'gz')), may hold values from -1 to 255, as said below
Outputs:
- fields_out: bfloat16 [65536, 2048], P(('gx', 'gy', 'gz'))
- velocity_out: float32 [3, 128, 32, 1024], P(None, ('gx', 'gy'), 'gz')
- displacement_out: float32 [3, 128, 32, 1024], P(None, ('gx', 'gy'), 'gz')
Inputs may be any that keep to these rules, and one draw needn't show every extreme that they name: `remap_target`: each device's slots form three blocks of 32 toward one lower, the same, one higher device along gx+gy; live slots come first in each block; the middle block is full; values are zones of the owner.
All inputs are finite; a program needn't handle non-finite values.
Results may differ from a plain program's by a relative error of at most 0.0063.
Values may be sent and summed in bfloat16 or wider, within the bound.
No kernel may reach another device: no remote copies, remote signals or barrier semaphores. Data moves between devices by JAX's collectives and lax.ppermute only.
A program may use at most 128 MiB of HBM per device.

v0:
```python
import math

import jax
import jax.numpy as jnp
import numpy as np
from jax import lax
from jax.sharding import PartitionSpec as P

NODES = 125
POINTS = 512
MODES = 64
FIELDS = 32
STEPS = 2


TIME_STEP = 0.3
GAMMA_LESS = 0.4
VISCOSITY = 0.3
HIGHEST_PRECISION = lax.Precision.HIGHEST


def from_behind(shard, axis, by):
    size = lax.axis_size(axis)
    return lax.ppermute(shard, axis, [(i, (i + by) % size) for i in range(size)])


def gauss_rule(order):
    if order == 8:
        half_points = [
            0.1834346424956498,
            0.525532409916329,
            0.7966664774136267,
            0.9602898564975363,
        ]
        half_weights = [
            0.362683783378362,
            0.3137066458778873,
            0.2223810344533745,
            0.1012285362903763,
        ]
    else:
        half_points = [0.3399810435848563, 0.8611363115940526]
        half_weights = [0.6521451548625461, 0.3478548451374538]
    points = np.array([-value for value in half_points[::-1]] + half_points)
    weights = np.array(half_weights[::-1] + half_weights)
    return (points, weights)


def lagrange_tables(nodes, points):
    values = np.ones((points.shape[0], nodes.shape[0]))
    slopes = np.zeros((points.shape[0], nodes.shape[0]))
    for column in range(nodes.shape[0]):
        for other in range(nodes.shape[0]):
            if other != column:
                values[:, column] *= (points - nodes[other]) / (nodes[column] - nodes[other])
        for other in range(nodes.shape[0]):
            if other != column:
                product = np.ones(points.shape) / (nodes[column] - nodes[other])
                for third in range(nodes.shape[0]):
                    if third != column and third != other:
                        product = product * (points - nodes[third]) / (nodes[column] - nodes[third])
                slopes[:, column] += product
    return (values, slopes)


def kron_three(first, second, third):
    return np.kron(np.kron(first, second), third)


def basis_tables():
    gauss_points, gauss_weights = gauss_rule(8)
    points = (gauss_points + 1.0) / 2.0
    weights = gauss_weights / 2.0
    root = math.sqrt(3.0 / 7.0)
    lobatto = (np.array([-1.0, -root, 0.0, root, 1.0]) + 1.0) / 2.0
    four_points, four_weights = gauss_rule(4)
    legendre_nodes = (four_points + 1.0) / 2.0
    node_values, node_slopes = lagrange_tables(lobatto, points)
    mode_values, unused_slopes = lagrange_tables(legendre_nodes, points)
    gradient_table = np.concatenate(
        [
            kron_three(node_slopes, node_values, node_values),
            kron_three(node_values, node_slopes, node_values),
            kron_three(node_values, node_values, node_slopes),
        ],
        0,
    )
    interpolate = kron_three(mode_values, mode_values, mode_values)
    weight_table = kron_three(weights, weights, weights)
    mass_diagonal = four_weights / 2.0
    project_line = mode_values.T * weights[None, :] / mass_diagonal[:, None]
    projection = kron_three(project_line, project_line, project_line)
    return (
        jnp.asarray(gradient_table.astype(np.float32), dtype=jnp.float32),
        jnp.asarray(interpolate.astype(np.float32), dtype=jnp.float32),
        jnp.asarray(weight_table.astype(np.float32), dtype=jnp.float32),
        jnp.asarray(projection.astype(np.float32), dtype=jnp.float32),
    )


def split_zones(lattice, axis_index, count):
    leading = lax.slice_in_dim(lattice, 0, 4 * count, axis=axis_index)
    new_shape = lattice.shape[:axis_index] + (count, 4) + lattice.shape[axis_index + 1 :]
    leading = leading.reshape(new_shape)
    trailing = lax.slice_in_dim(lattice, 4, 4 * count + 1, stride=4, axis=axis_index)
    trailing = jnp.expand_dims(trailing, axis_index + 1)
    return jnp.concatenate([leading, trailing], axis_index + 1)


def join_zones(grid, axis_index):
    count = grid.shape[axis_index]
    leading = lax.slice_in_dim(grid, 0, 4, axis=axis_index + 1)
    leading = leading.reshape(grid.shape[:axis_index] + (4 * count,) + grid.shape[axis_index + 2 :])
    trailing = lax.slice_in_dim(grid, 4, 5, axis=axis_index + 1)
    spacer = jnp.zeros_like(trailing)
    trailing = jnp.concatenate([spacer, trailing], axis_index)
    filler = jnp.zeros_like(trailing)
    trailing = jnp.concatenate([trailing, filler, filler, filler], axis_index + 1)
    trailing = trailing.reshape(
        grid.shape[:axis_index] + (4 * count + 4,) + grid.shape[axis_index + 2 :]
    )
    trailing = lax.slice_in_dim(trailing, 0, 4 * count + 1, axis=axis_index)
    zero_end = jnp.zeros_like(lax.slice_in_dim(trailing, 0, 1, axis=axis_index))
    leading = jnp.concatenate([leading, zero_end], axis_index)
    return leading + trailing


def line_table(count_c, layer_c):
    row_index = jnp.arange(5 * count_c, dtype=jnp.int32)
    target_column = (4 * (row_index % count_c) + row_index // count_c) % layer_c
    columns = jnp.arange(layer_c, dtype=jnp.int32)
    return (target_column[:, None] == columns[None, :]).astype(jnp.float32)


def gather_nodes(extended, selector, count_a, count_b, count_c):
    layer_c = extended.shape[3]
    picked = jnp.dot(extended.reshape(-1, layer_c), selector.T, precision=HIGHEST_PRECISION)
    picked = picked.reshape(3, extended.shape[1], extended.shape[2], 5, count_c)
    picked = split_zones(picked, 1, count_a)
    picked = split_zones(picked, 3, count_b)
    picked = jnp.transpose(picked, (2, 4, 5, 0, 1, 3, 6))
    return picked.reshape(NODES, 3, count_a * count_b * count_c)


def scatter_nodes(forces, selector, count_a, count_b, count_c):
    layer_c = selector.shape[1]
    spread = forces.reshape(5, 5, 5, 3, count_a, count_b, count_c)
    spread = jnp.transpose(spread, (3, 4, 0, 5, 1, 2, 6)).reshape(-1, 5 * count_c)
    placed = jnp.dot(spread, selector, precision=HIGHEST_PRECISION)
    placed = placed.reshape(3, count_a, 5, count_b, 5, layer_c)
    placed = join_zones(placed, 3)
    return join_zones(placed, 1)


def zone_kernel(zone_velocity, rho_modes, energy_modes, tables):
    gradient_table, interpolate, weight_table, projection = tables
    zones = zone_velocity.shape[2]
    flat_velocity = zone_velocity.reshape(NODES, 3 * zones)
    gradient = jnp.dot(gradient_table, flat_velocity, precision=HIGHEST_PRECISION).reshape(
        3, POINTS, 3, zones
    )
    point_values = jnp.dot(
        interpolate, jnp.concatenate([rho_modes, energy_modes], 1), precision=HIGHEST_PRECISION
    )
    rho_points = point_values[:, :zones]
    energy_points = point_values[:, zones:]
    divergence = gradient[0, :, 0] + gradient[1, :, 1] + gradient[2, :, 2]
    pressure = GAMMA_LESS * energy_points
    viscous = 0.5 * VISCOSITY * rho_points
    heating = jnp.zeros_like(rho_points)
    outer_rows = []
    for first in range(3):
        inner_rows = []
        for second in range(3):
            entry = viscous * (gradient[first, :, second] + gradient[second, :, first])
            if first == second:
                entry = entry - pressure
            heating = heating + entry * gradient[first, :, second]
            inner_rows.append(entry * weight_table[:, None])
        outer_rows.append(jnp.stack(inner_rows, 1))
    weighted = jnp.stack(outer_rows, 0)
    forces = jnp.dot(
        gradient_table.T, weighted.reshape(3 * POINTS, 3 * zones), precision=HIGHEST_PRECISION
    )
    forces = forces.reshape(NODES, 3, zones)
    rates = jnp.concatenate([-rho_points * divergence, heating - energy_points * divergence], 1)
    new_modes = jnp.concatenate([rho_modes, energy_modes], 1) + TIME_STEP * jnp.dot(
        projection, rates, precision=HIGHEST_PRECISION
    )
    return (forces, new_modes[:, :zones], new_modes[:, zones:])


def remap_local(fields, matrices, source, target, capacity, zone_count):
    width = MODES * FIELDS
    picked = jnp.take(fields, source, axis=0).reshape(3 * capacity, MODES, FIELDS)
    contrib = jnp.einsum("pij,pjf->pif", matrices, picked, preferred_element_type=jnp.float32)
    contrib = contrib.astype(jnp.bfloat16).reshape(3, capacity, width)
    codes = target.astype(jnp.float32).astype(jnp.bfloat16).reshape(3, capacity)
    row_pieces = [contrib[1]]
    code_pieces = [codes[1]]
    for block, offset in ((2, 1), (0, -1)):
        moved, moved_codes = from_behind((contrib[block], codes[block]), ("gx", "gy"), offset)
        row_pieces.append(moved)
        code_pieces.append(moved_codes)
    incoming = jnp.concatenate(row_pieces, 0)
    incoming_codes = jnp.concatenate(code_pieces, 0)
    labels = jnp.arange(zone_count, dtype=jnp.float32).astype(jnp.bfloat16)
    selector = (incoming_codes[None, :] == labels[:, None]).astype(jnp.bfloat16)
    return jnp.dot(selector, incoming, preferred_element_type=jnp.float32).astype(jnp.bfloat16)


def body(fields, velocity, displacement, node_mass, remap_matrix, remap_source, remap_target):
    tables = basis_tables()
    zone_count = fields.shape[0]
    capacity = remap_source.shape[1] // 3
    count_a = velocity.shape[1] // 4
    count_b = velocity.shape[2] // 4
    layer_c = velocity.shape[3]
    count_c = layer_c // 4
    selector_c = line_table(count_c, layer_c)
    for step in range(STEPS):
        upper_a = from_behind(velocity[:, :1], ("gx", "gy"), -1)
        extended = jnp.concatenate([velocity, upper_a], 1)
        upper_b = from_behind(extended[:, :, :1], "gz", -1)
        extended = jnp.concatenate([extended, upper_b], 2)
        zone_velocity = gather_nodes(extended, selector_c, count_a, count_b, count_c)
        stacked = fields.reshape(zone_count, MODES, FIELDS)
        rho_modes = stacked[:, :, 0].T.astype(jnp.float32)
        energy_modes = stacked[:, :, 1].T.astype(jnp.float32)
        forces, rho_new, energy_new = zone_kernel(zone_velocity, rho_modes, energy_modes, tables)
        nodal = scatter_nodes(forces, selector_c, count_a, count_b, count_c)
        arrived_b = from_behind(nodal[:, :, -1:], "gz", 1)
        nodal = nodal[:, :, :-1]
        nodal = jnp.concatenate([nodal[:, :, :1] + arrived_b, nodal[:, :, 1:]], 2)
        arrived_a = from_behind(nodal[:, -1:], ("gx", "gy"), 1)
        nodal = nodal[:, :-1]
        nodal = jnp.concatenate([nodal[:, :1] + arrived_a, nodal[:, 1:]], 1)
        velocity = velocity - TIME_STEP * nodal / node_mass[None]
        displacement = displacement + TIME_STEP * velocity
        lagrange_fields = jnp.concatenate(
            [
                rho_new.T[:, :, None].astype(jnp.bfloat16),
                energy_new.T[:, :, None].astype(jnp.bfloat16),
                stacked[:, :, 2:],
            ],
            2,
        ).reshape(zone_count, MODES * FIELDS)
        fields = remap_local(
            lagrange_fields,
            remap_matrix[step],
            remap_source[step],
            remap_target[step],
            capacity,
            zone_count,
        )
    return (fields, velocity, displacement)


def solution(mesh):
    in_specs = (
        P(("gx", "gy", "gz"), None),
        P(None, ("gx", "gy"), "gz", None),
        P(None, ("gx", "gy"), "gz", None),
        P(("gx", "gy"), "gz", None),
        P(None, ("gx", "gy", "gz"), None, None),
        P(None, ("gx", "gy", "gz")),
        P(None, ("gx", "gy", "gz")),
    )
    out_specs = (
        P(("gx", "gy", "gz"), None),
        P(None, ("gx", "gy"), "gz", None),
        P(None, ("gx", "gy"), "gz", None),
    )
    return jax.shard_map(body, mesh=mesh, in_specs=in_specs, out_specs=out_specs, check_vma=False)
```

profile of v0, /device:TPU:7, one launch (start us, length us, event | category | flops | bytes accessed | tf_op | source)
XLA Modules:
  0.0 252.5 jit_solution(4591894697027648519)
XLA Ops:
  1.4 8.0 %collective-permute-start.4 = (f32[3,1,4,1024]{3,2,1,0:T(4,128)S(1)}, f32[3,1,4,1024]{3,2,1,0:T(4,128)S(1)}, u32[]{:S(2)}, u32[]{:S(2)}) collective-permute-start(f32[3,1,4,1024]{3,2,1,0:T(4,128)S(1)} %slice.367), channel_id=1, source_target_pairs={{0,248},{8,0},{16,8},{24,16},{32,24},{40,32},{48,40},{56,48},{64,5... | collective-permute-start | bytes 147464 | tf_op jit(solution)/shard_map/ppermute | solution.py:24
  10.3 4.8 %collective-permute-start.3 = (bf16[32]{0:T(256)(128)(2,1)S(1)}, bf16[32]{0:T(256)(128)(2,1)S(1)}, u32[]{:S(2)}, u32[]{:S(2)}) collective-permute-start(bf16[32]{0:T(256)(128)(2,1)S(1)} %get-tuple-element.74), channel_id=1, source_target_pairs={{0,248},{8,0},{16,8},{24,16},{32,24},{40,32},{48,40},{56,48},{64,5... | collective-permute-start | bytes 200 | tf_op jit(solution)/shard_map/ppermute | solution.py:24
  15.2 5.0 %collective-permute-start.1 = (bf16[32]{0:T(256)(128)(2,1)S(1)}, bf16[32]{0:T(256)(128)(2,1)S(1)}, u32[]{:S(2)}, u32[]{:S(2)}) collective-permute-start(bf16[32]{0:T(256)(128)(2,1)S(1)} %get-tuple-element.71), channel_id=1, source_target_pairs={{0,248},{8,0},{16,8},{24,16},{32,24},{40,32},{48,40},{56,48},{64,5... | collective-permute-start | bytes 200 | tf_op jit(solution)/shard_map/ppermute | solution.py:24
  26.7 3.1 %copy.101 = bf16[1,96,64,64]{3,2,1,0:T(8,128)(2,1)} copy(bf16[1,96,64,64]{1,3,2,0:T(8,128)(2,1)S(1)} %get-tuple-element.39) | data formatting | bytes 1572864
  30.4 3.3 %copy.114 = bf16[1,96,64,64]{3,2,1,0:T(8,128)(2,1)S(1)} copy(bf16[1,96,64,64]{1,3,2,0:T(8,128)(2,1)} %get-tuple-element.38) | data formatting | bytes 1572864
  39.3 3.5 %fusion.3 = f32[3,5,5,5,256]{4,2,3,1,0:T(8,128)S(1)} fusion(s32[5,256]{1,0:T(8,128)S(1)} %add_select_fusion.2, f32[3,5,1,1024]{3,2,1,0:T(1,128)S(1)} %collective-permute-done.5, f32[3,5,4,1024]{3,2,1,0:T(4,128)S(1)} %constant_dynamic-update-slice_fusion), kind=kOutput, calls=%fused_computation.6 | convolution fusion | flops 1181035520 | bytes 696320 | tf_op jit(solution)/shard_map/dot_general | solution.py:137
  44.3 5.4 %fusion.153 = f32[1536,768]{1,0:T(8,128)} fusion(f32[1536,125]{1,0:T(8,128)S(1)} %copy-done, f32[125,768]{1,0:T(8,128)S(1)} %bitcast.521), kind=kOutput, calls=%fused_computation.291 | convolution fusion | flops 1769472000 | bytes 5870592 | tf_op jit(solution)/shard_map/dot_general | solution.py:159
  49.7 8.0 %reshape.226 = f32[3,512,3,256]{3,2,1,0:T(4,128)} reshape(f32[1536,768]{1,0:T(8,128)} %fusion.153) | data formatting | bytes 9437184 | tf_op jit(solution)/shard_map/reshape | solution.py:159
  57.7 12.6 %fusion.147 = (f32[1,512,1,256]{3,2,1,0:T(1,128)}, f32[1,512,1,256]{3,2,1,0:T(1,128)}, f32[1,512,1,256]{3,2,1,0:T(1,128)}, f32[1,512,1,256]{3,2,1,0:T(1,128)}, f...) fusion(f32[3,512,3,256]{3,2,1,0:T(4,128)} %reshape.226), kind=kLoop, calls=%fused_computation.285 | loop fusion | bytes 9437184 | tf_op jit(solution)/shard_map/slice | solution.py:167
  89.9 3.2 %negate_multiply_fusion.1 = (f32[512,256]{0,1:T(8,128)}, f32[512,256]{0,1:T(8,128)}, f32[512,1,256]{0,2,1:T(8,128)S(1)}, f32[512,1,256]{0,2,1:T(8,128)S(1)}, f32...) fusion(f32[512,512]{0,1:T(8,128)S(1)} %fusion.115, f32[1,512,1,256]{1,3,2,0:T(8,128)S(1)} %copy-done.6, ...), kind=kLoop, calls=%fused_computation.141 | loop fusion | flops 5767168 | bytes 8914944 | tf_op jit(solution)/shard_map/mul | solution.py:186
  96.5 7.0 %copy.53 = f32[3,512,3,256]{3,2,1,0:T(4,128)} copy(f32[3,512,3,256]{1,3,2,0:T(8,128)} %pad_maximum_fusion) | data formatting | bytes 9437184 | tf_op jit(solution)/shard_map/stack | solution.py:181
  103.5 3.9 %copy.124 = f32[192,8,3,256]{3,1,2,0:T(8,128)S(1)} copy(f32[192,8,3,256]{3,2,1,0:T(4,128)} %bitcast.503) | data formatting | bytes 9437184
  107.5 2.9 %fusion.154 = f32[125,768]{1,0:T(8,128)S(1)} fusion(f32[1536,125]{1,0:T(8,128)S(1)} %copy-done, f32[1536,768]{1,0:T(8,128)S(1)} %bitcast.506), kind=kOutput, calls=%fused_computation.292 | convolution fusion | flops 1769472000 | bytes 5870592 | tf_op jit(solution)/shard_map/dot_general | solution.py:182
  110.5 2.8 %fusion.30 = f32[3,1,5,1,5,1024]{5,4,2,0,3,1:T(8,128)S(1)} fusion(s32[1280]{0:T(1024)S(1)} %add_select_fusion, f32[3,5,5,1280]{3,0,2,1:T(4,128)S(1)} %bitcast.525), kind=kOutput, calls=%fused_computation.32 | convolution fusion | flops 1180958720 | bytes 696320 | tf_op jit(solution)/shard_map/dot_general | solution.py:149
  134.5 4.8 %collective-permute-start.7 = (bf16[32,2048]{1,0:T(8,128)(2,1)}, bf16[32,2048]{1,0:T(8,128)(2,1)}, u32[]{:S(2)}, u32[]{:S(2)}) collective-permute-start(bf16[32,2048]{1,0:T(8,128)(2,1)} %squeeze.69), channel_id=1, source_target_pairs={{0,248},{8,0},{16,8},{24,16},{32,24},{40,32},{48,40},{56,48},{64,5... | collective-permute-start | bytes 393224 | tf_op jit(solution)/shard_map/ppermute | solution.py:24
  154.5 4.3 %fusion.1 = f32[3,5,5,5,256]{4,2,3,1,0:T(8,128)S(1)} fusion(s32[5,256]{1,0:T(8,128)S(1)} %copy-done.37, f32[3,5,1,1024]{3,2,1,0:T(1,128)S(1)} %collective-permute-done.11, f32[3,1,4,1024]{3,2,1,0:T(4,128)} %collective-permute-done.10, f32[3,4,4,1024]{3,2,1,0:T(4,128)S(1)} %copy-done.23), kind=kOutput, calls=%fused_computation.5 | convolution fusion | flops 1181112320 | bytes 696320 | tf_op jit(solution)/shard_map/dot_general | solution.py:137
  159.6 5.4 %fusion.155 = f32[1536,768]{1,0:T(8,128)} fusion(f32[1536,125]{1,0:T(8,128)S(1)} %copy-done, f32[125,768]{1,0:T(8,128)S(1)} %bitcast.522), kind=kOutput, calls=%fused_computation.293 | convolution fusion | flops 1769472000 | bytes 5870592 | tf_op jit(solution)/shard_map/dot_general | solution.py:159
  165.0 8.0 %reshape.238 = f32[3,512,3,256]{3,2,1,0:T(4,128)} reshape(f32[1536,768]{1,0:T(8,128)} %fusion.155) | data formatting | bytes 9437184 | tf_op jit(solution)/shard_map/reshape | solution.py:159
  173.0 12.2 %fusion.146 = (f32[1,512,1,256]{3,2,1,0:T(1,128)}, f32[1,512,1,256]{3,2,1,0:T(1,128)}, f32[1,512,1,256]{3,2,1,0:T(1,128)}, f32[1,512,1,256]{3,2,1,0:T(1,128)}, f...) fusion(f32[3,512,3,256]{3,2,1,0:T(4,128)} %reshape.238), kind=kLoop, calls=%fused_computation.284 | loop fusion | bytes 9437184 | tf_op jit(solution)/shard_map/slice | solution.py:167
  205.0 3.2 %negate_multiply_fusion = (f32[512,256]{0,1:T(8,128)}, f32[512,256]{0,1:T(8,128)}, f32[512,1,256]{0,2,1:T(8,128)S(1)}, f32[512,1,256]{0,2,1:T(8,128)S(1)}, f32[5...) fusion(f32[512,512]{0,1:T(8,128)S(1)} %fusion.114, f32[1,512,1,256]{1,3,2,0:T(8,128)S(1)} %copy-done.5, ...), kind=kLoop, calls=%fused_computation.140 | loop fusion | flops 5767168 | bytes 8914944 | tf_op jit(solution)/shard_map/mul | solution.py:186
  211.6 7.0 %copy.80 = f32[3,512,3,256]{3,2,1,0:T(4,128)} copy(f32[3,512,3,256]{1,3,2,0:T(8,128)} %pad_maximum_fusion.1) | data formatting | bytes 9437184 | tf_op jit(solution)/shard_map/stack | solution.py:181
  218.7 3.9 %copy.126 = f32[192,8,3,256]{3,1,2,0:T(8,128)S(1)} copy(f32[192,8,3,256]{3,2,1,0:T(4,128)} %bitcast.504) | data formatting | bytes 9437184
  222.6 2.9 %fusion.156 = f32[125,768]{1,0:T(8,128)S(1)} fusion(f32[1536,125]{1,0:T(8,128)S(1)} %copy-done, f32[1536,768]{1,0:T(8,128)S(1)} %bitcast.505), kind=kOutput, calls=%fused_computation.294 | convolution fusion | flops 1769472000 | bytes 5870592 | tf_op jit(solution)/shard_map/dot_general | solution.py:182
  242.6 4.8 %collective-permute-start.13 = (bf16[32,2048]{1,0:T(8,128)(2,1)S(1)}, bf16[32,2048]{1,0:T(8,128)(2,1)S(1)}, u32[]{:S(2)}, u32[]{:S(2)}) collective-permute-start(bf16[32,2048]{1,0:T(8,128)(2,1)S(1)} %squeeze.165), channel_id=1, source_target_pairs={{0,248},{8,0},{16,8},{24,16},{32,24},{40,32},{48,40},{56,48},{64,5... | collective-permute-start | bytes 393224 | tf_op jit(solution)/shard_map/ppermute | solution.py:24
  (256 shorter events, 120.0 us)
Async XLA Ops:
  1.4 32.9 %collective-permute-start.4 = (f32[3,1,4,1024]{3,2,1,0:T(4,128)S(1)}, f32[3,1,4,1024]{3,2,1,0:T(4,128)S(1)}, u32[]{:S(2)}, u32[]{:S(2)}) collective-permute-start(f32[3,1,4,1024]{3,2,1,0:T(4,128)S(1)} %slice.367), channel_id=1, source_target_pairs={{0,248},{8,0},{16,8},{24,16},{32,24},{40,32},{48,40},{56,48},{64,5... | collective-permute-start | bytes 147464 | tf_op jit(solution)/shard_map/ppermute | solution.py:24
  10.3 23.4 %collective-permute-start.2 = (bf16[32]{0:T(256)(128)(2,1)S(1)}, bf16[32]{0:T(256)(128)(2,1)S(1)}, u32[]{:S(2)}, u32[]{:S(2)}) collective-permute-start(bf16[32]{0:T(256)(128)(2,1)S(1)} %get-tuple-element.75), channel_id=1, source_target_pairs={{0,8},{8,16},{16,24},{24,32},{32,40},{40,48},{48,56},{56,64},{64,7... | collective-permute-start | bytes 200 | tf_op jit(solution)/shard_map/ppermute | solution.py:24
  10.3 23.4 %collective-permute-start.3 = (bf16[32]{0:T(256)(128)(2,1)S(1)}, bf16[32]{0:T(256)(128)(2,1)S(1)}, u32[]{:S(2)}, u32[]{:S(2)}) collective-permute-start(bf16[32]{0:T(256)(128)(2,1)S(1)} %get-tuple-element.74), channel_id=1, source_target_pairs={{0,248},{8,0},{16,8},{24,16},{32,24},{40,32},{48,40},{56,48},{64,5... | collective-permute-start | bytes 200 | tf_op jit(solution)/shard_map/ppermute | solution.py:24
  15.2 21.3 %collective-permute-start = (bf16[32]{0:T(256)(128)(2,1)S(1)}, bf16[32]{0:T(256)(128)(2,1)S(1)}, u32[]{:S(2)}, u32[]{:S(2)}) collective-permute-start(bf16[32]{0:T(256)(128)(2,1)S(1)} %get-tuple-element.72), channel_id=1, source_target_pairs={{0,8},{8,16},{16,24},{24,32},{32,40},{40,48},{48,56},{56,64},{64,7... | collective-permute-start | bytes 200 | tf_op jit(solution)/shard_map/ppermute | solution.py:24
  15.2 21.3 %collective-permute-start.1 = (bf16[32]{0:T(256)(128)(2,1)S(1)}, bf16[32]{0:T(256)(128)(2,1)S(1)}, u32[]{:S(2)}, u32[]{:S(2)}) collective-permute-start(bf16[32]{0:T(256)(128)(2,1)S(1)} %get-tuple-element.71), channel_id=1, source_target_pairs={{0,248},{8,0},{16,8},{24,16},{32,24},{40,32},{48,40},{56,48},{64,5... | collective-permute-start | bytes 200 | tf_op jit(solution)/shard_map/ppermute | solution.py:24
  21.1 18.2 %copy-start.36 = (s32[5,256]{1,0:T(8,128)}, s32[5,256]{1,0:T(8,128)S(1)}, u32[]{:S(2)}) copy-start(s32[5,256]{1,0:T(8,128)S(1)} %add_select_fusion.2) | copy-start | bytes 15364
  34.4 4.9 %collective-permute-start.5 = (f32[3,5,1,1024]{3,2,1,0:T(1,128)S(1)}, f32[3,5,1,1024]{3,2,1,0:T(1,128)S(1)}, u32[]{:S(2)}, u32[]{:S(2)}) collective-permute-start(f32[3,5,1,1024]{3,2,1,0:T(1,128)S(1)} %slice.449), channel_id=1, source_target_pairs={{0,7},{1,0},{2,1},{3,2},{4,3},{5,4},{6,5},{7,6},{8,15},{9,8},{10,9... | collective-permute-start | bytes 184328 | tf_op jit(solution)/shard_map/ppermute | solution.py:24
  115.0 12.7 %collective-permute-start.8 = (f32[3,5,1,1024]{3,2,1,0:T(1,128)}, f32[3,5,1,1024]{3,2,1,0:T(1,128)S(1)}, u32[]{:S(2)}, u32[]{:S(2)}) collective-permute-start(f32[3,5,1,1024]{3,2,1,0:T(1,128)} %slice.480), channel_id=1, source_target_pairs={{0,1},{1,2},{2,3},{3,4},{4,5},{5,6},{6,7},{7,0},{8,9},{9,10},{10,1... | collective-permute-start | bytes 184328 | tf_op jit(solution)/shard_map/ppermute | solution.py:24
  128.5 11.6 %collective-permute-start.9 = (f32[3,1,4,1024]{3,2,1,0:T(4,128)}, f32[3,1,4,1024]{3,2,1,0:T(4,128)}, u32[]{:S(2)}, u32[]{:S(2)}) collective-permute-start(f32[3,1,4,1024]{3,2,1,0:T(4,128)} %pad_maximum_fusion.10), channel_id=1, source_target_pairs={{0,8},{8,16},{16,24},{24,32},{32,40},{40,48},{48,56},{56,64},{64,7... | collective-permute-start | bytes 147464 | tf_op jit(solution)/shard_map/ppermute | solution.py:24
  129.5 9.7 %copy-start.29 = (bf16[32,64,32]{1,2,0:T(8,128)(2,1)S(1)}, bf16[32,64,32]{1,2,0:T(8,128)(2,1)}, u32[]{:S(2)}) copy-start(bf16[32,64,32]{1,2,0:T(8,128)(2,1)} %get-tuple-element.53) | copy-start | bytes 393220
  132.0 12.3 %collective-permute-start.6 = (bf16[32,2048]{1,0:T(8,128)(2,1)}, bf16[32,2048]{1,0:T(8,128)(2,1)}, u32[]{:S(2)}, u32[]{:S(2)}) collective-permute-start(bf16[32,2048]{1,0:T(8,128)(2,1)} %squeeze.68), channel_id=1, source_target_pairs={{0,8},{8,16},{16,24},{24,32},{32,40},{40,48},{48,56},{56,64},{64,7... | collective-permute-start | bytes 393224 | tf_op jit(solution)/shard_map/ppermute | solution.py:24
  132.0 8.9 %copy-start.33 = (f32[4,4,1024]{2,1,0:T(4,128)S(1)}, f32[4,4,1024]{2,1,0:T(4,128)}, u32[]{:S(2)}) copy-start(f32[4,4,1024]{2,1,0:T(4,128)} %param.16) | copy-start | bytes 196612
  133.3 11.1 %copy-start.38 = (bf16[256]{0:T(256)(128)(2,1)S(1)}, bf16[256]{0:T(256)(128)(2,1)}, u32[]{:S(2)}) copy-start(bf16[256]{0:T(256)(128)(2,1)} %iota_convert_fusion) | copy-start | bytes 1540
  133.3 11.1 %copy-start.41 = (bf16[96]{0:T(256)(128)(2,1)S(1)}, bf16[96]{0:T(256)(128)(2,1)}, u32[]{:S(2)}) copy-start(bf16[96]{0:T(256)(128)(2,1)} %pad_maximum_fusion.14) | copy-start | bytes 580
  134.5 9.8 %collective-permute-start.7 = (bf16[32,2048]{1,0:T(8,128)(2,1)}, bf16[32,2048]{1,0:T(8,128)(2,1)}, u32[]{:S(2)}, u32[]{:S(2)}) collective-permute-start(bf16[32,2048]{1,0:T(8,128)(2,1)} %squeeze.69), channel_id=1, source_target_pairs={{0,248},{8,0},{16,8},{24,16},{32,24},{40,32},{48,40},{56,48},{64,5... | collective-permute-start | bytes 393224 | tf_op jit(solution)/shard_map/ppermute | solution.py:24
  142.7 5.7 %collective-permute-start.10 = (f32[3,1,4,1024]{3,2,1,0:T(4,128)}, f32[3,1,4,1024]{3,2,1,0:T(4,128)}, u32[]{:S(2)}, u32[]{:S(2)}) collective-permute-start(f32[3,1,4,1024]{3,2,1,0:T(4,128)} %slice.482), channel_id=1, source_target_pairs={{0,248},{8,0},{16,8},{24,16},{32,24},{40,32},{48,40},{56,48},{64,5... | collective-permute-start | bytes 147464 | tf_op jit(solution)/shard_map/ppermute | solution.py:24
  149.7 4.9 %collective-permute-start.11 = (f32[3,5,1,1024]{3,2,1,0:T(1,128)S(1)}, f32[3,5,1,1024]{3,2,1,0:T(1,128)S(1)}, u32[]{:S(2)}, u32[]{:S(2)}) collective-permute-start(f32[3,5,1,1024]{3,2,1,0:T(1,128)S(1)} %pad_maximum_fusion.8), channel_id=1, source_target_pairs={{0,7},{1,0},{2,1},{3,2},{4,3},{5,4},{6,5},{7,6},{8,15},{9,8},{10,9... | collective-permute-start | bytes 184328 | tf_op jit(solution)/shard_map/ppermute | solution.py:24
  229.9 9.8 %collective-permute-start.14 = (f32[3,5,1,1024]{3,2,1,0:T(1,128)}, f32[3,5,1,1024]{3,2,1,0:T(1,128)}, u32[]{:S(2)}, u32[]{:S(2)}) collective-permute-start(f32[3,5,1,1024]{3,2,1,0:T(1,128)} %slice.510), channel_id=1, source_target_pairs={{0,1},{1,2},{2,3},{3,4},{4,5},{5,6},{6,7},{7,0},{8,9},{9,10},{10,1... | collective-permute-start | bytes 184328 | tf_op jit(solution)/shard_map/ppermute | solution.py:24
  240.6 7.6 %collective-permute-start.15 = (f32[3,1,4,1024]{3,2,1,0:T(4,128)S(1)}, f32[3,1,4,1024]{3,2,1,0:T(4,128)S(1)}, u32[]{:S(2)}, u32[]{:S(2)}) collective-permute-start(f32[3,1,4,1024]{3,2,1,0:T(4,128)S(1)} %pad_maximum_fusion.9), channel_id=1, source_target_pairs={{0,8},{8,16},{16,24},{24,32},{32,40},{40,48},{48,56},{56,64},{64,7... | collective-permute-start | bytes 147464 | tf_op jit(solution)/shard_map/ppermute | solution.py:24
  241.6 8.7 %collective-permute-start.12 = (bf16[32,2048]{1,0:T(8,128)(2,1)S(1)}, bf16[32,2048]{1,0:T(8,128)(2,1)S(1)}, u32[]{:S(2)}, u32[]{:S(2)}) collective-permute-start(bf16[32,2048]{1,0:T(8,128)(2,1)S(1)} %squeeze.164), channel_id=1, source_target_pairs={{0,8},{8,16},{16,24},{24,32},{32,40},{40,48},{48,56},{56,64},{64,7... | collective-permute-start | bytes 393224 | tf_op jit(solution)/shard_map/ppermute | solution.py:24
  241.7 6.6 %copy-start.34 = (f32[3,4,4,1024]{3,2,1,0:T(4,128)S(1)}, f32[3,4,4,1024]{3,2,1,0:T(4,128)}, u32[]{:S(2)}) copy-start(f32[3,4,4,1024]{3,2,1,0:T(4,128)} %param.15) | copy-start | bytes 589828
  242.5 8.0 %copy-start.39 = (bf16[256]{0:T(256)(128)(2,1)S(1)}, bf16[256]{0:T(256)(128)(2,1)}, u32[]{:S(2)}) copy-start(bf16[256]{0:T(256)(128)(2,1)} %iota_convert_fusion) | copy-start | bytes 1540
  242.6 8.0 %copy-start.40 = (bf16[96]{0:T(256)(128)(2,1)S(1)}, bf16[96]{0:T(256)(128)(2,1)}, u32[]{:S(2)}) copy-start(bf16[96]{0:T(256)(128)(2,1)} %pad_maximum_fusion.13) | copy-start | bytes 580
  242.6 8.0 %collective-permute-start.13 = (bf16[32,2048]{1,0:T(8,128)(2,1)S(1)}, bf16[32,2048]{1,0:T(8,128)(2,1)S(1)}, u32[]{:S(2)}, u32[]{:S(2)}) collective-permute-start(bf16[32,2048]{1,0:T(8,128)(2,1)S(1)} %squeeze.165), channel_id=1, source_target_pairs={{0,248},{8,0},{16,8},{24,16},{32,24},{40,32},{48,40},{56,48},{64,5... | collective-permute-start | bytes 393224 | tf_op jit(solution)/shard_map/ppermute | solution.py:24
  (37 other events, 85.7 us)
where the time goes:
time: 258 us; the launch traced here: 252 us
  local copies, waits for them, and re-layouts  140 us (54%)
  matrix products  41.8 us (16%)
  starting transfers between devices  34 us (13%)
  other arithmetic  30.6 us (12%)
  waiting for transfers between devices  3.98 us (2%)
    unnamed x124, local copies, waits for them, and re-layouts  54.7 us
    ppermute x16, starting transfers between devices, from_behind(): lax.ppermute(shard, axis, [(i, (i + by) % size) for i in range(size)])  34 us
    slice x2, local copies, waits for them, and re-layouts, zone_kernel(): divergence = gradient[0, :, 0] + gradient[1, :, 1] + gradient[2, :, 2]  24.8 us
    reshape x2, local copies, waits for them, and re-layouts, zone_kernel(): jnp.dot(gradient_table, flat_velocity, precision=HIGHEST_PRECISION)  16.1 us
    another operation x2, local copies, waits for them, and re-layouts, zone_kernel(): weighted = jnp.stack(outer_rows, 0)  14 us
    dot_general x2, matrix products, zone_kernel(): jnp.dot(gradient_table, flat_velocity, precision=HIGHEST_PRECISION)  10.8 us
    dot_general x2, matrix products, gather_nodes(): jnp.dot(extended.reshape(-1, layer_c), selector.T, precision=HIGHEST_PREC...  7.72 us
    another operation x4, other arithmetic, zone_kernel(): weighted = jnp.stack(outer_rows, 0)  6.72 us
  transfers between devices with their start and end apart: 16, of which 4 were waited for; matrix products, arithmetic and copies ran while one was open for 22% of the time, Pallas kernels for 0%

commit v1 on v0

v1 whole, which is shorter than its diff:
```python
import math

import jax
import jax.numpy as jnp
import numpy as np
from jax import lax
from jax.experimental import pallas as pl
from jax.experimental.pallas import tpu as pltpu
from jax.sharding import PartitionSpec as P

NODES = 125
POINTS = 512
MODES = 64
FIELDS = 32
STEPS = 2


TIME_STEP = 0.3
GAMMA_LESS = 0.4
VISCOSITY = 0.3
F32 = jnp.float32
BF16 = jnp.bfloat16
ZONE_COUNT = 256
ROWS = 32
LINE = 1024
CAPACITY = 32
SLOTS = 96
WIDTH = MODES * FIELDS
SENT = WIDTH + 128


def from_behind(shard, axis, by):
    size = lax.axis_size(axis)
    return lax.ppermute(shard, axis, [(i, (i + by) % size) for i in range(size)])


def gauss_rule(order):
    if order == 8:
        half_points = [
            0.1834346424956498,
            0.525532409916329,
            0.7966664774136267,
            0.9602898564975363,
        ]
        half_weights = [
            0.362683783378362,
            0.3137066458778873,
            0.2223810344533745,
            0.1012285362903763,
        ]
    else:
        half_points = [0.3399810435848563, 0.8611363115940526]
        half_weights = [0.6521451548625461, 0.3478548451374538]
    points = np.array([-value for value in half_points[::-1]] + half_points)
    weights = np.array(half_weights[::-1] + half_weights)
    return (points, weights)


def lagrange_tables(nodes, points):
    values = np.ones((points.shape[0], nodes.shape[0]))
    slopes = np.zeros((points.shape[0], nodes.shape[0]))
    for column in range(nodes.shape[0]):
        for other in range(nodes.shape[0]):
            if other != column:
                values[:, column] *= (points - nodes[other]) / (nodes[column] - nodes[other])
        for other in range(nodes.shape[0]):
            if other != column:
                product = np.ones(points.shape) / (nodes[column] - nodes[other])
                for third in range(nodes.shape[0]):
                    if third != column and third != other:
                        product = product * (points - nodes[third]) / (nodes[column] - nodes[third])
                slopes[:, column] += product
    return (values, slopes)


def kron_three(first, second, third):
    return np.kron(np.kron(first, second), third)


def split_table(table):
    high = table.astype(jnp.bfloat16)
    low = (table - high.astype(np.float32)).astype(jnp.bfloat16)
    return (high, low)


def node_columns(table):
    grid = table.reshape(-1, 5, 25 // 5, 5).transpose(0, 3, 1, 2).reshape(-1, 5, 25)
    return np.pad(grid, ((0, 0), (0, 0), (0, ROWS - 25))).reshape(-1, 5 * ROWS)


def basis_tables():
    gauss_points, gauss_weights = gauss_rule(8)
    points = (gauss_points + 1.0) / 2.0
    weights = gauss_weights / 2.0
    root = math.sqrt(3.0 / 7.0)
    lobatto = (np.array([-1.0, -root, 0.0, root, 1.0]) + 1.0) / 2.0
    four_points, four_weights = gauss_rule(4)
    legendre_nodes = (four_points + 1.0) / 2.0
    node_values, node_slopes = lagrange_tables(lobatto, points)
    mode_values, unused_slopes = lagrange_tables(legendre_nodes, points)
    gradient_table = np.concatenate(
        [
            kron_three(node_slopes, node_values, node_values),
            kron_three(node_values, node_slopes, node_values),
            kron_three(node_values, node_values, node_slopes),
        ],
        0,
    )
    interpolate = kron_three(mode_values, mode_values, mode_values)
    weight_table = kron_three(weights, weights, weights)
    mass_diagonal = four_weights / 2.0
    project_line = mode_values.T * weights[None, :] / mass_diagonal[:, None]
    projection = kron_three(project_line, project_line, project_line)
    gradient_table = gradient_table.astype(np.float32)
    weighted_table = gradient_table * np.tile(weight_table.astype(np.float32), 3)[:, None]
    grad_hi, grad_lo = split_table(node_columns(gradient_table))
    force_hi, force_lo = split_table(node_columns(weighted_table).T)
    inter_hi, inter_lo = split_table(interpolate.astype(np.float32))
    proj_hi, proj_lo = split_table(projection.astype(np.float32))
    return (
        jnp.asarray(np.concatenate([grad_hi, grad_hi, grad_lo], 1)),
        jnp.asarray(np.concatenate([force_hi, force_lo], 0)),
        jnp.asarray(np.concatenate([inter_hi, inter_lo], 1)),
        jnp.asarray(np.concatenate([proj_hi, proj_lo], 0)),
    )


def split_two(values):
    high = values.astype(BF16)
    return (high, (values - high.astype(F32)).astype(BF16))


def split_three(values):
    high = values.astype(BF16)
    rest = values - high.astype(F32)
    middle = rest.astype(BF16)
    return (high, middle, (rest - middle.astype(F32)).astype(BF16))


def mm(left, right, dims=((1,), (0,))):
    return lax.dot_general(left, right, (dims, ((), ())), preferred_element_type=F32)


def iota(shape, axis):
    return lax.broadcasted_iota(jnp.int32, shape, axis)


def line_selector(to_zones):
    lattice = iota((512, 512), 0 if to_zones else 1)
    grouped = iota((512, 512), 1 if to_zones else 0)
    return jnp.where(4 * (grouped % 128) + grouped // 128 == lattice, 1.0, 0.0).astype(BF16)


def mode_columns():
    row = iota((2 * MODES, WIDTH), 0)
    column = iota((2 * MODES, WIDTH), 1)
    return jnp.where(FIELDS * (row % MODES) + row // MODES == column, 1.0, 0.0).astype(BF16)


def pick_modes(fields):
    return mm(mode_columns(), fields, ((1,), (1,)))


def zone_math(velocity_of, modes, grad_ref, force_ref, inter_ref, proj_ref, nodes_ref, high_ref, low_ref,
              rate_high_ref, rate_low_ref, lattice_ref, face_up_ref, face_down_ref, modes_ref):
    zones = ZONE_COUNT
    for comp in range(3):
        line = velocity_of(comp)
        lanes = slice(zones * comp, zones * (comp + 1))
        groups = [line[:, zones * u : zones * (u + 1)] for u in range(4)]
        groups.append(pltpu.roll(groups[0], zones - 1, 1))
        for u in range(5):
            high, low = split_two(groups[u])
            nodes_ref[ROWS * u : ROWS * (u + 1), lanes] = high
            nodes_ref[ROWS * (5 + u) : ROWS * (6 + u), lanes] = low
            nodes_ref[ROWS * (10 + u) : ROWS * (11 + u), lanes] = high
    both = jnp.concatenate([modes[:MODES], modes[MODES:]], 1)
    twice = jnp.concatenate([both, both], 0).astype(BF16)
    chunk = 128
    for part in range(POINTS // chunk):
        rows = slice(chunk * part, chunk * (part + 1))
        nodes = nodes_ref[...]
        grads = []
        for first in range(3):
            start = POINTS * first + chunk * part
            flat = mm(grad_ref[start : start + chunk, :], nodes)
            grads.append([flat[:, zones * c : zones * (c + 1)] for c in range(3)])
        points = mm(inter_ref[rows, :], twice)
        rho = points[:, :zones]
        energy = points[:, zones:]
        divergence = grads[0][0] + grads[1][1] + grads[2][2]
        pressure = GAMMA_LESS * energy
        viscous = 0.5 * VISCOSITY * rho
        heating = None
        for first in range(3):
            for second in range(first, 3):
                total = grads[first][second] + grads[second][first]
                entry = viscous * total
                if first == second:
                    entry = entry - pressure
                    work = entry * grads[first][first]
                else:
                    work = entry * total
                heating = work if heating is None else heating + work
                high, low = split_two(entry)
                for d, c in ((first, second), (second, first))[: 1 if first == second else 2]:
                    at = slice(POINTS * d + chunk * part, POINTS * d + chunk * (part + 1))
                    lanes = slice(zones * c, zones * (c + 1))
                    high_ref[at, lanes] = high
                    low_ref[at, lanes] = low
        for column, rate in ((0, -rho * divergence), (zones, heating - energy * divergence)):
            high, low = split_two(rate)
            rate_high_ref[rows, column : column + zones] = high
            rate_low_ref[rows, column : column + zones] = low
    nodal = 5 * ROWS
    main = mm(force_ref[...], high_ref[...])
    force = main[:nodal] + main[nodal:] + mm(force_ref[:nodal, :], low_ref[...])
    for comp in range(3):
        lanes = slice(zones * comp, zones * (comp + 1))
        for u in range(4):
            block = force[ROWS * u : ROWS * (u + 1), lanes]
            if u == 0:
                block = block + pltpu.roll(force[ROWS * 4 : ROWS * 5, lanes], 1, 1)
            lattice_ref[comp, :, zones * u : zones * (u + 1)] = block
    for comp in range(3):
        for s in range(5):
            face_up_ref[5 * comp + s, :] = lattice_ref[comp, 5 * s + 4, :]
            if face_down_ref is not None:
                face_down_ref[5 * comp + s, :] = lattice_ref[comp, 5 * s, :]
    main = mm(proj_ref[...], rate_high_ref[...])
    change = main[:MODES] + main[MODES:] + mm(proj_ref[:MODES, :], rate_low_ref[...])
    both = both + TIME_STEP * change
    modes_ref[:MODES, :] = both[:, :zones].astype(BF16)
    modes_ref[MODES:, :] = both[:, zones:].astype(BF16)


def zone_first_kernel(velocity_ref, mass_ref, halo_a_ref, halo_b_ref, halo_c_ref, fields_ref, grad_ref, force_ref,
                      inter_ref, proj_ref, state_ref, lattice_ref, up_ref, down_ref, modes_ref,
                      native_ref, *scratch):
    for comp in range(4):
        base = ROWS * comp
        native_ref[base + 24 : base + 32, :] = jnp.full((8, LINE), 1.0 if comp == 3 else 0.0, F32)
        for s in range(4):
            own = mass_ref[s] if comp == 3 else velocity_ref[comp, s]
            native_ref[base + 5 * s : base + 5 * s + 4, :] = own
            native_ref[base + 5 * s + 4, :] = halo_b_ref[comp, s, :]
        native_ref[base + 20 : base + 24, :] = halo_a_ref[comp]
        native_ref[base + 24, :] = halo_c_ref[comp, 0, :]
    selector = line_selector(True)
    count = 4 * ROWS
    for half in range(2):
        pieces = jnp.concatenate(split_three(native_ref[:, 512 * half : 512 * (half + 1)]), 0)
        moved = mm(pieces, selector)
        moved = moved[:count] + moved[count : 2 * count] + moved[2 * count :]
        for comp in range(4):
            for u in range(4):
                lanes = slice(256 * u + 128 * half, 256 * u + 128 * (half + 1))
                state_ref[comp, :, lanes] = moved[ROWS * comp : ROWS * (comp + 1), 128 * u : 128 * (u + 1)]
    modes = pick_modes(fields_ref[...])
    zone_math(lambda comp: state_ref[comp], modes, grad_ref, force_ref, inter_ref, proj_ref, *scratch,
              lattice_ref, up_ref, down_ref, modes_ref)


def zone_second_kernel(state_ref, first_ref, low_ref, upper_ref, block_0_ref, block_1_ref, block_2_ref, grad_ref,
                       force_ref, inter_ref, proj_ref, fields_ref, total_ref, lattice_ref, up_ref, modes_ref,
                       *scratch):
    fields = sum_slots(block_0_ref, block_1_ref, block_2_ref)
    fields_ref[...] = fields
    total_ref[...] = first_ref[...]
    for comp in range(3):
        total_ref[comp, 0:5, :] = total_ref[comp, 0:5, :] + low_ref[5 * comp : 5 * comp + 5, :]
        total_ref[comp, 20:25, :] = total_ref[comp, 20:25, :] + upper_ref[5 * comp : 5 * comp + 5, :]
    factor = TIME_STEP / state_ref[3]
    modes = pick_modes(fields)
    zone_math(lambda comp: state_ref[comp] - total_ref[comp] * factor, modes, grad_ref, force_ref, inter_ref,
              proj_ref, *scratch, lattice_ref, up_ref, None, modes_ref)


def sum_slots(*block_refs):
    incoming = jnp.concatenate([ref[...] for ref in block_refs], 0)
    codes = incoming[:, WIDTH:].astype(F32)
    label = iota((SLOTS, 128), 1).astype(F32)
    chosen = [jnp.where(codes == label + 128.0 * half, 1.0, 0.0).astype(BF16) for half in range(ZONE_COUNT // 128)]
    selector = jnp.concatenate(chosen, 1)
    return mm(selector, incoming[:, :WIDTH], ((0,), (0,))).astype(BF16)


def sum_kernel(block_0_ref, block_1_ref, block_2_ref, out_ref):
    out_ref[...] = sum_slots(block_0_ref, block_1_ref, block_2_ref)


def remap_kernel(step, fields_ref, modes_ref, matrix_ref, source_ref, target_ref, low_ref, middle_ref, upper_ref,
                 picked_ref, result_ref):
    zone = iota((ZONE_COUNT, SLOTS), 0)
    chosen = jnp.where(zone == source_ref[step : step + 1, :], 1.0, 0.0).astype(BF16)
    picked = mm(chosen, fields_ref[...], ((0,), (0,)))
    new = mm(chosen, modes_ref[...].T, ((0,), (0,))).astype(BF16)
    new = mm(new, mode_columns())
    lane = iota((SLOTS, 128), 1)
    group = lane // FIELDS
    renewed = lane % FIELDS < 2
    for g in range(WIDTH // 128):
        lanes = slice(128 * g, 128 * (g + 1))
        piece = jnp.where(renewed, new[:, lanes], picked[:, lanes])
        for r in range(4):
            picked_ref[pl.ds(4 * g + r, SLOTS, stride=MODES), :] = jnp.where(group == r, piece, 0.0)

    def multiply(trip, carry):
        for inner in range(8):
            slot = 8 * trip + inner
            at = pl.ds(pl.multiple_of(MODES * slot, MODES), MODES)
            result_ref[at, :] = mm(matrix_ref[0, slot], picked_ref[at, :].astype(BF16))
        return carry

    lax.fori_loop(0, SLOTS // 8, multiply, 0)
    outs = (low_ref, middle_ref, upper_ref)
    for g in range(WIDTH // 128):
        rows = [result_ref[pl.ds(4 * g + r, SLOTS, stride=MODES), :] for r in range(4)]
        total = None
        for shift in range(4):
            mixed = rows[3]
            for r in range(3):
                mixed = jnp.where(group == (r + shift) % 4, rows[r], mixed)
            if shift:
                mixed = pltpu.roll(mixed, 128 - FIELDS * shift, 1)
            total = mixed if total is None else total + mixed
        total = total.astype(BF16)
        for block in range(3):
            outs[block][:, 128 * g : 128 * (g + 1)] = total[CAPACITY * block : CAPACITY * (block + 1)]
    codes = jnp.broadcast_to(target_ref[step : step + 1, :].astype(F32), (8, SLOTS))
    codes = jnp.where(iota((8, SLOTS), 0) == 0, codes, 0.0).astype(BF16)
    codes = mm(codes, jnp.ones((8, 128), BF16), ((0,), (0,))).astype(BF16)
    for block in range(3):
        outs[block][:, WIDTH:] = codes[CAPACITY * block : CAPACITY * (block + 1)]


def fold_kernel(both, lattice_ref, *refs):
    if both:
        low_ref, upper_ref, out_ref, face_up_ref, face_down_ref = refs
    else:
        low_ref, out_ref, face_up_ref = refs
    out_ref[...] = lattice_ref[...]
    for comp in range(3):
        for s in range(5):
            out_ref[comp, 5 * s, :] = out_ref[comp, 5 * s, :] + low_ref[5 * comp + s, :]
            if both:
                out_ref[comp, 5 * s + 4, :] = out_ref[comp, 5 * s + 4, :] + upper_ref[5 * comp + s, :]
    for comp in range(3):
        face_up_ref[5 * comp : 5 * comp + 5, :] = out_ref[comp, 20:25, :]
        if both:
            face_down_ref[5 * comp : 5 * comp + 5, :] = out_ref[comp, 0:5, :]


def final_kernel(velocity_ref, displacement_ref, mass_ref, first_ref, second_ref, low_ref, velocity_out_ref,
                 displacement_out_ref, stage_ref, force_ref):
    for comp in range(3):
        for s in range(4):
            at = 16 * comp + 4 * s
            stage_ref[at : at + 4, :] = first_ref[comp, 5 * s : 5 * s + 4, :]
            second = second_ref[comp, 5 * s : 5 * s + 4, :]
            if s == 0:
                second = second + low_ref[5 * comp : 5 * comp + 4, :]
            stage_ref[48 + at : 48 + at + 4, :] = second
    selector = line_selector(False)
    for half in range(2):
        grouped = jnp.concatenate(
            [stage_ref[:, 256 * u + 128 * half : 256 * u + 128 * (half + 1)] for u in range(4)], 1
        )
        moved = mm(jnp.concatenate(split_two(grouped), 0), selector)
        force_ref[:, 512 * half : 512 * (half + 1)] = moved[:96] + moved[96:]
    for s in range(4):
        factor = TIME_STEP / mass_ref[s]
        for comp in range(3):
            at = 16 * comp + 4 * s
            middle = velocity_ref[comp, s] - force_ref[at : at + 4, :] * factor
            last = middle - force_ref[48 + at : 48 + at + 4, :] * factor
            velocity_out_ref[comp, s] = last
            displacement_out_ref[comp, s] = displacement_ref[comp, s] + TIME_STEP * middle + TIME_STEP * last


def shape(*dims, dtype=F32):
    return jax.ShapeDtypeStruct(dims, dtype)


LATTICE = (3, ROWS, LINE)
FACE = (15, LINE)


def zone_scratch():
    return [
        pltpu.VMEM((15 * ROWS, 3 * ZONE_COUNT), BF16),
        pltpu.VMEM((3 * POINTS, 3 * ZONE_COUNT), BF16),
        pltpu.VMEM((3 * POINTS, 3 * ZONE_COUNT), BF16),
        pltpu.VMEM((POINTS, 2 * ZONE_COUNT), BF16),
        pltpu.VMEM((POINTS, 2 * ZONE_COUNT), BF16),
    ]


def remap_call(step, fields, modes, matrix, source, target):
    whole = lambda *dims: pl.BlockSpec(dims, lambda i: (0,) * len(dims))
    block = shape(CAPACITY, SENT, dtype=BF16)
    return pl.pallas_call(
        lambda *refs: remap_kernel(step, *refs),
        grid=(1,),
        in_specs=[
            whole(ZONE_COUNT, WIDTH),
            whole(2 * MODES, ZONE_COUNT),
            pl.BlockSpec((1, SLOTS, MODES, MODES), lambda i: (step, 0, 0, 0)),
            whole(STEPS, SLOTS),
            whole(STEPS, SLOTS),
        ],
        out_specs=[whole(CAPACITY, SENT)] * 3,
        out_shape=[block] * 3,
        scratch_shapes=[pltpu.VMEM((SLOTS * MODES, 128), F32)] * 2,
        name="remap_step",
    )(fields, modes, matrix, source, target)


def body(fields, velocity, displacement, node_mass, remap_matrix, remap_source, remap_target):
    tables = basis_tables()
    lines = ("gx", "gy")
    send_a = jnp.concatenate([velocity[:, 0], node_mass[None, 0]], 0)
    send_b = jnp.concatenate([velocity[:, :, 0], node_mass[None, :, 0]], 0)
    send_c = send_a[:, :1]
    size_a = lax.axis_size(lines)
    size_b = lax.axis_size("gz")
    corner = [
        (((i + 1) % size_a) * size_b + (j + 1) % size_b, i * size_b + j)
        for i in range(size_a)
        for j in range(size_b)
    ]
    halo_a = from_behind(send_a, lines, -1)
    halo_b = from_behind(send_b, "gz", -1)
    halo_c = lax.ppermute(send_c, ("gx", "gy", "gz"), corner)
    lattice = shape(*LATTICE)
    face = shape(*FACE)
    modes_shape = shape(2 * MODES, ZONE_COUNT, dtype=BF16)
    state, partial, up, down, modes = pl.pallas_call(
        zone_first_kernel,
        out_shape=[shape(4, ROWS, LINE), lattice, face, face, modes_shape],
        scratch_shapes=[pltpu.VMEM((4 * ROWS, LINE), F32)] + zone_scratch(),
        name="zone_first",
    )(velocity, node_mass, halo_a, halo_b, halo_c, fields, *tables)
    from_low = from_behind(up, "gz", 1)
    from_up = from_behind(down, "gz", -1)
    low, middle, upper = remap_call(0, fields, modes, remap_matrix, remap_source, remap_target)
    in_upper = from_behind(upper, lines, 1)
    in_low = from_behind(low, lines, -1)
    partial, up, down = pl.pallas_call(
        lambda *refs: fold_kernel(True, *refs), out_shape=[lattice, face, face], name="fold_first"
    )(partial, from_low, from_up)
    from_low = from_behind(up, lines, 1)
    from_up = from_behind(down, lines, -1)
    fields, first, partial, up, modes = pl.pallas_call(
        zone_second_kernel,
        out_shape=[shape(ZONE_COUNT, WIDTH, dtype=BF16), lattice, lattice, face, modes_shape],
        scratch_shapes=zone_scratch(),
        name="zone_second",
    )(state, partial, from_low, from_up, middle, in_upper, in_low, *tables)
    from_low = from_behind(up, "gz", 1)
    low, middle, upper = remap_call(1, fields, modes, remap_matrix, remap_source, remap_target)
    in_upper = from_behind(upper, lines, 1)
    in_low = from_behind(low, lines, -1)
    partial, up = pl.pallas_call(
        lambda *refs: fold_kernel(False, *refs), out_shape=[lattice, face], name="fold_second"
    )(partial, from_low)
    from_low = from_behind(up, lines, 1)
    velocity_out, displacement_out = pl.pallas_call(
        final_kernel,
        out_shape=[shape(*velocity.shape), shape(*velocity.shape)],
        scratch_shapes=[pltpu.VMEM((96, LINE), F32)] * 2,
        name="final_update",
    )(velocity, displacement, node_mass, first, partial, from_low)
    fields_out = pl.pallas_call(
        sum_kernel, out_shape=shape(ZONE_COUNT, WIDTH, dtype=BF16), name="final_sum"
    )(middle, in_upper, in_low)
    return (fields_out, velocity_out, displacement_out)


def solution(mesh):
    in_specs = (
        P(("gx", "gy", "gz"), None),
        P(None, ("gx", "gy"), "gz", None),
        P(None, ("gx", "gy"), "gz", None),
        P(("gx", "gy"), "gz", None),
        P(None, ("gx", "gy", "gz"), None, None),
        P(None, ("gx", "gy", "gz")),
        P(None, ("gx", "gy", "gz")),
    )
    out_specs = (
        P(("gx", "gy", "gz"), None),
        P(None, ("gx", "gy"), "gz", None),
        P(None, ("gx", "gy"), "gz", None),
    )
    return jax.shard_map(body, mesh=mesh, in_specs=in_specs, out_specs=out_specs, check_vma=False)
```

time: 258 us -> 102 us (0.40)
  the two profiles are of different devices: /device:TPU:7 before, /device:TPU:0 now
where the time goes in v1:
time: 102 us
  Pallas kernels  41.1 us (40%)
  starting transfers between devices  28.5 us (28%)
  waiting for transfers between devices  17.1 us (17%)
  local copies, waits for them, and re-layouts  14.4 us (14%)
    ppermute x12, starting transfers between devices, from_behind(): lax.ppermute(shard, axis, [(i, (i + by) % size) for i in range(size)])  27.9 us
    pallas_call x2, Pallas kernels, remap_call(): pl.pallas_call(lambda *refs: remap_kernel(step, *refs), grid=(1,), in_spe...  17.6 us
    ppermute x12, waiting for transfers between devices, from_behind(): lax.ppermute(shard, axis, [(i, (i + by) % size) for i in range(size)])  17.1 us
    unnamed x35, local copies, waits for them, and re-layouts  11.1 us
    pallas_call x1, Pallas kernels, body(): pl.pallas_call(zone_first_kernel, out_shape=[shape(4, ROWS, LINE), lattic...  7.57 us
    pallas_call x1, Pallas kernels, body(): pl.pallas_call(zone_second_kernel, out_shape=[shape(ZONE_COUNT, WIDTH, dt...  7.09 us
    pallas_call x1, Pallas kernels, body(): pl.pallas_call(final_kernel, out_shape=[shape(*velocity.shape), shape(*ve...  2.62 us
    pallas_call x1, Pallas kernels, body(): pl.pallas_call(sum_kernel, out_shape=shape(ZONE_COUNT, WIDTH, dtype=BF16)...  2.47 us
  transfers between devices with their start and end apart: 13, of which 4 were waited for; matrix products, arithmetic and copies ran while one was open for 8% of the time, Pallas kernels for 6%

profile of v1, /device:TPU:0, one launch (start us, length us, event | category | flops | bytes accessed | tf_op | source)
XLA Modules:
  0.0 101.9 jit_solution(6808943241347288834)
XLA Ops:
  0.6 0.9 slice.18
  1.5 1.0 slice.17
  3.0 0.7 slice.16
  3.7 0.8 slice_bitcast_fusion
  4.5 8.4 %collective-permute-start = (f32[4,4,1024]{2,1,0:T(4,128)S(1)}, f32[4,4,1024]{2,1,0:T(4,128)S(1)}, u32[]{:S(2)}, u32[]{:S(2)}) collective-permute-start(f32[4,4,1024]{2,1,0:T(4,128)S(1)} %pad_maximum_fusion), channel_id=1, source_target_pairs={{0,248},{8,0},{16,8},{24,16},{32,24},{40,32},{48,40},{56,48},{64,5... | collective-permute-start | bytes 196616 | tf_op jit(solution)/shard_map/ppermute | solution.py:34
  12.9 0.7 collective-permute-start.2
  13.6 6.5 %copy.17.refs_2_ = bf16[2,96,64,64]{3,2,1,0:T(8,128)(2,1)} copy(bf16[2,96,64,64]{1,3,2,0:T(8,128)(2,1)} %param.15) | data formatting | bytes 3145728 | tf_op args[4]
  21.3 7.6 %zone_first.1 = (f32[4,32,1024]{2,1,0:T(8,128)}, f32[3,32,1024]{2,1,0:T(8,128)}, f32[15,1024]{1,0:T(8,128)}, f32[15,1024]{1,0:T(8,128)}, bf16[128,256]{1,0:T(8,128)(2,1)}) custom-call(f32[3,4,4,1024]{3,2,1,0:T(4,128)} %velocity_ref.3, f32[4,4,1024]{2,1,0:T(4,128)} %mass_ref.3, f32[4,4,1024]{2,1,0:T(4,128)} %copy-done.7, f32[4,4,1024]{2,1,0:T(4,128)} %copy-done.6, ...), custom_call_target="tpu_custom_call" | custom-call | tf_op jit(solution)/shard_map/zone_first/pallas_call | solution.py:438
  28.9 8.8 %remap_step.2 = (bf16[32,2176]{1,0:T(8,128)(2,1)}, bf16[32,2176]{1,0:T(8,128)(2,1)}, bf16[32,2176]{1,0:T(8,128)(2,1)}) custom-call(bf16[256,2048]{1,0:T(8,128)(2,1)} %refs_0_.1, bf16[128,256]{1,0:T(8,128)(2,1)} %get-tuple-element.33.refs_1_, bf16[2,96,64,64]{3,2,1,0:T(8,128)(2,1)} %copy.17.refs_2_, s32[2,96]{1,0:T(2,128)} %refs_3_.3, s32[2,96]{1,0:T(2,128)} %refs_4_.3), custom_call_target="tpu_custom_call" | custom-call | tf_op jit(solution)/shard_map/remap_step/pallas_call | solution.py:402
  37.7 1.3 %collective-permute-start.7 = (bf16[32,2176]{1,0:T(8,128)(2,1)}, bf16[32,2176]{1,0:T(8,128)(2,1)S(1)}, u32[]{:S(2)}, u32[]{:S(2)}) collective-permute-start(bf16[32,2176]{1,0:T(8,128)(2,1)} %get-tuple-element.35), channel_id=1, source_target_pairs={{0,8},{8,16},{16,24},{24,32},{32,40},{40,48},{48,56},{56,64},{64,7... | collective-permute-start | bytes 417800 | tf_op jit(solution)/shard_map/ppermute | solution.py:34
  39.0 4.1 %collective-permute-start.8 = (bf16[32,2176]{1,0:T(8,128)(2,1)}, bf16[32,2176]{1,0:T(8,128)(2,1)S(1)}, u32[]{:S(2)}, u32[]{:S(2)}) collective-permute-start(bf16[32,2176]{1,0:T(8,128)(2,1)} %get-tuple-element.36), channel_id=1, source_target_pairs={{0,248},{8,0},{16,8},{24,16},{32,24},{40,32},{48,40},{56,48},{64,5... | collective-permute-start | bytes 417800 | tf_op jit(solution)/shard_map/ppermute | solution.py:34
  43.1 3.0 %collective-permute-start.4 = (f32[15,1024]{1,0:T(8,128)S(1)}, f32[15,1024]{1,0:T(8,128)S(1)}, u32[]{:S(2)}, u32[]{:S(2)}) collective-permute-start(f32[15,1024]{1,0:T(8,128)S(1)} %copy-done.14), channel_id=1, source_target_pairs={{0,7},{1,0},{2,1},{3,2},{4,3},{5,4},{6,5},{7,6},{8,15},{9,8},{10,9... | collective-permute-start | bytes 184328 | tf_op jit(solution)/shard_map/ppermute | solution.py:34
  46.0 1.9 %collective-permute-done.3.refs_1_ = f32[15,1024]{1,0:T(8,128)S(1)} collective-permute-done((f32[15,1024]{1,0:T(8,128)S(1)}, f32[15,1024]{1,0:T(8,128)S(1)}, u32[]{:S(2)}, u32[]{:S(2)}) %collective-permute-start.3) | collective-permute-done | bytes 61472 | tf_op jit(solution)/shard_map/ppermute | solution.py:34
  48.6 1.9 %fold_first.1 = (f32[3,32,1024]{2,1,0:T(8,128)}, f32[15,1024]{1,0:T(8,128)}, f32[15,1024]{1,0:T(8,128)}) custom-call(f32[3,32,1024]{2,1,0:T(8,128)} %get-tuple-element.27.refs_0_, f32[15,1024]{1,0:T(8,128)} %copy-done.10, f32[15,1024]{1,0:T(8,128)} %copy-done.11), custom_call_target="tpu_custom_call" | custom-call | tf_op jit(solution)/shard_map/fold_first/pallas_call | solution.py:449
  50.6 5.3 %collective-permute-start.6 = (f32[15,1024]{1,0:T(8,128)}, f32[15,1024]{1,0:T(8,128)S(1)}, u32[]{:S(2)}, u32[]{:S(2)}) collective-permute-start(f32[15,1024]{1,0:T(8,128)} %get-tuple-element.32), channel_id=1, source_target_pairs={{0,248},{8,0},{16,8},{24,16},{32,24},{40,32},{48,40},{56,48},{64,5... | collective-permute-start | bytes 184328 | tf_op jit(solution)/shard_map/ppermute | solution.py:34
  55.9 2.4 %collective-permute-done.5.low_ref = f32[15,1024]{1,0:T(8,128)S(1)} collective-permute-done((f32[15,1024]{1,0:T(8,128)}, f32[15,1024]{1,0:T(8,128)S(1)}, u32[]{:S(2)}, u32[]{:S(2)}) %collective-permute-start.5) | collective-permute-done | bytes 61472 | tf_op jit(solution)/shard_map/ppermute | solution.py:34
  59.1 7.1 %zone_second.1 = (bf16[256,2048]{1,0:T(8,128)(2,1)}, f32[3,32,1024]{2,1,0:T(8,128)}, f32[3,32,1024]{2,1,0:T(8,128)}, f32[15,1024]{1,0:T(8,128)}, bf16[128,256]{1,0:T(8,128)(2,1)}) custom-call(f32[4,32,1024]{2,1,0:T(8,128)} %get-tuple-element.26.state_ref, f32[3,32,1024]{2,1,0:T(8,128)} %get-tuple-element.30.first_ref, f32[15,1024]{1,0:T(8,128)} %copy-done.4, ...), custom_call_target="tpu_custom_call" | custom-call | tf_op jit(solution)/shard_map/zone_second/pallas_call | solution.py:454
  66.2 8.8 %remap_step.3 = (bf16[32,2176]{1,0:T(8,128)(2,1)}, bf16[32,2176]{1,0:T(8,128)(2,1)}, bf16[32,2176]{1,0:T(8,128)(2,1)}) custom-call(bf16[256,2048]{1,0:T(8,128)(2,1)} %get-tuple-element.37.refs_0_, bf16[128,256]{1,0:T(8,128)(2,1)} %get-tuple-element.38.refs_1_, bf16[2,96,64,64]{3,2,1,0:T(8,128)(2,1)} %copy.17.refs_2_, s32[2,96]{1,0:T(2,128)} %refs_3_.3, ...), custom_call_target="tpu_custom_call" | custom-call | tf_op jit(solution)/shard_map/remap_step/pallas_call | solution.py:402
  75.0 5.3 %collective-permute-start.10 = (bf16[32,2176]{1,0:T(8,128)(2,1)}, bf16[32,2176]{1,0:T(8,128)(2,1)S(1)}, u32[]{:S(2)}, u32[]{:S(2)}) collective-permute-start(bf16[32,2176]{1,0:T(8,128)(2,1)} %get-tuple-element.41), channel_id=1, source_target_pairs={{0,248},{8,0},{16,8},{24,16},{32,24},{40,32},{48,40},{56,48},{64,5... | collective-permute-start | bytes 417800 | tf_op jit(solution)/shard_map/ppermute | solution.py:34
  80.4 4.9 %collective-permute-done.11.refs_1_ = f32[15,1024]{1,0:T(8,128)S(1)} collective-permute-done((f32[15,1024]{1,0:T(8,128)S(1)}, f32[15,1024]{1,0:T(8,128)S(1)}, u32[]{:S(2)}, u32[]{:S(2)}) %collective-permute-start.11) | collective-permute-done | bytes 61472 | tf_op jit(solution)/shard_map/ppermute | solution.py:34
  85.9 1.8 %fold_second.1 = (f32[3,32,1024]{2,1,0:T(8,128)}, f32[15,1024]{1,0:T(8,128)}) custom-call(f32[3,32,1024]{2,1,0:T(8,128)} %get-tuple-element.43.refs_0_, f32[15,1024]{1,0:T(8,128)} %copy-done.9), custom_call_target="tpu_custom_call" | custom-call | tf_op jit(solution)/shard_map/fold_second/pallas_call | solution.py:464
  87.7 7.8 %collective-permute-done.12.low_ref = f32[15,1024]{1,0:T(8,128)S(1)} collective-permute-done((f32[15,1024]{1,0:T(8,128)}, f32[15,1024]{1,0:T(8,128)S(1)}, u32[]{:S(2)}, u32[]{:S(2)}) %collective-permute-start.12) | collective-permute-done | bytes 61472 | tf_op jit(solution)/shard_map/ppermute | solution.py:34
  96.1 2.6 %final_update.1 = (f32[3,4,4,1024]{3,2,1,0:T(4,128)}, f32[3,4,4,1024]{3,2,1,0:T(4,128)}) custom-call(f32[3,4,4,1024]{3,2,1,0:T(4,128)} %velocity_ref.3, f32[3,4,4,1024]{3,2,1,0:T(4,128)} %displacement_ref.1, f32[4,4,1024]{2,1,0:T(4,128)} %mass_ref.3, f32[3,32,1024]{2,1,0:T(8,128)} %get-tuple-element.42.first_ref, ...), custom_call_target="tpu_custom_call" | custom-call | tf_op jit(solution)/shard_map/final_update/pallas_call | solution.py:468
  99.5 2.5 %final_sum.1 = bf16[256,2048]{1,0:T(8,128)(2,1)} custom-call(bf16[32,2176]{1,0:T(8,128)(2,1)} %get-tuple-element.39.block_0_ref, bf16[32,2176]{1,0:T(8,128)(2,1)} %copy-done.2, bf16[32,2176]{1,0:T(8,128)(2,1)} %copy-done.3), custom_call_target="tpu_custom_call" | custom-call | tf_op jit(solution)/shard_map/final_sum/pallas_call | solution.py:474
  (52 shorter events, 5.2 us)
Async XLA Ops:
  2.5 17.5 %collective-permute-start.1 = (f32[4,4,1024]{2,1,0:T(4,128)S(1)}, f32[4,4,1024]{2,1,0:T(4,128)S(1)}, u32[]{:S(2)}, u32[]{:S(2)}) collective-permute-start(f32[4,4,1024]{2,1,0:T(4,128)S(1)} %pad_maximum_fusion.1), channel_id=1, source_target_pairs={{0,7},{1,0},{2,1},{3,2},{4,3},{5,4},{6,5},{7,6},{8,15},{9,8},{10,9... | collective-permute-start | bytes 196616 | tf_op jit(solution)/shard_map/ppermute | solution.py:34
  4.5 15.5 %collective-permute-start = (f32[4,4,1024]{2,1,0:T(4,128)S(1)}, f32[4,4,1024]{2,1,0:T(4,128)S(1)}, u32[]{:S(2)}, u32[]{:S(2)}) collective-permute-start(f32[4,4,1024]{2,1,0:T(4,128)S(1)} %pad_maximum_fusion), channel_id=1, source_target_pairs={{0,248},{8,0},{16,8},{24,16},{32,24},{40,32},{48,40},{56,48},{64,5... | collective-permute-start | bytes 196616 | tf_op jit(solution)/shard_map/ppermute | solution.py:34
  12.9 7.1 %collective-permute-start.2 = (f32[4,1,1024]{2,1,0:T(1,128)S(1)}, f32[4,1,1024]{2,1,0:T(1,128)S(1)}, u32[]{:S(2)}, u32[]{:S(2)}) collective-permute-start(f32[4,1,1024]{2,1,0:T(1,128)S(1)} %fusion), channel_id=1, source_target_pairs={{9,0},{10,1},{11,2},{12,3},{13,4},{14,5},{15,6},{8,7},{17,8},{18,9... | collective-permute-start | bytes 49160 | tf_op jit(solution)/shard_map/ppermute | solution.py:434
  20.1 0.6 copy-start.6
  28.9 14.2 %copy-start.15 = (f32[15,1024]{1,0:T(8,128)S(1)}, f32[15,1024]{1,0:T(8,128)}, u32[]{:S(2)}) copy-start(f32[15,1024]{1,0:T(8,128)} %get-tuple-element.28) | copy-start | bytes 184324
  28.9 14.2 %copy-start.14 = (f32[15,1024]{1,0:T(8,128)S(1)}, f32[15,1024]{1,0:T(8,128)}, u32[]{:S(2)}) copy-start(f32[15,1024]{1,0:T(8,128)} %get-tuple-element.29) | copy-start | bytes 184324
  37.7 20.6 %collective-permute-start.7 = (bf16[32,2176]{1,0:T(8,128)(2,1)}, bf16[32,2176]{1,0:T(8,128)(2,1)S(1)}, u32[]{:S(2)}, u32[]{:S(2)}) collective-permute-start(bf16[32,2176]{1,0:T(8,128)(2,1)} %get-tuple-element.35), channel_id=1, source_target_pairs={{0,8},{8,16},{16,24},{24,32},{32,40},{40,48},{48,56},{56,64},{64,7... | collective-permute-start | bytes 417800 | tf_op jit(solution)/shard_map/ppermute | solution.py:34
  39.0 19.4 %collective-permute-start.8 = (bf16[32,2176]{1,0:T(8,128)(2,1)}, bf16[32,2176]{1,0:T(8,128)(2,1)S(1)}, u32[]{:S(2)}, u32[]{:S(2)}) collective-permute-start(bf16[32,2176]{1,0:T(8,128)(2,1)} %get-tuple-element.36), channel_id=1, source_target_pairs={{0,248},{8,0},{16,8},{24,16},{32,24},{40,32},{48,40},{56,48},{64,5... | collective-permute-start | bytes 417800 | tf_op jit(solution)/shard_map/ppermute | solution.py:34
  43.1 4.9 %collective-permute-start.3 = (f32[15,1024]{1,0:T(8,128)S(1)}, f32[15,1024]{1,0:T(8,128)S(1)}, u32[]{:S(2)}, u32[]{:S(2)}) collective-permute-start(f32[15,1024]{1,0:T(8,128)S(1)} %copy-done.15), channel_id=1, source_target_pairs={{0,1},{1,2},{2,3},{3,4},{4,5},{5,6},{6,7},{7,0},{8,9},{9,10},{10,1... | collective-permute-start | bytes 184328 | tf_op jit(solution)/shard_map/ppermute | solution.py:34
  43.1 4.9 %collective-permute-start.4 = (f32[15,1024]{1,0:T(8,128)S(1)}, f32[15,1024]{1,0:T(8,128)S(1)}, u32[]{:S(2)}, u32[]{:S(2)}) collective-permute-start(f32[15,1024]{1,0:T(8,128)S(1)} %copy-done.14), channel_id=1, source_target_pairs={{0,7},{1,0},{2,1},{3,2},{4,3},{5,4},{6,5},{7,6},{8,15},{9,8},{10,9... | collective-permute-start | bytes 184328 | tf_op jit(solution)/shard_map/ppermute | solution.py:34
  48.0 0.7 copy-start.11
  50.5 7.8 %collective-permute-start.5 = (f32[15,1024]{1,0:T(8,128)}, f32[15,1024]{1,0:T(8,128)S(1)}, u32[]{:S(2)}, u32[]{:S(2)}) collective-permute-start(f32[15,1024]{1,0:T(8,128)} %get-tuple-element.31), channel_id=1, source_target_pairs={{0,8},{8,16},{16,24},{24,32},{32,40},{40,48},{48,56},{56,64},{64,7... | collective-permute-start | bytes 184328 | tf_op jit(solution)/shard_map/ppermute | solution.py:34
  50.6 7.8 %collective-permute-start.6 = (f32[15,1024]{1,0:T(8,128)}, f32[15,1024]{1,0:T(8,128)S(1)}, u32[]{:S(2)}, u32[]{:S(2)}) collective-permute-start(f32[15,1024]{1,0:T(8,128)} %get-tuple-element.32), channel_id=1, source_target_pairs={{0,248},{8,0},{16,8},{24,16},{32,24},{40,32},{48,40},{56,48},{64,5... | collective-permute-start | bytes 184328 | tf_op jit(solution)/shard_map/ppermute | solution.py:34
  58.3 0.7 copy-start.5
  58.4 0.7 copy-start
  58.4 0.7 copy-start.1
  66.2 14.2 %copy-start.13 = (f32[15,1024]{1,0:T(8,128)S(1)}, f32[15,1024]{1,0:T(8,128)}, u32[]{:S(2)}) copy-start(f32[15,1024]{1,0:T(8,128)} %get-tuple-element.44) | copy-start | bytes 184324
  75.0 23.8 %collective-permute-start.9 = (bf16[32,2176]{1,0:T(8,128)(2,1)}, bf16[32,2176]{1,0:T(8,128)(2,1)S(1)}, u32[]{:S(2)}, u32[]{:S(2)}) collective-permute-start(bf16[32,2176]{1,0:T(8,128)(2,1)} %get-tuple-element.40), channel_id=1, source_target_pairs={{0,8},{8,16},{16,24},{24,32},{32,40},{40,48},{48,56},{56,64},{64,7... | collective-permute-start | bytes 417800 | tf_op jit(solution)/shard_map/ppermute | solution.py:34
  75.0 23.8 %collective-permute-start.10 = (bf16[32,2176]{1,0:T(8,128)(2,1)}, bf16[32,2176]{1,0:T(8,128)(2,1)S(1)}, u32[]{:S(2)}, u32[]{:S(2)}) collective-permute-start(bf16[32,2176]{1,0:T(8,128)(2,1)} %get-tuple-element.41), channel_id=1, source_target_pairs={{0,248},{8,0},{16,8},{24,16},{32,24},{40,32},{48,40},{56,48},{64,5... | collective-permute-start | bytes 417800 | tf_op jit(solution)/shard_map/ppermute | solution.py:34
  80.4 4.9 %collective-permute-start.11 = (f32[15,1024]{1,0:T(8,128)S(1)}, f32[15,1024]{1,0:T(8,128)S(1)}, u32[]{:S(2)}, u32[]{:S(2)}) collective-permute-start(f32[15,1024]{1,0:T(8,128)S(1)} %copy-done.13), channel_id=1, source_target_pairs={{0,1},{1,2},{2,3},{3,4},{4,5},{5,6},{6,7},{7,0},{8,9},{9,10},{10,1... | collective-permute-start | bytes 184328 | tf_op jit(solution)/shard_map/ppermute | solution.py:34
  87.7 7.8 %collective-permute-start.12 = (f32[15,1024]{1,0:T(8,128)}, f32[15,1024]{1,0:T(8,128)S(1)}, u32[]{:S(2)}, u32[]{:S(2)}) collective-permute-start(f32[15,1024]{1,0:T(8,128)} %get-tuple-element.46), channel_id=1, source_target_pairs={{0,8},{8,16},{16,24},{24,32},{32,40},{40,48},{48,56},{56,64},{64,7... | collective-permute-start | bytes 184328 | tf_op jit(solution)/shard_map/ppermute | solution.py:34
  95.5 0.6 copy-start.8
  98.8 0.6 copy-start.2
  98.8 0.7 copy-start.3
  (5 other events, 3.1 us)

commit v2 on v1

--- a/solution.py
+++ b/solution.py
@@ -27,6 +27,7 @@
 SLOTS = 96
 WIDTH = MODES * FIELDS
 SENT = WIDTH + 128
+FOLDED = CAPACITY + 16
 
 
 def from_behind(shard, axis, by):
@@ -162,7 +163,7 @@
 
 
 def zone_math(velocity_of, modes, grad_ref, force_ref, inter_ref, proj_ref, nodes_ref, high_ref, low_ref,
-              rate_high_ref, rate_low_ref, lattice_ref, face_up_ref, face_down_ref, modes_ref):
+              rate_high_ref, rate_low_ref, lattice_ref, face_up_ref, edge_up_ref, face_down_ref, edge_down_ref, modes_ref):
     zones = ZONE_COUNT
     for comp in range(3):
         line = velocity_of(comp)
@@ -227,6 +228,9 @@
             face_up_ref[5 * comp + s, :] = lattice_ref[comp, 5 * s + 4, :]
             if face_down_ref is not None:
                 face_down_ref[5 * comp + s, :] = lattice_ref[comp, 5 * s, :]
+        edge_up_ref[5 * comp : 5 * comp + 5, :] = lattice_ref[comp, 20:25, :]
+        if edge_down_ref is not None:
+            edge_down_ref[5 * comp : 5 * comp + 5, :] = lattice_ref[comp, 0:5, :]
     main = mm(proj_ref[...], rate_high_ref[...])
     change = main[:MODES] + main[MODES:] + mm(proj_ref[:MODES, :], rate_low_ref[...])
     both = both + TIME_STEP * change
@@ -235,7 +239,7 @@
 
 
 def zone_first_kernel(velocity_ref, mass_ref, halo_a_ref, halo_b_ref, halo_c_ref, fields_ref, grad_ref, force_ref,
-                      inter_ref, proj_ref, state_ref, lattice_ref, up_ref, down_ref, modes_ref,
+                      inter_ref, proj_ref, state_ref, lattice_ref, up_ref, edge_up_ref, down_ref, edge_down_ref, modes_ref,
                       native_ref, *scratch):
     for comp in range(4):
         base = ROWS * comp
@@ -258,35 +262,48 @@
                 state_ref[comp, :, lanes] = moved[ROWS * comp : ROWS * (comp + 1), 128 * u : 128 * (u + 1)]
     modes = pick_modes(fields_ref[...])
     zone_math(lambda comp: state_ref[comp], modes, grad_ref, force_ref, inter_ref, proj_ref, *scratch,
-              lattice_ref, up_ref, down_ref, modes_ref)
-
-
-def zone_second_kernel(state_ref, first_ref, low_ref, upper_ref, block_0_ref, block_1_ref, block_2_ref, grad_ref,
-                       force_ref, inter_ref, proj_ref, fields_ref, total_ref, lattice_ref, up_ref, modes_ref,
-                       *scratch):
-    fields = sum_slots(block_0_ref, block_1_ref, block_2_ref)
+              lattice_ref, up_ref, edge_up_ref, down_ref, edge_down_ref, modes_ref)
+
+
+def add_faces(total_ref, low_ref, upper_ref):
+    for comp in range(3):
+        for s in range(5):
+            at = 5 * comp + s
+            total_ref[comp, 5 * s, :] = total_ref[comp, 5 * s, :] + low_ref[at, :]
+            if upper_ref is not None:
+                total_ref[comp, 5 * s + 4, :] = total_ref[comp, 5 * s + 4, :] + upper_ref[at, :]
+
+
+def join_edge(block_ref):
+    pair = block_ref[CAPACITY:FOLDED, :WIDTH].astype(F32)
+    return pair[:, :LINE] + pair[:, LINE:]
+
+
+def zone_second_kernel(state_ref, first_ref, low_ref, upper_ref, middle_ref, in_low_ref, in_upper_ref, grad_ref,
+                       force_ref, inter_ref, proj_ref, fields_ref, total_ref, lattice_ref, up_ref, edge_up_ref,
+                       modes_ref, edge_ref, *scratch):
+    fields = sum_slots(middle_ref, in_low_ref, in_upper_ref)
     fields_ref[...] = fields
     total_ref[...] = first_ref[...]
-    for comp in range(3):
-        total_ref[comp, 0:5, :] = total_ref[comp, 0:5, :] + low_ref[5 * comp : 5 * comp + 5, :]
-        total_ref[comp, 20:25, :] = total_ref[comp, 20:25, :] + upper_ref[5 * comp : 5 * comp + 5, :]
+    add_faces(total_ref, low_ref, upper_ref)
+    for row, block_ref in ((0, in_low_ref), (20, in_upper_ref)):
+        edge_ref[...] = join_edge(block_ref)
+        for comp in range(3):
+            at = slice(5 * comp, 5 * comp + 5)
+            total_ref[comp, row : row + 5, :] = total_ref[comp, row : row + 5, :] + edge_ref[at, :]
     factor = TIME_STEP / state_ref[3]
     modes = pick_modes(fields)
     zone_math(lambda comp: state_ref[comp] - total_ref[comp] * factor, modes, grad_ref, force_ref, inter_ref,
-              proj_ref, *scratch, lattice_ref, up_ref, None, modes_ref)
+              proj_ref, *scratch, lattice_ref, up_ref, edge_up_ref, None, None, modes_ref)
 
 
 def sum_slots(*block_refs):
-    incoming = jnp.concatenate([ref[...] for ref in block_refs], 0)
+    incoming = jnp.concatenate([ref[:CAPACITY, :] for ref in block_refs], 0)
     codes = incoming[:, WIDTH:].astype(F32)
     label = iota((SLOTS, 128), 1).astype(F32)
     chosen = [jnp.where(codes == label + 128.0 * half, 1.0, 0.0).astype(BF16) for half in range(ZONE_COUNT // 128)]
     selector = jnp.concatenate(chosen, 1)
     return mm(selector, incoming[:, :WIDTH], ((0,), (0,))).astype(BF16)
-
-
-def sum_kernel(block_0_ref, block_1_ref, block_2_ref, out_ref):
-    out_ref[...] = sum_slots(block_0_ref, block_1_ref, block_2_ref)
 
 
 def remap_kernel(step, fields_ref, modes_ref, matrix_ref, source_ref, target_ref, low_ref, middle_ref, upper_ref,
@@ -334,40 +351,49 @@
         outs[block][:, WIDTH:] = codes[CAPACITY * block : CAPACITY * (block + 1)]
 
 
-def fold_kernel(both, lattice_ref, *refs):
-    if both:
-        low_ref, upper_ref, out_ref, face_up_ref, face_down_ref = refs
-    else:
-        low_ref, out_ref, face_up_ref = refs
-    out_ref[...] = lattice_ref[...]
-    for comp in range(3):
-        for s in range(5):
-            out_ref[comp, 5 * s, :] = out_ref[comp, 5 * s, :] + low_ref[5 * comp + s, :]
-            if both:
-                out_ref[comp, 5 * s + 4, :] = out_ref[comp, 5 * s + 4, :] + upper_ref[5 * comp + s, :]
-    for comp in range(3):
-        face_up_ref[5 * comp : 5 * comp + 5, :] = out_ref[comp, 20:25, :]
-        if both:
-            face_down_ref[5 * comp : 5 * comp + 5, :] = out_ref[comp, 0:5, :]
-
-
-def final_kernel(velocity_ref, displacement_ref, mass_ref, first_ref, second_ref, low_ref, velocity_out_ref,
-                 displacement_out_ref, stage_ref, force_ref):
-    for comp in range(3):
-        for s in range(4):
-            at = 16 * comp + 4 * s
-            stage_ref[at : at + 4, :] = first_ref[comp, 5 * s : 5 * s + 4, :]
-            second = second_ref[comp, 5 * s : 5 * s + 4, :]
-            if s == 0:
-                second = second + low_ref[5 * comp : 5 * comp + 4, :]
-            stage_ref[48 + at : 48 + at + 4, :] = second
+def fold_edge(edge_ref, source_row, low_ref, upper_ref, stage_ref, out_ref):
+    stage_ref[15:16, :] = jnp.zeros((1, LINE), F32)
+    stage_ref[0:15, :] = edge_ref[...]
+    for comp in range(3):
+        at = 5 * comp
+        stage_ref[at, :] = stage_ref[at, :] + low_ref[at + source_row, :]
+        if upper_ref is not None:
+            stage_ref[at + 4, :] = stage_ref[at + 4, :] + upper_ref[at + source_row, :]
+    high, low = split_two(stage_ref[...])
+    out_ref[:, :LINE] = high
+    out_ref[:, LINE:WIDTH] = low
+    out_ref[:, WIDTH:] = jnp.zeros((16, 128), BF16)
+
+
+def fold_first_kernel(up_any, down_any, edge_up_ref, edge_down_ref, low_ref, upper_ref, up_ref, down_ref, stage_ref):
+    fold_edge(edge_up_ref, 4, low_ref, upper_ref, stage_ref, up_ref)
+    fold_edge(edge_down_ref, 0, low_ref, upper_ref, stage_ref, down_ref)
+
+
+def fold_second_kernel(up_any, edge_up_ref, low_ref, up_ref, stage_ref):
+    fold_edge(edge_up_ref, 4, low_ref, None, stage_ref, up_ref)
+
+
+def interleave(stage_ref, force_ref):
+    count = stage_ref.shape[0]
     selector = line_selector(False)
     for half in range(2):
         grouped = jnp.concatenate(
             [stage_ref[:, 256 * u + 128 * half : 256 * u + 128 * (half + 1)] for u in range(4)], 1
         )
         moved = mm(jnp.concatenate(split_two(grouped), 0), selector)
-        force_ref[:, 512 * half : 512 * (half + 1)] = moved[:96] + moved[96:]
+        force_ref[:, 512 * half : 512 * (half + 1)] = moved[:count] + moved[count:]
+
+
+def update_kernel(velocity_ref, displacement_ref, mass_ref, first_ref, second_ref, low_ref, velocity_out_ref,
+                  displacement_out_ref, stage_ref, force_ref):
+    for comp in range(3):
+        for s in range(4):
+            at = 16 * comp + 4 * s
+            stage_ref[at : at + 4, :] = first_ref[comp, 5 * s : 5 * s + 4, :]
+            stage_ref[48 + at : 48 + at + 4, :] = second_ref[comp, 5 * s : 5 * s + 4, :]
+            stage_ref[48 + at, :] = stage_ref[48 + at, :] + low_ref[5 * comp + s, :]
+    interleave(stage_ref, force_ref)
     for s in range(4):
         factor = TIME_STEP / mass_ref[s]
         for comp in range(3):
@@ -378,6 +404,28 @@
             displacement_out_ref[comp, s] = displacement_ref[comp, s] + TIME_STEP * middle + TIME_STEP * last
 
 
+def finish_kernel(velocity_ref, displacement_ref, mass_ref, middle_ref, in_low_ref, in_upper_ref, fields_ref,
+                  velocity_out_ref, displacement_out_ref, stage_ref, force_ref):
+    fields_ref[...] = sum_slots(middle_ref, in_low_ref, in_upper_ref)
+    stage_ref[...] = join_edge(in_low_ref)
+    interleave(stage_ref, force_ref)
+    factor = TIME_STEP / mass_ref[0]
+    for comp in range(3):
+        change = force_ref[5 * comp : 5 * comp + 4, :] * factor
+        velocity_out_ref[comp, 0] = velocity_ref[comp, 0] - change
+        displacement_out_ref[comp, 0] = displacement_ref[comp, 0] - TIME_STEP * change
+
+
+def pack_kernel(velocity_ref, mass_ref, send_a_ref, send_b_ref, send_c_ref):
+    for comp in range(4):
+        for s in range(4):
+            own = mass_ref[s] if comp == 3 else velocity_ref[comp, s]
+            if s == 0:
+                send_a_ref[comp] = own
+                send_c_ref[comp] = own[:1]
+            send_b_ref[comp, s : s + 1, :] = own[:1]
+
+
 def shape(*dims, dtype=F32):
     return jax.ShapeDtypeStruct(dims, dtype)
 
@@ -396,32 +444,46 @@
     ]
 
 
+def whole(*dims):
+    return pl.BlockSpec(dims, lambda i: (0,) * len(dims))
+
+
+def cost(microseconds):
+    return pl.CostEstimate(flops=int(microseconds * 1e9), bytes_accessed=int(microseconds * 3e6), transcendentals=0)
+
+
+ANYWHERE = pl.BlockSpec(memory_space=pl.ANY)
+EDGE_BLOCK = pl.BlockSpec((16, SENT), lambda i: (CAPACITY // 16, 0))
+
+
 def remap_call(step, fields, modes, matrix, source, target):
-    whole = lambda *dims: pl.BlockSpec(dims, lambda i: (0,) * len(dims))
-    block = shape(CAPACITY, SENT, dtype=BF16)
     return pl.pallas_call(
         lambda *refs: remap_kernel(step, *refs),
         grid=(1,),
         in_specs=[
             whole(ZONE_COUNT, WIDTH),
             whole(2 * MODES, ZONE_COUNT),
-            pl.BlockSpec((1, SLOTS, MODES, MODES), lambda i: (step, 0, 0, 0)),
+            whole(1, SLOTS, MODES, MODES),
             whole(STEPS, SLOTS),
             whole(STEPS, SLOTS),
         ],
         out_specs=[whole(CAPACITY, SENT)] * 3,
-        out_shape=[block] * 3,
+        out_shape=[shape(rows, SENT, dtype=BF16) for rows in (FOLDED if step == 0 else CAPACITY, CAPACITY, FOLDED)],
         scratch_shapes=[pltpu.VMEM((SLOTS * MODES, 128), F32)] * 2,
+        cost_estimate=cost(9),
         name="remap_step",
-    )(fields, modes, matrix, source, target)
+    )(fields, modes, matrix[step : step + 1], source, target)
 
 
 def body(fields, velocity, displacement, node_mass, remap_matrix, remap_source, remap_target):
     tables = basis_tables()
     lines = ("gx", "gy")
-    send_a = jnp.concatenate([velocity[:, 0], node_mass[None, 0]], 0)
-    send_b = jnp.concatenate([velocity[:, :, 0], node_mass[None, :, 0]], 0)
-    send_c = send_a[:, :1]
+    send_a, send_b, send_c = pl.pallas_call(
+        pack_kernel,
+        out_shape=[shape(4, 4, LINE), shape(4, 4, LINE), shape(4, 1, LINE)],
+        cost_estimate=cost(1),
+        name="pack_halo",
+    )(velocity, node_mass)
     size_a = lax.axis_size(lines)
     size_b = lax.axis_size("gz")
     corner = [
@@ -435,45 +497,79 @@
     lattice = shape(*LATTICE)
     face = shape(*FACE)
     modes_shape = shape(2 * MODES, ZONE_COUNT, dtype=BF16)
-    state, partial, up, down, modes = pl.pallas_call(
+    folded = shape(FOLDED, SENT, dtype=BF16)
+    state, partial, up, edge_up, down, edge_down, modes = pl.pallas_call(
         zone_first_kernel,
-        out_shape=[shape(4, ROWS, LINE), lattice, face, face, modes_shape],
+        out_shape=[shape(4, ROWS, LINE), lattice, face, face, face, face, modes_shape],
         scratch_shapes=[pltpu.VMEM((4 * ROWS, LINE), F32)] + zone_scratch(),
+        cost_estimate=cost(7),
         name="zone_first",
     )(velocity, node_mass, halo_a, halo_b, halo_c, fields, *tables)
     from_low = from_behind(up, "gz", 1)
     from_up = from_behind(down, "gz", -1)
     low, middle, upper = remap_call(0, fields, modes, remap_matrix, remap_source, remap_target)
-    in_upper = from_behind(upper, lines, 1)
-    in_low = from_behind(low, lines, -1)
-    partial, up, down = pl.pallas_call(
-        lambda *refs: fold_kernel(True, *refs), out_shape=[lattice, face, face], name="fold_first"
-    )(partial, from_low, from_up)
-    from_low = from_behind(up, lines, 1)
-    from_up = from_behind(down, lines, -1)
-    fields, first, partial, up, modes = pl.pallas_call(
+    upper, low = pl.pallas_call(
+        fold_first_kernel,
+        grid=(1,),
+        in_specs=[ANYWHERE, ANYWHERE] + [whole(*FACE)] * 4,
+        out_specs=[EDGE_BLOCK, EDGE_BLOCK],
+        out_shape=[folded, folded],
+        input_output_aliases={0: 0, 1: 1},
+        scratch_shapes=[pltpu.VMEM((16, LINE), F32)],
+        cost_estimate=cost(1),
+        name="fold_first",
+    )(upper, low, edge_up, edge_down, from_low, from_up)
+    in_low = from_behind(upper, lines, 1)
+    in_upper = from_behind(low, lines, -1)
+    fields, first, partial, up, edge_up, modes = pl.pallas_call(
         zone_second_kernel,
-        out_shape=[shape(ZONE_COUNT, WIDTH, dtype=BF16), lattice, lattice, face, modes_shape],
-        scratch_shapes=zone_scratch(),
+        out_shape=[shape(ZONE_COUNT, WIDTH, dtype=BF16), lattice, lattice, face, face, modes_shape],
+        scratch_shapes=[pltpu.VMEM((16, LINE), F32)] + zone_scratch(),
+        cost_estimate=cost(7),
         name="zone_second",
-    )(state, partial, from_low, from_up, middle, in_upper, in_low, *tables)
+    )(state, partial, from_low, from_up, middle, in_low, in_upper, *tables)
     from_low = from_behind(up, "gz", 1)
     low, middle, upper = remap_call(1, fields, modes, remap_matrix, remap_source, remap_target)
-    in_upper = from_behind(upper, lines, 1)
-    in_low = from_behind(low, lines, -1)
-    partial, up = pl.pallas_call(
-        lambda *refs: fold_kernel(False, *refs), out_shape=[lattice, face], name="fold_second"
-    )(partial, from_low)
-    from_low = from_behind(up, lines, 1)
-    velocity_out, displacement_out = pl.pallas_call(
-        final_kernel,
-        out_shape=[shape(*velocity.shape), shape(*velocity.shape)],
+    upper = pl.pallas_call(
+        fold_second_kernel,
+        grid=(1,),
+        in_specs=[ANYWHERE] + [whole(*FACE)] * 2,
+        out_specs=EDGE_BLOCK,
+        out_shape=folded,
+        input_output_aliases={0: 0},
+        scratch_shapes=[pltpu.VMEM((16, LINE), F32)],
+        cost_estimate=cost(1),
+        name="fold_second",
+    )(upper, edge_up, from_low)
+    in_upper = from_behind(low, lines, -1)
+    in_low = from_behind(upper, lines, 1)
+    nodal = shape(*velocity.shape)
+    velocity_part, displacement_part = pl.pallas_call(
+        update_kernel,
+        out_shape=[nodal, nodal],
         scratch_shapes=[pltpu.VMEM((96, LINE), F32)] * 2,
-        name="final_update",
+        cost_estimate=cost(2.5),
+        name="update_nodes",
     )(velocity, displacement, node_mass, first, partial, from_low)
-    fields_out = pl.pallas_call(
-        sum_kernel, out_shape=shape(ZONE_COUNT, WIDTH, dtype=BF16), name="final_sum"
-    )(middle, in_upper, in_low)
+    bottom = whole(3, 1, 4, LINE)
+    fields_out, velocity_out, displacement_out = pl.pallas_call(
+        finish_kernel,
+        grid=(1,),
+        in_specs=[
+            bottom,
+            bottom,
+            whole(1, 4, LINE),
+            whole(CAPACITY, SENT),
+            whole(FOLDED, SENT),
+            whole(CAPACITY, SENT),
+        ],
+        out_specs=[whole(ZONE_COUNT, WIDTH), bottom, bottom],
+        out_shape=[shape(ZONE_COUNT, WIDTH, dtype=BF16), nodal, nodal],
+        input_output_aliases={0: 1, 1: 2},
+        scratch_shapes=[pltpu.VMEM((16, LINE), F32)] * 2,
+        cost_estimate=cost(3),
+        name="finish_step",
+    )(velocity_part, displacement_part, node_mass, middle, in_low, in_upper)
     return (fields_out, velocity_out, displacement_out)
 
 

time: 102 us -> 88.8 us (0.87)
  the two profiles are of different devices: /device:TPU:0 before, /device:TPU:7 now
where the time goes in v2:
time: 88.8 us; the launch traced here: 88.4 us
  Pallas kernels  42.5 us (48%)
  starting transfers between devices  23.4 us (26%)
  local copies, waits for them, and re-layouts  11.9 us (13%)
  waiting for transfers between devices  10 us (11%)
    ppermute x9, starting transfers between devices, from_behind(): lax.ppermute(shard, axis, [(i, (i + by) % size) for i in range(size)])  23 us
    pallas_call x2, Pallas kernels, remap_call(): pl.pallas_call(lambda *refs: remap_kernel(step, *refs), grid=(1,), in_spe...  17.6 us
    unnamed x22, local copies, waits for them, and re-layouts  10.2 us
    ppermute x9, waiting for transfers between devices, from_behind(): lax.ppermute(shard, axis, [(i, (i + by) % size) for i in range(size)])  9.71 us
    pallas_call x1, Pallas kernels, body(): pl.pallas_call(zone_first_kernel, out_shape=[shape(4, ROWS, LINE), lattic...  7.7 us
    pallas_call x1, Pallas kernels, body(): pl.pallas_call(zone_second_kernel, out_shape=[shape(ZONE_COUNT, WIDTH, dt...  7.15 us
    pallas_call x1, Pallas kernels, body(): pl.pallas_call(finish_kernel, grid=(1,), in_specs=[bottom, bottom, whole(...  2.68 us
    pallas_call x1, Pallas kernels, body(): pl.pallas_call(update_kernel, out_shape=[nodal, nodal], scratch_shapes=[p...  2.63 us
  transfers between devices with their start and end apart: 10, of which 3 were waited for; matrix products, arithmetic and copies ran while one was open for 9% of the time, Pallas kernels for 25%

profile of v2, /device:TPU:7, one launch (start us, length us, event | category | flops | bytes accessed | tf_op | source)
XLA Modules:
  0.0 88.4 jit_solution(11599235979614763663)
XLA Ops:
  0.6 1.6 %pack_halo.1 = (f32[4,4,1024]{2,1,0:T(4,128)}, f32[4,4,1024]{2,1,0:T(4,128)}, f32[4,1,1024]{2,1,0:T(1,128)}) custom-call(f32[3,4,4,1024]{3,2,1,0:T(4,128)} %velocity_ref.5, f32[4,4,1024]{2,1,0:T(4,128)} %mass_ref.7), custom_call_target="tpu_custom_call" | custom-call | flops 1000000000 | bytes 3000000 | tf_op jit(solution)/shard_map/pack_halo/pallas_call | solution.py:481
  2.2 8.0 %collective-permute-start = (f32[4,4,1024]{2,1,0:T(4,128)}, f32[4,4,1024]{2,1,0:T(4,128)S(1)}, u32[]{:S(2)}, u32[]{:S(2)}) collective-permute-start(f32[4,4,1024]{2,1,0:T(4,128)} %get-tuple-element.29), channel_id=1, source_target_pairs={{0,248},{8,0},{16,8},{24,16},{32,24},{40,32},{48,40},{56,48},{64,5... | collective-permute-start | bytes 196616 | tf_op jit(solution)/shard_map/ppermute | solution.py:35
  10.3 1.0 %collective-permute-start.1 = (f32[4,4,1024]{2,1,0:T(4,128)}, f32[4,4,1024]{2,1,0:T(4,128)S(1)}, u32[]{:S(2)}, u32[]{:S(2)}) collective-permute-start(f32[4,4,1024]{2,1,0:T(4,128)} %get-tuple-element.30), channel_id=1, source_target_pairs={{0,7},{1,0},{2,1},{3,2},{4,3},{5,4},{6,5},{7,6},{8,15},{9,8},{10,9... | collective-permute-start | bytes 196616 | tf_op jit(solution)/shard_map/ppermute | solution.py:35
  11.6 1.7 %fusion = (bf16[1,96,64,64]{1,3,2,0:T(8,128)(2,1)S(1)}, bf16[1,96,64,64]{1,3,2,0:T(8,128)(2,1)S(1)}) fusion(bf16[2,96,64,64]{1,3,2,0:T(8,128)(2,1)} %param.15), kind=kLoop, calls=%fused_computation | loop fusion | bytes 3145728 | tf_op jit(solution)/shard_map/slice | solution.py:475
  13.3 3.1 %copy.21.refs_2_ = bf16[1,96,64,64]{3,2,1,0:T(8,128)(2,1)} copy(bf16[1,96,64,64]{1,3,2,0:T(8,128)(2,1)S(1)} %get-tuple-element.56) | data formatting | bytes 1572864
  18.0 7.7 %zone_first.1 = (f32[4,32,1024]{2,1,0:T(8,128)}, f32[3,32,1024]{2,1,0:T(8,128)}, f32[15,1024]{1,0:T(8,128)}, f32[15,1024]{1,0:T(8,128)}, f32[15,1024]{1,0:T(8,12...) custom-call(f32[3,4,4,1024]{3,2,1,0:T(4,128)} %velocity_ref.5, f32[4,4,1024]{2,1,0:T(4,128)} %mass_ref.7, ...), custom_call_target="tpu_custom_call" | custom-call | flops 7000000000 | bytes 21000000 | tf_op jit(solution)/shard_map/zone_first/pallas_call | solution.py:501
  25.7 2.5 %collective-permute-start.3 = (f32[15,1024]{1,0:T(8,128)}, f32[15,1024]{1,0:T(8,128)S(1)}, u32[]{:S(2)}, u32[]{:S(2)}) collective-permute-start(f32[15,1024]{1,0:T(8,128)} %get-tuple-element.34), channel_id=1, source_target_pairs={{0,1},{1,2},{2,3},{3,4},{4,5},{5,6},{6,7},{7,0},{8,9},{9,10},{10,1... | collective-permute-start | bytes 184328 | tf_op jit(solution)/shard_map/ppermute | solution.py:35
  28.2 8.8 %remap_step.2 = (bf16[48,2176]{1,0:T(8,128)(2,1)}, bf16[32,2176]{1,0:T(8,128)(2,1)}, bf16[48,2176]{1,0:T(8,128)(2,1)}) custom-call(bf16[256,2048]{1,0:T(8,128)(2,1)} %refs_0_.1, bf16[128,256]{1,0:T(8,128)(2,1)} %get-tuple-element.36.refs_1_, bf16[1,96,64,64]{3,2,1,0:T(8,128)(2,1)} %copy.21.refs_2_, s32[2,96]{1,0:T(2,128)} %refs_3_.3, s32[2,96]{1,0:T(2,128)} %refs_4_.3), custom_call_target="tpu_custom_call" | custom-call | flops 8999999488 | bytes 27000000 | tf_op jit(solution)/shard_map/remap_step/pallas_call | solution.py:460
  37.6 1.6 %fold_first.1 = (bf16[48,2176]{1,0:T(8,128)(2,1)}, bf16[48,2176]{1,0:T(8,128)(2,1)}) custom-call(bf16[48,2176]{1,0:T(8,128)(2,1)} %get-tuple-element.38.up_any, bf16[48,2176]{1,0:T(8,128)(2,1)} %get-tuple-element.39.down_any, f32[15,1024]{1,0:T(8,128)} %get-tuple-element.40.edge_up_ref, ...), custom_call_target="tpu_custom_call", output_to_operand_aliasing={{0}: (0, {}), {1}: (1, {})} | custom-call | flops 1000000000 | bytes 3000000 | tf_op jit(solution)/shard_map/fold_first/pallas_call | solution.py:511
  39.2 1.0 %collective-permute-start.5 = (bf16[48,2176]{1,0:T(8,128)(2,1)}, bf16[48,2176]{1,0:T(8,128)(2,1)S(1)}, u32[]{:S(2)}, u32[]{:S(2)}) collective-permute-start(bf16[48,2176]{1,0:T(8,128)(2,1)} %get-tuple-element.42), channel_id=1, source_target_pairs={{0,8},{8,16},{16,24},{24,32},{32,40},{40,48},{48,56},{56,64},{64,7... | collective-permute-start | bytes 626696 | tf_op jit(solution)/shard_map/ppermute | solution.py:35
  40.2 3.8 %collective-permute-start.6 = (bf16[48,2176]{1,0:T(8,128)(2,1)}, bf16[48,2176]{1,0:T(8,128)(2,1)S(1)}, u32[]{:S(2)}, u32[]{:S(2)}) collective-permute-start(bf16[48,2176]{1,0:T(8,128)(2,1)} %get-tuple-element.43), channel_id=1, source_target_pairs={{0,248},{8,0},{16,8},{24,16},{32,24},{40,32},{48,40},{56,48},{64,5... | collective-permute-start | bytes 626696 | tf_op jit(solution)/shard_map/ppermute | solution.py:35
  44.0 3.1 %copy.22.refs_2_ = bf16[1,96,64,64]{3,2,1,0:T(8,128)(2,1)} copy(bf16[1,96,64,64]{1,3,2,0:T(8,128)(2,1)S(1)} %get-tuple-element.55) | data formatting | bytes 1572864
  47.1 2.6 %collective-permute-done.5.in_low_ref = bf16[48,2176]{1,0:T(8,128)(2,1)S(1)} collective-permute-done((bf16[48,2176]{1,0:T(8,128)(2,1)}, bf16[48,2176]{1,0:T(8,128)(2,1)S(1)}, u32[]{:S(2)}, u32[]{:S(2)}) %collective-permute-start.5) | collective-permute-done | bytes 208928 | tf_op jit(solution)/shard_map/ppermute | solution.py:35
  49.7 0.7 copy-done
  50.5 7.2 %zone_second.1 = (bf16[256,2048]{1,0:T(8,128)(2,1)}, f32[3,32,1024]{2,1,0:T(8,128)}, f32[3,32,1024]{2,1,0:T(8,128)}, f32[15,1024]{1,0:T(8,128)}, f32[15,1024]{1,0:T(8,128)}, /*index=5*/bf16[128,256]{1,0:T(8,128)(2,1)}) custom-call(f32[4,32,1024]{2,1,0:T(8,128)} %get-tuple-element.32.state_ref, f32[3,32,1024]{2,1,0:T(8,128)} %get-tuple-element.33.first_ref, ...), custom_call_target="tpu_custom_call" | custom-call | flops 7000000000 | bytes 21000000 | tf_op jit(solution)/shard_map/zone_second/pallas_call | solution.py:524
  57.6 1.8 %collective-permute-start.7 = (f32[15,1024]{1,0:T(8,128)}, f32[15,1024]{1,0:T(8,128)S(1)}, u32[]{:S(2)}, u32[]{:S(2)}) collective-permute-start(f32[15,1024]{1,0:T(8,128)} %get-tuple-element.46), channel_id=1, source_target_pairs={{0,1},{1,2},{2,3},{3,4},{4,5},{5,6},{6,7},{7,0},{8,9},{9,10},{10,1... | collective-permute-start | bytes 184328 | tf_op jit(solution)/shard_map/ppermute | solution.py:35
  59.4 8.8 %remap_step.3 = (bf16[32,2176]{1,0:T(8,128)(2,1)}, bf16[32,2176]{1,0:T(8,128)(2,1)}, bf16[48,2176]{1,0:T(8,128)(2,1)}) custom-call(bf16[256,2048]{1,0:T(8,128)(2,1)} %get-tuple-element.49.refs_0_, bf16[128,256]{1,0:T(8,128)(2,1)} %get-tuple-element.50.refs_1_, bf16[1,96,64,64]{3,2,1,0:T(8,128)(2,1)} %copy.22.refs_2_, s32[2,96]{1,0:T(2,128)} %refs_3_.3, ...), custom_call_target="tpu_custom_call" | custom-call | flops 8999999488 | bytes 27000000 | tf_op jit(solution)/shard_map/remap_step/pallas_call | solution.py:460
  68.2 5.0 %collective-permute-start.9 = (bf16[32,2176]{1,0:T(8,128)(2,1)}, bf16[32,2176]{1,0:T(8,128)(2,1)S(1)}, u32[]{:S(2)}, u32[]{:S(2)}) collective-permute-start(bf16[32,2176]{1,0:T(8,128)(2,1)} %get-tuple-element.54), channel_id=1, source_target_pairs={{0,248},{8,0},{16,8},{24,16},{32,24},{40,32},{48,40},{56,48},{64,5... | collective-permute-start | bytes 417800 | tf_op jit(solution)/shard_map/ppermute | solution.py:35
  73.2 0.6 copy-done.8
  73.8 1.5 %fold_second.1 = bf16[48,2176]{1,0:T(8,128)(2,1)} custom-call(bf16[48,2176]{1,0:T(8,128)(2,1)} %get-tuple-element.52.up_any, f32[15,1024]{1,0:T(8,128)} %get-tuple-element.53.edge_up_ref, f32[15,1024]{1,0:T(8,128)} %copy-done.8), custom_call_target="tpu_custom_call", output_to_operand_aliasing={{}: (0, {})} | custom-call | flops 1000000000 | bytes 3000000 | tf_op jit(solution)/shard_map/fold_second/pallas_call | solution.py:533
  75.4 2.6 %update_nodes.1 = (f32[3,4,4,1024]{3,2,1,0:T(4,128)}, f32[3,4,4,1024]{3,2,1,0:T(4,128)}) custom-call(f32[3,4,4,1024]{3,2,1,0:T(4,128)} %velocity_ref.5, f32[3,4,4,1024]{3,2,1,0:T(4,128)} %displacement_ref.1, f32[4,4,1024]{2,1,0:T(4,128)} %mass_ref.7, f32[3,32,1024]{2,1,0:T(8,128)} %get-tuple-element.44.first_ref, ...), custom_call_target="tpu_custom_call" | custom-call | flops 2500000000 | bytes 7500000 | tf_op jit(solution)/shard_map/update_nodes/pallas_call | solution.py:547
  78.0 7.1 %collective-permute-done.8.in_low_ref = bf16[48,2176]{1,0:T(8,128)(2,1)S(1)} collective-permute-done((bf16[48,2176]{1,0:T(8,128)(2,1)}, bf16[48,2176]{1,0:T(8,128)(2,1)S(1)}, u32[]{:S(2)}, u32[]{:S(2)}) %collective-permute-start.8) | collective-permute-done | bytes 208928 | tf_op jit(solution)/shard_map/ppermute | solution.py:35
  85.1 0.7 copy-done.2
  85.7 2.7 %finish_step.1 = (bf16[256,2048]{1,0:T(8,128)(2,1)}, f32[3,4,4,1024]{3,2,1,0:T(4,128)}, f32[3,4,4,1024]{3,2,1,0:T(4,128)}) custom-call(f32[3,4,4,1024]{3,2,1,0:T(4,128)} %get-tuple-element.47.velocity_ref, f32[3,4,4,1024]{3,2,1,0:T(4,128)} %get-tuple-element.48.displacement_ref, ...), custom_call_target="tpu_custom_call", output_to_operand_aliasing={{1}: (0, {}), {2}: (1, {})} | custom-call | flops 3000000000 | bytes 9000000 | tf_op jit(solution)/shard_map/finish_step/pallas_call | solution.py:555
  (28 shorter events, 2.6 us)
Async XLA Ops:
  2.2 14.5 %collective-permute-start = (f32[4,4,1024]{2,1,0:T(4,128)}, f32[4,4,1024]{2,1,0:T(4,128)S(1)}, u32[]{:S(2)}, u32[]{:S(2)}) collective-permute-start(f32[4,4,1024]{2,1,0:T(4,128)} %get-tuple-element.29), channel_id=1, source_target_pairs={{0,248},{8,0},{16,8},{24,16},{32,24},{40,32},{48,40},{56,48},{64,5... | collective-permute-start | bytes 196616 | tf_op jit(solution)/shard_map/ppermute | solution.py:35
  10.3 6.5 %collective-permute-start.1 = (f32[4,4,1024]{2,1,0:T(4,128)}, f32[4,4,1024]{2,1,0:T(4,128)S(1)}, u32[]{:S(2)}, u32[]{:S(2)}) collective-permute-start(f32[4,4,1024]{2,1,0:T(4,128)} %get-tuple-element.30), channel_id=1, source_target_pairs={{0,7},{1,0},{2,1},{3,2},{4,3},{5,4},{6,5},{7,6},{8,15},{9,8},{10,9... | collective-permute-start | bytes 196616 | tf_op jit(solution)/shard_map/ppermute | solution.py:35
  11.2 5.5 %collective-permute-start.2 = (f32[4,1,1024]{2,1,0:T(1,128)}, f32[4,1,1024]{2,1,0:T(1,128)S(1)}, u32[]{:S(2)}, u32[]{:S(2)}) collective-permute-start(f32[4,1,1024]{2,1,0:T(1,128)} %get-tuple-element.31), channel_id=1, source_target_pairs={{9,0},{10,1},{11,2},{12,3},{13,4},{14,5},{15,6},{8,7},{17,8},{18,9... | collective-permute-start | bytes 49160 | tf_op jit(solution)/shard_map/ppermute | solution.py:496
  16.7 0.6 copy-start.9
  16.7 0.6 copy-start.6
  17.3 0.6 copy-start.7
  25.7 11.3 %collective-permute-start.3 = (f32[15,1024]{1,0:T(8,128)}, f32[15,1024]{1,0:T(8,128)S(1)}, u32[]{:S(2)}, u32[]{:S(2)}) collective-permute-start(f32[15,1024]{1,0:T(8,128)} %get-tuple-element.34), channel_id=1, source_target_pairs={{0,1},{1,2},{2,3},{3,4},{4,5},{5,6},{6,7},{7,0},{8,9},{9,10},{10,1... | collective-permute-start | bytes 184328 | tf_op jit(solution)/shard_map/ppermute | solution.py:35
  28.2 8.8 %collective-permute-start.4 = (f32[15,1024]{1,0:T(8,128)}, f32[15,1024]{1,0:T(8,128)S(1)}, u32[]{:S(2)}, u32[]{:S(2)}) collective-permute-start(f32[15,1024]{1,0:T(8,128)} %get-tuple-element.35), channel_id=1, source_target_pairs={{0,7},{1,0},{2,1},{3,2},{4,3},{5,4},{6,5},{7,6},{8,15},{9,8},{10,9... | collective-permute-start | bytes 184328 | tf_op jit(solution)/shard_map/ppermute | solution.py:35
  36.9 0.6 copy-start.4
  37.0 0.6 copy-start.5
  39.2 10.5 %collective-permute-start.5 = (bf16[48,2176]{1,0:T(8,128)(2,1)}, bf16[48,2176]{1,0:T(8,128)(2,1)S(1)}, u32[]{:S(2)}, u32[]{:S(2)}) collective-permute-start(bf16[48,2176]{1,0:T(8,128)(2,1)} %get-tuple-element.42), channel_id=1, source_target_pairs={{0,8},{8,16},{16,24},{24,32},{32,40},{40,48},{48,56},{56,64},{64,7... | collective-permute-start | bytes 626696 | tf_op jit(solution)/shard_map/ppermute | solution.py:35
  40.2 9.5 %collective-permute-start.6 = (bf16[48,2176]{1,0:T(8,128)(2,1)}, bf16[48,2176]{1,0:T(8,128)(2,1)S(1)}, u32[]{:S(2)}, u32[]{:S(2)}) collective-permute-start(bf16[48,2176]{1,0:T(8,128)(2,1)} %get-tuple-element.43), channel_id=1, source_target_pairs={{0,248},{8,0},{16,8},{24,16},{32,24},{40,32},{48,40},{56,48},{64,5... | collective-permute-start | bytes 626696 | tf_op jit(solution)/shard_map/ppermute | solution.py:35
  49.7 0.7 copy-start
  49.7 0.8 copy-start.1
  57.6 15.6 %collective-permute-start.7 = (f32[15,1024]{1,0:T(8,128)}, f32[15,1024]{1,0:T(8,128)S(1)}, u32[]{:S(2)}, u32[]{:S(2)}) collective-permute-start(f32[15,1024]{1,0:T(8,128)} %get-tuple-element.46), channel_id=1, source_target_pairs={{0,1},{1,2},{2,3},{3,4},{4,5},{5,6},{6,7},{7,0},{8,9},{9,10},{10,1... | collective-permute-start | bytes 184328 | tf_op jit(solution)/shard_map/ppermute | solution.py:35
  68.2 9.8 %collective-permute-start.9 = (bf16[32,2176]{1,0:T(8,128)(2,1)}, bf16[32,2176]{1,0:T(8,128)(2,1)S(1)}, u32[]{:S(2)}, u32[]{:S(2)}) collective-permute-start(bf16[32,2176]{1,0:T(8,128)(2,1)} %get-tuple-element.54), channel_id=1, source_target_pairs={{0,248},{8,0},{16,8},{24,16},{32,24},{40,32},{48,40},{56,48},{64,5... | collective-permute-start | bytes 417800 | tf_op jit(solution)/shard_map/ppermute | solution.py:35
  73.2 0.6 copy-start.8
  75.3 9.7 %collective-permute-start.8 = (bf16[48,2176]{1,0:T(8,128)(2,1)}, bf16[48,2176]{1,0:T(8,128)(2,1)S(1)}, u32[]{:S(2)}, u32[]{:S(2)}) collective-permute-start(bf16[48,2176]{1,0:T(8,128)(2,1)} %fold_second.1), channel_id=1, source_target_pairs={{0,8},{8,16},{16,24},{24,32},{32,40},{40,48},{48,56},{56,64},{64,7... | collective-permute-start | bytes 626696 | tf_op jit(solution)/shard_map/ppermute | solution.py:35
  78.0 7.1 %copy-start.3 = (bf16[32,2176]{1,0:T(8,128)(2,1)}, bf16[32,2176]{1,0:T(8,128)(2,1)S(1)}, u32[]{:S(2)}) copy-start(bf16[32,2176]{1,0:T(8,128)(2,1)S(1)} %collective-permute-done.9.in_upper_ref) | copy-start | bytes 417796
  85.1 0.7 copy-start.2

commit v3 on v2

--- a/solution.py
+++ b/solution.py
@@ -306,33 +306,41 @@
     return mm(selector, incoming[:, :WIDTH], ((0,), (0,))).astype(BF16)
 
 
-def remap_kernel(step, fields_ref, modes_ref, matrix_ref, source_ref, target_ref, low_ref, middle_ref, upper_ref,
-                 picked_ref, result_ref):
-    zone = iota((ZONE_COUNT, SLOTS), 0)
-    chosen = jnp.where(zone == source_ref[step : step + 1, :], 1.0, 0.0).astype(BF16)
+def remap_kernel(step, blocks, fields_ref, modes_ref, source_ref, target_ref, *refs):
+    number = len(blocks)
+    matrix_refs, outs = refs[:number], refs[number : 2 * number]
+    picked_ref, result_ref = refs[2 * number :]
+    slots = CAPACITY * number
+
+    def slots_of(ref):
+        pieces = [ref[step : step + 1, CAPACITY * block : CAPACITY * (block + 1)] for block in blocks]
+        return pieces[0] if number == 1 else jnp.concatenate(pieces, 1)
+
+    zone = iota((ZONE_COUNT, slots), 0)
+    chosen = jnp.where(zone == slots_of(source_ref), 1.0, 0.0).astype(BF16)
     picked = mm(chosen, fields_ref[...], ((0,), (0,)))
     new = mm(chosen, modes_ref[...].T, ((0,), (0,))).astype(BF16)
     new = mm(new, mode_columns())
-    lane = iota((SLOTS, 128), 1)
+    lane = iota((slots, 128), 1)
     group = lane // FIELDS
     renewed = lane % FIELDS < 2
     for g in range(WIDTH // 128):
         lanes = slice(128 * g, 128 * (g + 1))
         piece = jnp.where(renewed, new[:, lanes], picked[:, lanes])
         for r in range(4):
-            picked_ref[pl.ds(4 * g + r, SLOTS, stride=MODES), :] = jnp.where(group == r, piece, 0.0)
-
-    def multiply(trip, carry):
-        for inner in range(8):
-            slot = 8 * trip + inner
-            at = pl.ds(pl.multiple_of(MODES * slot, MODES), MODES)
-            result_ref[at, :] = mm(matrix_ref[0, slot], picked_ref[at, :].astype(BF16))
-        return carry
-
-    lax.fori_loop(0, SLOTS // 8, multiply, 0)
-    outs = (low_ref, middle_ref, upper_ref)
+            picked_ref[pl.ds(4 * g + r, slots, stride=MODES), :] = jnp.where(group == r, piece, 0.0)
+    for place, matrix_ref in enumerate(matrix_refs):
+
+        def multiply(trip, carry):
+            for inner in range(16):
+                slot = 16 * trip + inner
+                at = pl.ds(pl.multiple_of(MODES * (CAPACITY * place + slot), MODES), MODES)
+                result_ref[at, :] = mm(matrix_ref[0, slot], picked_ref[at, :].astype(BF16))
+            return carry
+
+        lax.fori_loop(0, CAPACITY // 16, multiply, 0)
     for g in range(WIDTH // 128):
-        rows = [result_ref[pl.ds(4 * g + r, SLOTS, stride=MODES), :] for r in range(4)]
+        rows = [result_ref[pl.ds(4 * g + r, slots, stride=MODES), :] for r in range(4)]
         total = None
         for shift in range(4):
             mixed = rows[3]
@@ -342,13 +350,13 @@
                 mixed = pltpu.roll(mixed, 128 - FIELDS * shift, 1)
             total = mixed if total is None else total + mixed
         total = total.astype(BF16)
-        for block in range(3):
-            outs[block][:, 128 * g : 128 * (g + 1)] = total[CAPACITY * block : CAPACITY * (block + 1)]
-    codes = jnp.broadcast_to(target_ref[step : step + 1, :].astype(F32), (8, SLOTS))
-    codes = jnp.where(iota((8, SLOTS), 0) == 0, codes, 0.0).astype(BF16)
+        for place in range(number):
+            outs[place][:, 128 * g : 128 * (g + 1)] = total[CAPACITY * place : CAPACITY * (place + 1)]
+    codes = jnp.broadcast_to(slots_of(target_ref).astype(F32), (8, slots))
+    codes = jnp.where(iota((8, slots), 0) == 0, codes, 0.0).astype(BF16)
     codes = mm(codes, jnp.ones((8, 128), BF16), ((0,), (0,))).astype(BF16)
-    for block in range(3):
-        outs[block][:, WIDTH:] = codes[CAPACITY * block : CAPACITY * (block + 1)]
+    for place in range(number):
+        outs[place][:, WIDTH:] = codes[CAPACITY * place : CAPACITY * (place + 1)]
 
 
 def fold_edge(edge_ref, source_row, low_ref, upper_ref, stage_ref, out_ref):
@@ -370,7 +378,7 @@
     fold_edge(edge_down_ref, 0, low_ref, upper_ref, stage_ref, down_ref)
 
 
-def fold_second_kernel(up_any, edge_up_ref, low_ref, up_ref, stage_ref):
+def fold_second_kernel(up_any, down_any, edge_up_ref, low_ref, up_ref, down_ref, stage_ref):
     fold_edge(edge_up_ref, 4, low_ref, None, stage_ref, up_ref)
 
 
@@ -452,27 +460,28 @@
     return pl.CostEstimate(flops=int(microseconds * 1e9), bytes_accessed=int(microseconds * 3e6), transcendentals=0)
 
 
+LIMIT = pltpu.CompilerParams(vmem_limit_bytes=40 * 1024 * 1024)
 ANYWHERE = pl.BlockSpec(memory_space=pl.ANY)
 EDGE_BLOCK = pl.BlockSpec((16, SENT), lambda i: (CAPACITY // 16, 0))
 
 
-def remap_call(step, fields, modes, matrix, source, target):
+def remap_call(step, blocks, rows, fields, modes, matrix, source, target):
     return pl.pallas_call(
-        lambda *refs: remap_kernel(step, *refs),
+        lambda *refs: remap_kernel(step, blocks, *refs),
         grid=(1,),
-        in_specs=[
-            whole(ZONE_COUNT, WIDTH),
-            whole(2 * MODES, ZONE_COUNT),
-            whole(1, SLOTS, MODES, MODES),
-            whole(STEPS, SLOTS),
-            whole(STEPS, SLOTS),
-        ],
-        out_specs=[whole(CAPACITY, SENT)] * 3,
-        out_shape=[shape(rows, SENT, dtype=BF16) for rows in (FOLDED if step == 0 else CAPACITY, CAPACITY, FOLDED)],
-        scratch_shapes=[pltpu.VMEM((SLOTS * MODES, 128), F32)] * 2,
-        cost_estimate=cost(9),
+        in_specs=[whole(ZONE_COUNT, WIDTH), whole(2 * MODES, ZONE_COUNT), whole(STEPS, SLOTS), whole(STEPS, SLOTS)]
+        + [pl.BlockSpec((1, CAPACITY, MODES, MODES), lambda i, block=block: (0, block, 0, 0)) for block in blocks],
+        out_specs=[whole(CAPACITY, SENT)] * len(blocks),
+        out_shape=[shape(count, SENT, dtype=BF16) for count in rows],
+        scratch_shapes=[pltpu.VMEM((CAPACITY * len(blocks) * MODES, 128), F32)] * 2,
+        compiler_params=LIMIT,
+        cost_estimate=cost(3 * len(blocks)),
         name="remap_step",
-    )(fields, modes, matrix[step : step + 1], source, target)
+    )(fields, modes, source, target, *[matrix] * len(blocks))
+
+
+def near(*arrays):
+    return [pltpu.with_memory_space_constraint(array, pltpu.VMEM) for array in arrays]
 
 
 def body(fields, velocity, displacement, node_mass, remap_matrix, remap_source, remap_target):
@@ -481,6 +490,7 @@
     send_a, send_b, send_c = pl.pallas_call(
         pack_kernel,
         out_shape=[shape(4, 4, LINE), shape(4, 4, LINE), shape(4, 1, LINE)],
+        compiler_params=LIMIT,
         cost_estimate=cost(1),
         name="pack_halo",
     )(velocity, node_mass)
@@ -502,12 +512,15 @@
         zone_first_kernel,
         out_shape=[shape(4, ROWS, LINE), lattice, face, face, face, face, modes_shape],
         scratch_shapes=[pltpu.VMEM((4 * ROWS, LINE), F32)] + zone_scratch(),
+        compiler_params=LIMIT,
         cost_estimate=cost(7),
         name="zone_first",
-    )(velocity, node_mass, halo_a, halo_b, halo_c, fields, *tables)
+    )(velocity, node_mass, *near(halo_a, halo_b, halo_c), fields, *near(*tables))
     from_low = from_behind(up, "gz", 1)
     from_up = from_behind(down, "gz", -1)
-    low, middle, upper = remap_call(0, fields, modes, remap_matrix, remap_source, remap_target)
+    index = (remap_source, remap_target)
+    matrix = remap_matrix[0:1]
+    low, upper = remap_call(0, (0, 2), (FOLDED, FOLDED), fields, modes, matrix, *index)
     upper, low = pl.pallas_call(
         fold_first_kernel,
         grid=(1,),
@@ -516,41 +529,50 @@
         out_shape=[folded, folded],
         input_output_aliases={0: 0, 1: 1},
         scratch_shapes=[pltpu.VMEM((16, LINE), F32)],
+        compiler_params=LIMIT,
         cost_estimate=cost(1),
         name="fold_first",
-    )(upper, low, edge_up, edge_down, from_low, from_up)
+    )(upper, low, edge_up, edge_down, *near(from_low, from_up))
+    near_fields, modes, upper, low = lax.optimization_barrier((fields, modes, upper, low))
     in_low = from_behind(upper, lines, 1)
     in_upper = from_behind(low, lines, -1)
+    (middle,) = remap_call(0, (1,), (CAPACITY,), near_fields, modes, matrix, *index)
     fields, first, partial, up, edge_up, modes = pl.pallas_call(
         zone_second_kernel,
         out_shape=[shape(ZONE_COUNT, WIDTH, dtype=BF16), lattice, lattice, face, face, modes_shape],
         scratch_shapes=[pltpu.VMEM((16, LINE), F32)] + zone_scratch(),
+        compiler_params=LIMIT,
         cost_estimate=cost(7),
         name="zone_second",
-    )(state, partial, from_low, from_up, middle, in_low, in_upper, *tables)
+    )(state, partial, *near(from_low, from_up), middle, *near(in_low, in_upper, *tables))
     from_low = from_behind(up, "gz", 1)
-    low, middle, upper = remap_call(1, fields, modes, remap_matrix, remap_source, remap_target)
-    upper = pl.pallas_call(
+    matrix = remap_matrix[1:2]
+    low, upper = remap_call(1, (0, 2), (CAPACITY, FOLDED), fields, modes, matrix, *index)
+    upper, low = pl.pallas_call(
         fold_second_kernel,
         grid=(1,),
-        in_specs=[ANYWHERE] + [whole(*FACE)] * 2,
-        out_specs=EDGE_BLOCK,
-        out_shape=folded,
-        input_output_aliases={0: 0},
+        in_specs=[ANYWHERE, ANYWHERE] + [whole(*FACE)] * 2,
+        out_specs=[EDGE_BLOCK, ANYWHERE],
+        out_shape=[folded, shape(CAPACITY, SENT, dtype=BF16)],
+        input_output_aliases={0: 0, 1: 1},
         scratch_shapes=[pltpu.VMEM((16, LINE), F32)],
+        compiler_params=LIMIT,
         cost_estimate=cost(1),
         name="fold_second",
-    )(upper, edge_up, from_low)
+    )(upper, low, edge_up, *near(from_low))
+    fields, modes, upper, low = lax.optimization_barrier((fields, modes, upper, low))
     in_upper = from_behind(low, lines, -1)
     in_low = from_behind(upper, lines, 1)
+    (middle,) = remap_call(1, (1,), (CAPACITY,), fields, modes, matrix, *index)
     nodal = shape(*velocity.shape)
     velocity_part, displacement_part = pl.pallas_call(
         update_kernel,
         out_shape=[nodal, nodal],
         scratch_shapes=[pltpu.VMEM((96, LINE), F32)] * 2,
+        compiler_params=LIMIT,
         cost_estimate=cost(2.5),
         name="update_nodes",
-    )(velocity, displacement, node_mass, first, partial, from_low)
+    )(velocity, displacement, node_mass, first, partial, *near(from_low))
     bottom = whole(3, 1, 4, LINE)
     fields_out, velocity_out, displacement_out = pl.pallas_call(
         finish_kernel,
@@ -567,9 +589,10 @@
         out_shape=[shape(ZONE_COUNT, WIDTH, dtype=BF16), nodal, nodal],
         input_output_aliases={0: 1, 1: 2},
         scratch_shapes=[pltpu.VMEM((16, LINE), F32)] * 2,
+        compiler_params=LIMIT,
         cost_estimate=cost(3),
         name="finish_step",
-    )(velocity_part, displacement_part, node_mass, middle, in_low, in_upper)
+    )(velocity_part, displacement_part, node_mass, middle, *near(in_low, in_upper))
     return (fields_out, velocity_out, displacement_out)
 
 

time: 88.8 us -> 69.3 us (0.78)
  Pallas kernels: 42.5 us -> 25.5 us
  waiting for transfers between devices: 10 us -> 3.93 us
  local copies, waits for them, and re-layouts: 11.9 us -> 14.3 us
  starting transfers between devices: 23.4 us -> 24.3 us
    pallas_call x3 -> x5, Pallas kernels: 19.1 us -> 12.3 us  [the longest x4 12.3 us: remap_call(): pl.pallas_call(lambda *refs: remap_kernel(step, blocks, *refs), grid=(1,)...]
    ppermute x9, waiting for transfers between devices: 9.71 us -> 3.93 us  [from_behind(): lax.ppermute(shard, axis, [(i, (i + by) % size) for i in range(size)])]
    pallas_call x1, Pallas kernels: 7.7 us -> 4.64 us  [body(): pl.pallas_call(zone_first_kernel, out_shape=[shape(4, ROWS, LINE), lattic...]
    pallas_call x1, Pallas kernels: 7.15 us -> 4.15 us  [body(): pl.pallas_call(zone_second_kernel, out_shape=[shape(ZONE_COUNT, WIDTH, dt...]
    unnamed x22 -> x38, local copies, waits for them, and re-layouts: 10.2 us -> 13.1 us
    pallas_call x1, Pallas kernels: 1.63 us -> 0.06 us  [body(): pl.pallas_call(fold_first_kernel, grid=(1,), in_specs=[ANYWHERE, ANYWHERE...]
    pallas_call x1, Pallas kernels: 2.63 us -> 1.34 us  [body(): pl.pallas_call(update_kernel, out_shape=[nodal, nodal], scratch_shapes=[p...]
    pallas_call x1, Pallas kernels: 1.61 us -> 0.67 us  [body(): pl.pallas_call(pack_kernel, out_shape=[shape(4, 4, LINE), shape(4, 4, LIN...]
  transfers between devices with their start and end apart: 10 -> 10, of which waited for: 3 -> 3; matrix products, arithmetic and copies ran while one was open for 9% -> 10% of each run, Pallas kernels for 25% -> 20%
where the time goes in v3:
time: 69.3 us; the launch traced here: 68.9 us
  Pallas kernels  25.5 us (37%)
  starting transfers between devices  24.3 us (35%)
  local copies, waits for them, and re-layouts  14.3 us (21%)
  waiting for transfers between devices  3.93 us (6%)
  between operations  0.89 us (1%)
    ppermute x9, starting transfers between devices, from_behind(): lax.ppermute(shard, axis, [(i, (i + by) % size) for i in range(size)])  23.9 us
    unnamed x38, local copies, waits for them, and re-layouts  13.1 us
    pallas_call x4, Pallas kernels, remap_call(): pl.pallas_call(lambda *refs: remap_kernel(step, blocks, *refs), grid=(1,)...  12.3 us
    pallas_call x1, Pallas kernels, body(): pl.pallas_call(zone_first_kernel, out_shape=[shape(4, ROWS, LINE), lattic...  4.64 us
    pallas_call x1, Pallas kernels, body(): pl.pallas_call(zone_second_kernel, out_shape=[shape(ZONE_COUNT, WIDTH, dt...  4.15 us
    ppermute x9, waiting for transfers between devices, from_behind(): lax.ppermute(shard, axis, [(i, (i + by) % size) for i in range(size)])  3.93 us
    pallas_call x1, Pallas kernels, body(): pl.pallas_call(finish_kernel, grid=(1,), in_specs=[bottom, bottom, whole(...  2.36 us
  transfers between devices with their start and end apart: 10, of which 3 were waited for; matrix products, arithmetic and copies ran while one was open for 10% of the time, Pallas kernels for 20%

profile of v3, /device:TPU:7, one launch (start us, length us, event | category | flops | bytes accessed | tf_op | source)
XLA Modules:
  0.0 68.9 jit_solution(1747479839929264487)
XLA Ops:
  0.6 0.9 %copy-done.2 = f32[3,4,4,1024]{3,2,1,0:T(4,128)S(1)} copy-done((f32[3,4,4,1024]{3,2,1,0:T(4,128)S(1)}, f32[3,4,4,1024]{3,2,1,0:T(4,128)}, u32[]{:S(2)}) %copy-start.2) | copy-done | bytes 196632
  3.1 8.0 %collective-permute-start = (f32[4,4,1024]{2,1,0:T(4,128)}, f32[4,4,1024]{2,1,0:T(4,128)S(1)}, u32[]{:S(2)}, u32[]{:S(2)}) collective-permute-start(f32[4,4,1024]{2,1,0:T(4,128)} %get-tuple-element.37), channel_id=1, source_target_pairs={{0,248},{8,0},{16,8},{24,16},{32,24},{40,32},{48,40},{56,48},{64,5... | collective-permute-start | bytes 196616 | tf_op jit(solution)/shard_map/ppermute | solution.py:35
  11.1 1.0 %collective-permute-start.1 = (f32[4,4,1024]{2,1,0:T(4,128)}, f32[4,4,1024]{2,1,0:T(4,128)S(1)}, u32[]{:S(2)}, u32[]{:S(2)}) collective-permute-start(f32[4,4,1024]{2,1,0:T(4,128)} %get-tuple-element.38), channel_id=1, source_target_pairs={{0,7},{1,0},{2,1},{3,2},{4,3},{5,4},{6,5},{7,6},{8,15},{9,8},{10,9... | collective-permute-start | bytes 196616 | tf_op jit(solution)/shard_map/ppermute | solution.py:35
  12.4 1.1 %fusion = (bf16[1,96,64,64]{1,3,2,0:T(8,128)(2,1)}, bf16[1,96,64,64]{1,3,2,0:T(8,128)(2,1)S(1)}) fusion(bf16[2,96,64,64]{1,3,2,0:T(8,128)(2,1)S(1)} %copy-done.17), kind=kLoop, calls=%fused_computation | loop fusion | bytes 3145728 | tf_op jit(solution)/shard_map/slice | solution.py:549
  13.6 2.3 %copy.22.refs_4_.refs_5_ = bf16[1,96,64,64]{3,2,1,0:T(8,128)(2,1)S(1)} copy(bf16[1,96,64,64]{1,3,2,0:T(8,128)(2,1)S(1)} %get-tuple-element.72) | data formatting | bytes 1572864
  15.9 3.3 %copy.23.refs_4_.refs_5_ = bf16[1,96,64,64]{3,2,1,0:T(8,128)(2,1)S(1)} copy(bf16[1,96,64,64]{1,3,2,0:T(8,128)(2,1)} %get-tuple-element.71) | data formatting | bytes 1572864
  19.3 1.2 %copy-done = bf16[256,2048]{1,0:T(8,128)(2,1)S(1)} copy-done((bf16[256,2048]{1,0:T(8,128)(2,1)S(1)}, bf16[256,2048]{1,0:T(8,128)(2,1)}, u32[]{:S(2)}) %copy-start) | copy-done | bytes 1048600
  20.6 1.4 %copy-done.9 = bf16[1536,480]{1,0:T(8,128)(2,1)S(1)} copy-done((bf16[1536,480]{1,0:T(8,128)(2,1)S(1)}, bf16[1536,480]{1,0:T(8,128)(2,1)}, u32[]{:S(2)}) %copy-start.9) | copy-done | bytes 1474584
  22.0 1.2 %copy-done.11 = bf16[320,1536]{1,0:T(8,128)(2,1)S(1)} copy-done((bf16[320,1536]{1,0:T(8,128)(2,1)S(1)}, bf16[320,1536]{1,0:T(8,128)(2,1)}, u32[]{:S(2)}) %copy-start.11) | copy-done | bytes 983064
  25.0 4.6 %zone_first.1 = (f32[4,32,1024]{2,1,0:T(8,128)S(1)}, f32[3,32,1024]{2,1,0:T(8,128)S(1)}, f32[15,1024]{1,0:T(8,128)S(1)}, f32[15,1024]{1,0:T(8,128)S(1)}, f32[15,...) custom-call(f32[3,4,4,1024]{3,2,1,0:T(4,128)S(1)} %copy-done.3, ...), custom_call_target="tpu_custom_call" | custom-call | flops 7000000000 | bytes 21000000 | tf_op jit(solution)/shard_map/zone_first/pallas_call | solution.py:511
  29.6 2.8 %collective-permute-start.3 = (f32[15,1024]{1,0:T(8,128)S(1)}, f32[15,1024]{1,0:T(8,128)S(1)}, u32[]{:S(2)}, u32[]{:S(2)}) collective-permute-start(f32[15,1024]{1,0:T(8,128)S(1)} %get-tuple-element.42), channel_id=1, source_target_pairs={{0,1},{1,2},{2,3},{3,4},{4,5},{5,6},{6,7},{7,0},{8,9},{9,10},{10,1... | collective-permute-start | bytes 184328 | tf_op jit(solution)/shard_map/ppermute | solution.py:35
  32.4 3.9 %remap_step.4 = (bf16[48,2176]{1,0:T(8,128)(2,1)S(1)}, bf16[48,2176]{1,0:T(8,128)(2,1)S(1)}) custom-call(bf16[256,2048]{1,0:T(8,128)(2,1)S(1)} %copy-done.1, bf16[128,256]{1,0:T(8,128)(2,1)S(1)} %get-tuple-element.52.refs_1_, s32[2,96]{1,0:T(2,128)S(1)} %copy-done.7, s32[2,96]{1,0:T(2,128)S(1)} %copy-done.8, ...), custom_call_target="tpu_custom_call" | custom-call | flops 6000000000 | bytes 18000000 | tf_op jit(solution)/shard_map/remap_step/pallas_call | solution.py:469
  36.4 0.9 %collective-permute-done.4.upper_ref = f32[15,1024]{1,0:T(8,128)S(1)} collective-permute-done((f32[15,1024]{1,0:T(8,128)S(1)}, f32[15,1024]{1,0:T(8,128)S(1)}, u32[]{:S(2)}, u32[]{:S(2)}) %collective-permute-start.4) | collective-permute-done | bytes 61472 | tf_op jit(solution)/shard_map/ppermute | solution.py:35
  37.4 1.3 %collective-permute-start.5 = (bf16[48,2176]{1,0:T(8,128)(2,1)S(1)}, bf16[48,2176]{1,0:T(8,128)(2,1)S(1)}, u32[]{:S(2)}, u32[]{:S(2)}) collective-permute-start(bf16[48,2176]{1,0:T(8,128)(2,1)S(1)} %get-tuple-element.53), channel_id=1, source_target_pairs={{0,8},{8,16},{16,24},{24,32},{32,40},{40,48},{48,56},{56,64},{64,7... | collective-permute-start | bytes 626696 | tf_op jit(solution)/shard_map/ppermute | solution.py:35
  38.7 3.8 %collective-permute-start.6 = (bf16[48,2176]{1,0:T(8,128)(2,1)S(1)}, bf16[48,2176]{1,0:T(8,128)(2,1)S(1)}, u32[]{:S(2)}, u32[]{:S(2)}) collective-permute-start(bf16[48,2176]{1,0:T(8,128)(2,1)S(1)} %get-tuple-element.54), channel_id=1, source_target_pairs={{0,248},{8,0},{16,8},{24,16},{32,24},{40,32},{48,40},{56,48},{64,5... | collective-permute-start | bytes 626696 | tf_op jit(solution)/shard_map/ppermute | solution.py:35
  42.5 2.2 %remap_step.5.middle_ref = bf16[32,2176]{1,0:T(8,128)(2,1)S(1)} custom-call(bf16[256,2048]{1,0:T(8,128)(2,1)S(1)} %copy-done.1, bf16[128,256]{1,0:T(8,128)(2,1)S(1)} %get-tuple-element.52.refs_1_, s32[2,96]{1,0:T(2,128)S(1)} %copy-done.7, s32[2,96]{1,0:T(2,128)S(1)} %copy-done.8, bf16[1,96,64,64]{3,2,1,0:T(8,128)(2,1)S(1)} %copy.22.refs_4_.refs_5_), custom_call_target="tpu_custom_call" | custom-call | flops 3000000000 | bytes 9000000 | tf_op jit(solution)/shard_map/remap_step/pallas_call | solution.py:469
  44.7 2.4 %collective-permute-done.5.in_low_ref = bf16[48,2176]{1,0:T(8,128)(2,1)S(1)} collective-permute-done((bf16[48,2176]{1,0:T(8,128)(2,1)S(1)}, bf16[48,2176]{1,0:T(8,128)(2,1)S(1)}, u32[]{:S(2)}, u32[]{:S(2)}) %collective-permute-start.5) | collective-permute-done | bytes 208928 | tf_op jit(solution)/shard_map/ppermute | solution.py:35
  47.2 4.2 %zone_second.1 = (bf16[256,2048]{1,0:T(8,128)(2,1)S(1)}, f32[3,32,1024]{2,1,0:T(8,128)S(1)}, f32[3,32,1024]{2,1,0:T(8,128)S(1)}, f32[15,1024]{1,0:T(8,128)S(1)},...) custom-call(f32[4,32,1024]{2,1,0:T(8,128)S(1)} %get-tuple-element.40.state_ref, ...), custom_call_target="tpu_custom_call" | custom-call | flops 7000000000 | bytes 21000000 | tf_op jit(solution)/shard_map/zone_second/pallas_call | solution.py:540
  51.4 1.7 %collective-permute-start.7 = (f32[15,1024]{1,0:T(8,128)S(1)}, f32[15,1024]{1,0:T(8,128)S(1)}, u32[]{:S(2)}, u32[]{:S(2)}) collective-permute-start(f32[15,1024]{1,0:T(8,128)S(1)} %get-tuple-element.57), channel_id=1, source_target_pairs={{0,1},{1,2},{2,3},{3,4},{4,5},{5,6},{6,7},{7,0},{8,9},{9,10},{10,1... | collective-permute-start | bytes 184328 | tf_op jit(solution)/shard_map/ppermute | solution.py:35
  53.0 3.9 %remap_step.6 = (bf16[32,2176]{1,0:T(8,128)(2,1)S(1)}, bf16[48,2176]{1,0:T(8,128)(2,1)S(1)}) custom-call(bf16[256,2048]{1,0:T(8,128)(2,1)S(1)} %get-tuple-element.67.refs_0_, bf16[128,256]{1,0:T(8,128)(2,1)S(1)} %get-tuple-element.68.refs_1_, s32[2,96]{1,0:T(2,128)S(1)} %copy-done.7, s32[2,96]{1,0:T(2,128)S(1)} %copy-done.8, ...), custom_call_target="tpu_custom_call" | custom-call | flops 6000000000 | bytes 18000000 | tf_op jit(solution)/shard_map/remap_step/pallas_call | solution.py:469
  57.1 5.4 %collective-permute-start.9 = (bf16[32,2176]{1,0:T(8,128)(2,1)S(1)}, bf16[32,2176]{1,0:T(8,128)(2,1)S(1)}, u32[]{:S(2)}, u32[]{:S(2)}) collective-permute-start(bf16[32,2176]{1,0:T(8,128)(2,1)S(1)} %get-tuple-element.70), channel_id=1, source_target_pairs={{0,248},{8,0},{16,8},{24,16},{32,24},{40,32},{48,40},{56,48},{64,5... | collective-permute-start | bytes 417800 | tf_op jit(solution)/shard_map/ppermute | solution.py:35
  62.4 2.2 %remap_step.7.middle_ref = bf16[32,2176]{1,0:T(8,128)(2,1)S(1)} custom-call(bf16[256,2048]{1,0:T(8,128)(2,1)S(1)} %get-tuple-element.67.refs_0_, bf16[128,256]{1,0:T(8,128)(2,1)S(1)} %get-tuple-element.68.refs_1_, s32[2,96]{1,0:T(2,128)S(1)} %copy-done.7, s32[2,96]{1,0:T(2,128)S(1)} %copy-done.8, bf16[1,96,64,64]{3,2,1,0:T(8,128)(2,1)S(1)} %copy.23.refs_4_.refs_5_), custom_call_target="tpu_custom_call" | custom-call | flops 3000000000 | bytes 9000000 | tf_op jit(solution)/shard_map/remap_step/pallas_call | solution.py:469
  64.7 1.3 %update_nodes.1 = (f32[3,4,4,1024]{3,2,1,0:T(4,128)}, f32[3,4,4,1024]{3,2,1,0:T(4,128)}) custom-call(f32[3,4,4,1024]{3,2,1,0:T(4,128)S(1)} %copy-done.3, f32[3,4,4,1024]{3,2,1,0:T(4,128)S(1)} %copy-done.4, f32[4,4,1024]{2,1,0:T(4,128)S(1)} %copy-done.6, f32[3,32,1024]{2,1,0:T(8,128)S(1)} %get-tuple-element.55.first_ref, ...), custom_call_target="tpu_custom_call" | custom-call | flops 2500000000 | bytes 7500000 | tf_op jit(solution)/shard_map/update_nodes/pallas_call | solution.py:568
  66.6 2.4 %finish_step.1 = (bf16[256,2048]{1,0:T(8,128)(2,1)}, f32[3,4,4,1024]{3,2,1,0:T(4,128)}, f32[3,4,4,1024]{3,2,1,0:T(4,128)}) custom-call(f32[3,4,4,1024]{3,2,1,0:T(4,128)} %get-tuple-element.58.velocity_ref, f32[3,4,4,1024]{3,2,1,0:T(4,128)} %get-tuple-element.59.displacement_ref, ...), custom_call_target="tpu_custom_call", output_to_operand_aliasing={{1}: (0, {}), {2}: (1, {})} | custom-call | flops 3000000000 | bytes 9000000 | tf_op jit(solution)/shard_map/finish_step/pallas_call | solution.py:577
  (46 shorter events, 4.5 us)
Async XLA Ops:
  2.4 10.0 %copy-start.17 = (bf16[2,96,64,64]{1,3,2,0:T(8,128)(2,1)S(1)}, bf16[2,96,64,64]{1,3,2,0:T(8,128)(2,1)}, u32[]{:S(2)}) copy-start(bf16[2,96,64,64]{1,3,2,0:T(8,128)(2,1)} %param.15) | copy-start | bytes 4718596
  3.1 16.2 %collective-permute-start = (f32[4,4,1024]{2,1,0:T(4,128)}, f32[4,4,1024]{2,1,0:T(4,128)S(1)}, u32[]{:S(2)}, u32[]{:S(2)}) collective-permute-start(f32[4,4,1024]{2,1,0:T(4,128)} %get-tuple-element.37), channel_id=1, source_target_pairs={{0,248},{8,0},{16,8},{24,16},{32,24},{40,32},{48,40},{56,48},{64,5... | collective-permute-start | bytes 196616 | tf_op jit(solution)/shard_map/ppermute | solution.py:35
  11.1 8.2 %collective-permute-start.1 = (f32[4,4,1024]{2,1,0:T(4,128)}, f32[4,4,1024]{2,1,0:T(4,128)S(1)}, u32[]{:S(2)}, u32[]{:S(2)}) collective-permute-start(f32[4,4,1024]{2,1,0:T(4,128)} %get-tuple-element.38), channel_id=1, source_target_pairs={{0,7},{1,0},{2,1},{3,2},{4,3},{5,4},{6,5},{7,6},{8,15},{9,8},{10,9... | collective-permute-start | bytes 196616 | tf_op jit(solution)/shard_map/ppermute | solution.py:35
  12.1 7.2 %collective-permute-start.2 = (f32[4,1,1024]{2,1,0:T(1,128)}, f32[4,1,1024]{2,1,0:T(1,128)S(1)}, u32[]{:S(2)}, u32[]{:S(2)}) collective-permute-start(f32[4,1,1024]{2,1,0:T(1,128)} %get-tuple-element.39), channel_id=1, source_target_pairs={{9,0},{10,1},{11,2},{12,3},{13,4},{14,5},{15,6},{8,7},{17,8},{18,9... | collective-permute-start | bytes 49160 | tf_op jit(solution)/shard_map/ppermute | solution.py:506
  15.9 3.4 %copy-start.3 = (f32[3,4,4,1024]{3,2,1,0:T(4,128)S(1)}, f32[3,4,4,1024]{3,2,1,0:T(4,128)}, u32[]{:S(2)}) copy-start(f32[3,4,4,1024]{3,2,1,0:T(4,128)} %velocity_ref.5) | copy-start | bytes 589828
  15.9 3.4 %copy-start.6 = (f32[4,4,1024]{2,1,0:T(4,128)S(1)}, f32[4,4,1024]{2,1,0:T(4,128)}, u32[]{:S(2)}) copy-start(f32[4,4,1024]{2,1,0:T(4,128)} %mass_ref.7) | copy-start | bytes 196612
  19.3 1.2 %copy-start = (bf16[256,2048]{1,0:T(8,128)(2,1)S(1)}, bf16[256,2048]{1,0:T(8,128)(2,1)}, u32[]{:S(2)}) copy-start(bf16[256,2048]{1,0:T(8,128)(2,1)} %refs_0_.2) | copy-start | bytes 3145732
  20.6 1.4 %copy-start.9 = (bf16[1536,480]{1,0:T(8,128)(2,1)S(1)}, bf16[1536,480]{1,0:T(8,128)(2,1)}, u32[]{:S(2)}) copy-start(bf16[1536,480]{1,0:T(8,128)(2,1)} %constant.8.clone.grad_ref) | copy-start | bytes 4423684
  22.0 1.2 %copy-start.11 = (bf16[320,1536]{1,0:T(8,128)(2,1)S(1)}, bf16[320,1536]{1,0:T(8,128)(2,1)}, u32[]{:S(2)}) copy-start(bf16[320,1536]{1,0:T(8,128)(2,1)} %constant.9.clone.force_ref) | copy-start | bytes 2949124
  25.0 7.5 %copy-start.1 = (bf16[256,2048]{1,0:T(8,128)(2,1)S(1)}, bf16[256,2048]{1,0:T(8,128)(2,1)}, u32[]{:S(2)}) copy-start(bf16[256,2048]{1,0:T(8,128)(2,1)} %refs_0_.2) | copy-start | bytes 3145732
  25.0 7.5 %copy-start.7 = (s32[2,96]{1,0:T(2,128)S(1)}, s32[2,96]{1,0:T(2,128)}, u32[]{:S(2)}) copy-start(s32[2,96]{1,0:T(2,128)} %refs_2_.7) | copy-start | bytes 2308
  25.0 7.5 %copy-start.8 = (s32[2,96]{1,0:T(2,128)S(1)}, s32[2,96]{1,0:T(2,128)}, u32[]{:S(2)}) copy-start(s32[2,96]{1,0:T(2,128)} %refs_3_.7) | copy-start | bytes 2308
  29.6 6.8 %collective-permute-start.3 = (f32[15,1024]{1,0:T(8,128)S(1)}, f32[15,1024]{1,0:T(8,128)S(1)}, u32[]{:S(2)}, u32[]{:S(2)}) collective-permute-start(f32[15,1024]{1,0:T(8,128)S(1)} %get-tuple-element.42), channel_id=1, source_target_pairs={{0,1},{1,2},{2,3},{3,4},{4,5},{5,6},{6,7},{7,0},{8,9},{9,10},{10,1... | collective-permute-start | bytes 184328 | tf_op jit(solution)/shard_map/ppermute | solution.py:35
  32.4 4.9 %collective-permute-start.4 = (f32[15,1024]{1,0:T(8,128)S(1)}, f32[15,1024]{1,0:T(8,128)S(1)}, u32[]{:S(2)}, u32[]{:S(2)}) collective-permute-start(f32[15,1024]{1,0:T(8,128)S(1)} %get-tuple-element.43), channel_id=1, source_target_pairs={{0,7},{1,0},{2,1},{3,2},{4,3},{5,4},{6,5},{7,6},{8,15},{9,8},{10,9... | collective-permute-start | bytes 184328 | tf_op jit(solution)/shard_map/ppermute | solution.py:35
  37.4 9.8 %copy-start.10 = (bf16[1536,480]{1,0:T(8,128)(2,1)S(1)}, bf16[1536,480]{1,0:T(8,128)(2,1)}, u32[]{:S(2)}) copy-start(bf16[1536,480]{1,0:T(8,128)(2,1)} %constant.8.clone.grad_ref) | copy-start | bytes 4423684
  37.4 9.8 %copy-start.12 = (bf16[320,1536]{1,0:T(8,128)(2,1)S(1)}, bf16[320,1536]{1,0:T(8,128)(2,1)}, u32[]{:S(2)}) copy-start(bf16[320,1536]{1,0:T(8,128)(2,1)} %constant.9.clone.force_ref) | copy-start | bytes 2949124
  37.4 9.8 %copy-start.14 = (bf16[512,128]{1,0:T(8,128)(2,1)S(1)}, bf16[512,128]{1,0:T(8,128)(2,1)}, u32[]{:S(2)}) copy-start(bf16[512,128]{1,0:T(8,128)(2,1)} %constant.10.clone.inter_ref) | copy-start | bytes 393220
  37.4 9.8 %copy-start.16 = (bf16[128,512]{1,0:T(8,128)(2,1)S(1)}, bf16[128,512]{1,0:T(8,128)(2,1)}, u32[]{:S(2)}) copy-start(bf16[128,512]{1,0:T(8,128)(2,1)} %constant.11.clone.proj_ref) | copy-start | bytes 393220
  37.4 9.7 %collective-permute-start.5 = (bf16[48,2176]{1,0:T(8,128)(2,1)S(1)}, bf16[48,2176]{1,0:T(8,128)(2,1)S(1)}, u32[]{:S(2)}, u32[]{:S(2)}) collective-permute-start(bf16[48,2176]{1,0:T(8,128)(2,1)S(1)} %get-tuple-element.53), channel_id=1, source_target_pairs={{0,8},{8,16},{16,24},{24,32},{32,40},{40,48},{48,56},{56,64},{64,7... | collective-permute-start | bytes 626696 | tf_op jit(solution)/shard_map/ppermute | solution.py:35
  38.7 8.5 %collective-permute-start.6 = (bf16[48,2176]{1,0:T(8,128)(2,1)S(1)}, bf16[48,2176]{1,0:T(8,128)(2,1)S(1)}, u32[]{:S(2)}, u32[]{:S(2)}) collective-permute-start(bf16[48,2176]{1,0:T(8,128)(2,1)S(1)} %get-tuple-element.54), channel_id=1, source_target_pairs={{0,248},{8,0},{16,8},{24,16},{32,24},{40,32},{48,40},{56,48},{64,5... | collective-permute-start | bytes 626696 | tf_op jit(solution)/shard_map/ppermute | solution.py:35
  51.4 5.6 %collective-permute-start.7 = (f32[15,1024]{1,0:T(8,128)S(1)}, f32[15,1024]{1,0:T(8,128)S(1)}, u32[]{:S(2)}, u32[]{:S(2)}) collective-permute-start(f32[15,1024]{1,0:T(8,128)S(1)} %get-tuple-element.57), channel_id=1, source_target_pairs={{0,1},{1,2},{2,3},{3,4},{4,5},{5,6},{6,7},{7,0},{8,9},{9,10},{10,1... | collective-permute-start | bytes 184328 | tf_op jit(solution)/shard_map/ppermute | solution.py:35
  57.0 7.7 %copy-start.4 = (f32[3,4,4,1024]{3,2,1,0:T(4,128)S(1)}, f32[3,4,4,1024]{3,2,1,0:T(4,128)}, u32[]{:S(2)}) copy-start(f32[3,4,4,1024]{3,2,1,0:T(4,128)} %displacement_ref.1) | copy-start | bytes 589828
  57.0 9.6 %collective-permute-start.8 = (bf16[48,2176]{1,0:T(8,128)(2,1)S(1)}, bf16[48,2176]{1,0:T(8,128)(2,1)S(1)}, u32[]{:S(2)}, u32[]{:S(2)}) collective-permute-start(bf16[48,2176]{1,0:T(8,128)(2,1)S(1)} %get-tuple-element.69), channel_id=1, source_target_pairs={{0,8},{8,16},{16,24},{24,32},{32,40},{40,48},{48,56},{56,64},{64,7... | collective-permute-start | bytes 626696 | tf_op jit(solution)/shard_map/ppermute | solution.py:35
  57.1 9.0 %collective-permute-start.9 = (bf16[32,2176]{1,0:T(8,128)(2,1)S(1)}, bf16[32,2176]{1,0:T(8,128)(2,1)S(1)}, u32[]{:S(2)}, u32[]{:S(2)}) collective-permute-start(bf16[32,2176]{1,0:T(8,128)(2,1)S(1)} %get-tuple-element.70), channel_id=1, source_target_pairs={{0,248},{8,0},{16,8},{24,16},{32,24},{40,32},{48,40},{56,48},{64,5... | collective-permute-start | bytes 417800 | tf_op jit(solution)/shard_map/ppermute | solution.py:35
  (4 other events, 3.6 us)

commit v4 on v3

--- a/solution.py
+++ b/solution.py
@@ -238,9 +238,14 @@
     modes_ref[MODES:, :] = both[:, zones:].astype(BF16)
 
 
-def zone_first_kernel(velocity_ref, mass_ref, halo_a_ref, halo_b_ref, halo_c_ref, fields_ref, grad_ref, force_ref,
-                      inter_ref, proj_ref, state_ref, lattice_ref, up_ref, edge_up_ref, down_ref, edge_down_ref, modes_ref,
-                      native_ref, *scratch):
+def zone_first_kernel(velocity_ref, mass_ref, halo_a_ref, halo_b_ref, halo_c_ref, fields_hbm, grad_hbm, force_hbm,
+                      inter_hbm, proj_hbm, state_ref, lattice_ref, up_ref, edge_up_ref, down_ref, edge_down_ref, modes_ref,
+                      native_ref, fields_ref, grad_ref, force_ref, inter_ref, proj_ref, sems, *scratch):
+    copies = fetch(
+        (fields_hbm, grad_hbm, force_hbm, inter_hbm, proj_hbm),
+        (fields_ref, grad_ref, force_ref, inter_ref, proj_ref),
+        sems,
+    )
     for comp in range(4):
         base = ROWS * comp
         native_ref[base + 24 : base + 32, :] = jnp.full((8, LINE), 1.0 if comp == 3 else 0.0, F32)
@@ -260,7 +265,10 @@
             for u in range(4):
                 lanes = slice(256 * u + 128 * half, 256 * u + 128 * (half + 1))
                 state_ref[comp, :, lanes] = moved[ROWS * comp : ROWS * (comp + 1), 128 * u : 128 * (u + 1)]
+    copies[0].wait()
     modes = pick_modes(fields_ref[...])
+    for copy in copies[1:]:
+        copy.wait()
     zone_math(lambda comp: state_ref[comp], modes, grad_ref, force_ref, inter_ref, proj_ref, *scratch,
               lattice_ref, up_ref, edge_up_ref, down_ref, edge_down_ref, modes_ref)
 
@@ -373,13 +381,9 @@
     out_ref[:, WIDTH:] = jnp.zeros((16, 128), BF16)
 
 
-def fold_first_kernel(up_any, down_any, edge_up_ref, edge_down_ref, low_ref, upper_ref, up_ref, down_ref, stage_ref):
-    fold_edge(edge_up_ref, 4, low_ref, upper_ref, stage_ref, up_ref)
-    fold_edge(edge_down_ref, 0, low_ref, upper_ref, stage_ref, down_ref)
-
-
-def fold_second_kernel(up_any, down_any, edge_up_ref, low_ref, up_ref, down_ref, stage_ref):
-    fold_edge(edge_up_ref, 4, low_ref, None, stage_ref, up_ref)
+def fold_kernel(source_row, block_any, edge_ref, *refs):
+    upper_ref = refs[1] if len(refs) == 4 else None
+    fold_edge(edge_ref, source_row, refs[0], upper_ref, refs[-1], refs[-2])
 
 
 def interleave(stage_ref, force_ref):
@@ -424,7 +428,16 @@
         displacement_out_ref[comp, 0] = displacement_ref[comp, 0] - TIME_STEP * change
 
 
-def pack_kernel(velocity_ref, mass_ref, send_a_ref, send_b_ref, send_c_ref):
+def fetch(sources, targets, sems):
+    copies = [pltpu.make_async_copy(a, b, sems.at[i]) for i, (a, b) in enumerate(zip(sources, targets))]
+    for copy in copies:
+        copy.start()
+    return copies
+
+
+def pack_kernel(velocity_hbm, mass_hbm, send_a_ref, send_b_ref, send_c_ref, velocity_ref, mass_ref, sems):
+    for copy in fetch((velocity_hbm, mass_hbm), (velocity_ref, mass_ref), sems):
+        copy.wait()
     for comp in range(4):
         for s in range(4):
             own = mass_ref[s] if comp == 3 else velocity_ref[comp, s]
@@ -461,6 +474,7 @@
 
 
 LIMIT = pltpu.CompilerParams(vmem_limit_bytes=40 * 1024 * 1024)
+FAR = pl.BlockSpec(memory_space=pltpu.HBM)
 ANYWHERE = pl.BlockSpec(memory_space=pl.ANY)
 EDGE_BLOCK = pl.BlockSpec((16, SENT), lambda i: (CAPACITY // 16, 0))
 
@@ -475,9 +489,28 @@
         out_shape=[shape(count, SENT, dtype=BF16) for count in rows],
         scratch_shapes=[pltpu.VMEM((CAPACITY * len(blocks) * MODES, 128), F32)] * 2,
         compiler_params=LIMIT,
-        cost_estimate=cost(3 * len(blocks)),
+        cost_estimate=cost(0.7),
         name="remap_step",
     )(fields, modes, source, target, *[matrix] * len(blocks))
+
+
+def far(*arrays):
+    return [pltpu.with_memory_space_constraint(array, pltpu.HBM) for array in arrays]
+
+
+def fold_call(source_row, block, edge, *faces):
+    return pl.pallas_call(
+        lambda *refs: fold_kernel(source_row, *refs),
+        grid=(1,),
+        in_specs=[ANYWHERE] + [whole(*FACE)] * (1 + len(faces)),
+        out_specs=EDGE_BLOCK,
+        out_shape=shape(FOLDED, SENT, dtype=BF16),
+        input_output_aliases={0: 0},
+        scratch_shapes=[pltpu.VMEM((16, LINE), F32)],
+        compiler_params=LIMIT,
+        cost_estimate=cost(0.5),
+        name="fold_edges",
+    )(block, edge, *near(*faces))
 
 
 def near(*arrays):
@@ -489,11 +522,17 @@
     lines = ("gx", "gy")
     send_a, send_b, send_c = pl.pallas_call(
         pack_kernel,
+        in_specs=[FAR] * 2,
         out_shape=[shape(4, 4, LINE), shape(4, 4, LINE), shape(4, 1, LINE)],
+        scratch_shapes=[
+            pltpu.VMEM((3, 4, 4, LINE), F32),
+            pltpu.VMEM((4, 4, LINE), F32),
+            pltpu.SemaphoreType.DMA((2,)),
+        ],
         compiler_params=LIMIT,
         cost_estimate=cost(1),
         name="pack_halo",
-    )(velocity, node_mass)
+    )(*far(velocity, node_mass))
     size_a = lax.axis_size(lines)
     size_b = lax.axis_size("gz")
     corner = [
@@ -510,33 +549,30 @@
     folded = shape(FOLDED, SENT, dtype=BF16)
     state, partial, up, edge_up, down, edge_down, modes = pl.pallas_call(
         zone_first_kernel,
+        in_specs=[pl.BlockSpec(memory_space=pltpu.VMEM)] * 5 + [FAR] * 5,
         out_shape=[shape(4, ROWS, LINE), lattice, face, face, face, face, modes_shape],
-        scratch_shapes=[pltpu.VMEM((4 * ROWS, LINE), F32)] + zone_scratch(),
+        scratch_shapes=[pltpu.VMEM((4 * ROWS, LINE), F32)]
+        + [pltpu.VMEM(array.shape, array.dtype) for array in (fields,) + tables]
+        + [pltpu.SemaphoreType.DMA((5,))]
+        + zone_scratch(),
         compiler_params=LIMIT,
         cost_estimate=cost(7),
         name="zone_first",
-    )(velocity, node_mass, *near(halo_a, halo_b, halo_c), fields, *near(*tables))
+    )(velocity, node_mass, *near(halo_a, halo_b, halo_c), *far(fields, *tables))
     from_low = from_behind(up, "gz", 1)
     from_up = from_behind(down, "gz", -1)
     index = (remap_source, remap_target)
     matrix = remap_matrix[0:1]
-    low, upper = remap_call(0, (0, 2), (FOLDED, FOLDED), fields, modes, matrix, *index)
-    upper, low = pl.pallas_call(
-        fold_first_kernel,
-        grid=(1,),
-        in_specs=[ANYWHERE, ANYWHERE] + [whole(*FACE)] * 4,
-        out_specs=[EDGE_BLOCK, EDGE_BLOCK],
-        out_shape=[folded, folded],
-        input_output_aliases={0: 0, 1: 1},
-        scratch_shapes=[pltpu.VMEM((16, LINE), F32)],
-        compiler_params=LIMIT,
-        cost_estimate=cost(1),
-        name="fold_first",
-    )(upper, low, edge_up, edge_down, *near(from_low, from_up))
-    near_fields, modes, upper, low = lax.optimization_barrier((fields, modes, upper, low))
+    matrix_late = remap_matrix[1:2]
+    (upper,) = remap_call(0, (2,), (FOLDED,), fields, modes, matrix, *index)
+    upper = fold_call(4, upper, edge_up, from_low, from_up)
+    fields, modes, upper = lax.optimization_barrier((fields, modes, upper))
     in_low = from_behind(upper, lines, 1)
+    (low,) = remap_call(0, (0,), (FOLDED,), fields, modes, matrix, *index)
+    low = fold_call(0, low, edge_down, from_low, from_up)
+    fields, modes, low, matrix_late = lax.optimization_barrier((fields, modes, low, matrix_late))
     in_upper = from_behind(low, lines, -1)
-    (middle,) = remap_call(0, (1,), (CAPACITY,), near_fields, modes, matrix, *index)
+    (middle,) = remap_call(0, (1,), (CAPACITY,), fields, modes, matrix, *index)
     fields, first, partial, up, edge_up, modes = pl.pallas_call(
         zone_second_kernel,
         out_shape=[shape(ZONE_COUNT, WIDTH, dtype=BF16), lattice, lattice, face, face, modes_shape],
@@ -546,22 +582,13 @@
         name="zone_second",
     )(state, partial, *near(from_low, from_up), middle, *near(in_low, in_upper, *tables))
     from_low = from_behind(up, "gz", 1)
-    matrix = remap_matrix[1:2]
-    low, upper = remap_call(1, (0, 2), (CAPACITY, FOLDED), fields, modes, matrix, *index)
-    upper, low = pl.pallas_call(
-        fold_second_kernel,
-        grid=(1,),
-        in_specs=[ANYWHERE, ANYWHERE] + [whole(*FACE)] * 2,
-        out_specs=[EDGE_BLOCK, ANYWHERE],
-        out_shape=[folded, shape(CAPACITY, SENT, dtype=BF16)],
-        input_output_aliases={0: 0, 1: 1},
-        scratch_shapes=[pltpu.VMEM((16, LINE), F32)],
-        compiler_params=LIMIT,
-        cost_estimate=cost(1),
-        name="fold_second",
-    )(upper, low, edge_up, *near(from_low))
-    fields, modes, upper, low = lax.optimization_barrier((fields, modes, upper, low))
+    matrix = matrix_late
+    (low,) = remap_call(1, (0,), (CAPACITY,), fields, modes, matrix, *index)
+    fields, modes, low = lax.optimization_barrier((fields, modes, low))
     in_upper = from_behind(low, lines, -1)
+    (upper,) = remap_call(1, (2,), (FOLDED,), fields, modes, matrix, *index)
+    upper = fold_call(4, upper, edge_up, from_low)
+    fields, modes, upper = lax.optimization_barrier((fields, modes, upper))
     in_low = from_behind(upper, lines, 1)
     (middle,) = remap_call(1, (1,), (CAPACITY,), fields, modes, matrix, *index)
     nodal = shape(*velocity.shape)

time: 69.3 us -> 67.7 us (0.977)
  the two profiles are of different devices: /device:TPU:7 before, /device:TPU:1 now
where the time goes in v4:
time: 67.7 us; the launch traced here: 67.5 us
  Pallas kernels  29.4 us (43%)
  starting transfers between devices  20.2 us (30%)
  waiting for transfers between devices  10.2 us (15%)
  local copies, waits for them, and re-layouts  6.9 us (10%)
  between operations  0.9 us (1%)
    pallas_call x6, Pallas kernels, remap_call(): pl.pallas_call(lambda *refs: remap_kernel(step, blocks, *refs), grid=(1,)...  13.4 us
    ppermute x9, starting transfers between devices, from_behind(): lax.ppermute(shard, axis, [(i, (i + by) % size) for i in range(size)])  10.7 us
    ppermute x9, waiting for transfers between devices, from_behind(): lax.ppermute(shard, axis, [(i, (i + by) % size) for i in range(size)])  10.2 us
    ppermute x1, starting transfers between devices, body(): halo_c = lax.ppermute(send_c, ('gx', 'gy', 'gz'), corner)  9.49 us
    pallas_call x1, Pallas kernels, body(): pl.pallas_call(zone_first_kernel, in_specs=[pl.BlockSpec(memory_space=plt...  6.18 us
    pallas_call x1, Pallas kernels, body(): pl.pallas_call(zone_second_kernel, out_shape=[shape(ZONE_COUNT, WIDTH, dt...  4.29 us
    unnamed x23, local copies, waits for them, and re-layouts  3.41 us
    pallas_call x1, Pallas kernels, body(): pl.pallas_call(finish_kernel, grid=(1,), in_specs=[bottom, bottom, whole(...  2.37 us
  transfers between devices with their start and end apart: 10, of which 4 were waited for; matrix products, arithmetic and copies ran while one was open for 10% of the time, Pallas kernels for 19%

profile of v4, /device:TPU:1, one launch (start us, length us, event | category | flops | bytes accessed | tf_op | source)
XLA Modules:
  0.0 67.5 jit_solution(12821743697798777110)
XLA Ops:
  0.6 1.8 %pack_halo.1 = (f32[4,4,1024]{2,1,0:T(4,128)}, f32[4,4,1024]{2,1,0:T(4,128)}, f32[4,1,1024]{2,1,0:T(1,128)}) custom-call(f32[3,4,4,1024]{3,2,1,0:T(4,128)} %velocity_ref.3, f32[4,4,1024]{2,1,0:T(4,128)} %mass_ref.5), custom_call_target="tpu_custom_call" | custom-call | flops 1000000000 | bytes 3000000 | tf_op jit(solution)/shard_map/pack_halo/pallas_call | solution.py:523
  2.4 9.5 %collective-permute-start.2 = (f32[4,1,1024]{2,1,0:T(1,128)}, f32[4,1,1024]{2,1,0:T(1,128)S(1)}, u32[]{:S(2)}, u32[]{:S(2)}) collective-permute-start(f32[4,1,1024]{2,1,0:T(1,128)} %get-tuple-element.36), channel_id=1, source_target_pairs={{9,0},{10,1},{11,2},{12,3},{13,4},{14,5},{15,6},{8,7},{17,8},{18,9... | collective-permute-start | bytes 49160 | tf_op jit(solution)/shard_map/ppermute | solution.py:545
  12.4 2.3 %collective-permute-start.1 = (f32[4,4,1024]{2,1,0:T(4,128)}, f32[4,4,1024]{2,1,0:T(4,128)S(1)}, u32[]{:S(2)}, u32[]{:S(2)}) collective-permute-start(f32[4,4,1024]{2,1,0:T(4,128)} %get-tuple-element.35), channel_id=1, source_target_pairs={{0,7},{1,0},{2,1},{3,2},{4,3},{5,4},{6,5},{7,6},{8,15},{9,8},{10,9... | collective-permute-start | bytes 196616 | tf_op jit(solution)/shard_map/ppermute | solution.py:35
  14.7 1.1 %fusion = (bf16[1,96,64,64]{1,3,2,0:T(8,128)(2,1)S(1)}, bf16[1,96,64,64]{1,3,2,0:T(8,128)(2,1)}) fusion(bf16[2,96,64,64]{1,3,2,0:T(8,128)(2,1)S(1)} %copy-done.10), kind=kLoop, calls=%fused_computation | loop fusion | bytes 3145728 | tf_op jit(solution)/shard_map/slice | solution.py:566
  15.8 2.3 %copy.22.refs_4_ = bf16[1,96,64,64]{3,2,1,0:T(8,128)(2,1)S(1)} copy(bf16[1,96,64,64]{1,3,2,0:T(8,128)(2,1)S(1)} %get-tuple-element.65) | data formatting | bytes 1572864 | tf_op jit(solution)/shard_map/optimization_barrier | solution.py:573
  18.2 3.3 %copy.21.refs_4_ = bf16[1,96,64,64]{3,2,1,0:T(8,128)(2,1)S(1)} copy(bf16[1,96,64,64]{1,3,2,0:T(8,128)(2,1)} %get-tuple-element.66) | data formatting | bytes 1572864
  21.6 6.2 %zone_first.1 = (f32[4,32,1024]{2,1,0:T(8,128)S(1)}, f32[3,32,1024]{2,1,0:T(8,128)S(1)}, f32[15,1024]{1,0:T(8,128)S(1)}, f32[15,1024]{1,0:T(8,128)S(1)}, f32[15,...) custom-call(f32[3,4,4,1024]{3,2,1,0:T(4,128)S(1)} %copy-done.3, ...), custom_call_target="tpu_custom_call" | custom-call | flops 7000000000 | bytes 21000000 | tf_op jit(solution)/shard_map/zone_first/pallas_call | solution.py:550
  27.9 0.6 collective-permute-start.4
  28.5 2.3 %remap_step.6.refs_0_ = bf16[48,2176]{1,0:T(8,128)(2,1)S(1)} custom-call(bf16[256,2048]{1,0:T(8,128)(2,1)S(1)} %copy-done, bf16[128,256]{1,0:T(8,128)(2,1)S(1)} %get-tuple-element.47.refs_1_, s32[2,96]{1,0:T(2,128)S(1)} %copy-done.1, s32[2,96]{1,0:T(2,128)S(1)} %copy-done.2, bf16[1,96,64,64]{3,2,1,0:T(8,128)(2,1)S(1)} %copy.21.refs_4_), custom_call_target="tpu_custom_call" | custom-call | flops 700000000 | bytes 2100000 | tf_op jit(solution)/shard_map/remap_step/pallas_call | solution.py:483
  30.7 0.8 %collective-permute-done.4.refs_3_.upper_ref = f32[15,1024]{1,0:T(8,128)S(1)} collective-permute-done((f32[15,1024]{1,0:T(8,128)S(1)}, f32[15,1024]{1,0:T(8,128)S(1)}, u32[]{:S(2)}, u32[]{:S(2)}) %collective-permute-start.4) | collective-permute-done | bytes 61472 | tf_op jit(solution)/shard_map/ppermute | solution.py:35
  31.6 2.2 %remap_step.7.refs_0_ = bf16[48,2176]{1,0:T(8,128)(2,1)S(1)} custom-call(bf16[256,2048]{1,0:T(8,128)(2,1)S(1)} %copy-done, bf16[128,256]{1,0:T(8,128)(2,1)S(1)} %get-tuple-element.47.refs_1_, s32[2,96]{1,0:T(2,128)S(1)} %copy-done.1, s32[2,96]{1,0:T(2,128)S(1)} %copy-done.2, bf16[1,96,64,64]{3,2,1,0:T(8,128)(2,1)S(1)} %copy.21.refs_4_), custom_call_target="tpu_custom_call" | custom-call | flops 700000000 | bytes 2100000 | tf_op jit(solution)/shard_map/remap_step/pallas_call | solution.py:483
  34.3 1.3 %collective-permute-start.5 = (bf16[48,2176]{1,0:T(8,128)(2,1)S(1)}, bf16[48,2176]{1,0:T(8,128)(2,1)S(1)}, u32[]{:S(2)}, u32[]{:S(2)}) collective-permute-start(bf16[48,2176]{1,0:T(8,128)(2,1)S(1)} %fold_edges.3), channel_id=1, source_target_pairs={{0,8},{8,16},{16,24},{24,32},{32,40},{40,48},{48,56},{56,64},{64,7... | collective-permute-start | bytes 626696 | tf_op jit(solution)/shard_map/ppermute | solution.py:35
  35.6 2.2 %remap_step.8.middle_ref = bf16[32,2176]{1,0:T(8,128)(2,1)S(1)} custom-call(bf16[256,2048]{1,0:T(8,128)(2,1)S(1)} %copy-done, bf16[128,256]{1,0:T(8,128)(2,1)S(1)} %get-tuple-element.47.refs_1_, s32[2,96]{1,0:T(2,128)S(1)} %copy-done.1, s32[2,96]{1,0:T(2,128)S(1)} %copy-done.2, bf16[1,96,64,64]{3,2,1,0:T(8,128)(2,1)S(1)} %copy.21.refs_4_), custom_call_target="tpu_custom_call" | custom-call | flops 700000000 | bytes 2100000 | tf_op jit(solution)/shard_map/remap_step/pallas_call | solution.py:483
  37.9 0.9 %collective-permute-done.6.in_upper_ref = bf16[48,2176]{1,0:T(8,128)(2,1)S(1)} collective-permute-done((bf16[48,2176]{1,0:T(8,128)(2,1)S(1)}, bf16[48,2176]{1,0:T(8,128)(2,1)S(1)}, u32[]{:S(2)}, u32[]{:S(2)}) %collective-permute-start.6) | collective-permute-done | bytes 208928 | tf_op jit(solution)/shard_map/ppermute | solution.py:35
  38.8 3.5 %collective-permute-done.5.in_low_ref = bf16[48,2176]{1,0:T(8,128)(2,1)S(1)} collective-permute-done((bf16[48,2176]{1,0:T(8,128)(2,1)S(1)}, bf16[48,2176]{1,0:T(8,128)(2,1)S(1)}, u32[]{:S(2)}, u32[]{:S(2)}) %collective-permute-start.5) | collective-permute-done | bytes 208928 | tf_op jit(solution)/shard_map/ppermute | solution.py:35
  42.3 4.3 %zone_second.1 = (bf16[256,2048]{1,0:T(8,128)(2,1)S(1)}, f32[3,32,1024]{2,1,0:T(8,128)S(1)}, f32[3,32,1024]{2,1,0:T(8,128)S(1)}, f32[15,1024]{1,0:T(8,128)S(1)},...) custom-call(f32[4,32,1024]{2,1,0:T(8,128)S(1)} %get-tuple-element.37.state_ref, ...), custom_call_target="tpu_custom_call" | custom-call | flops 7000000000 | bytes 21000000 | tf_op jit(solution)/shard_map/zone_second/pallas_call | solution.py:576
  46.6 3.7 %collective-permute-start.7 = (f32[15,1024]{1,0:T(8,128)S(1)}, f32[15,1024]{1,0:T(8,128)S(1)}, u32[]{:S(2)}, u32[]{:S(2)}) collective-permute-start(f32[15,1024]{1,0:T(8,128)S(1)} %get-tuple-element.52), channel_id=1, source_target_pairs={{0,1},{1,2},{2,3},{3,4},{4,5},{5,6},{6,7},{7,0},{8,9},{9,10},{10,1... | collective-permute-start | bytes 184328 | tf_op jit(solution)/shard_map/ppermute | solution.py:35
  50.3 2.2 %remap_step.9 = bf16[32,2176]{1,0:T(8,128)(2,1)S(1)} custom-call(bf16[256,2048]{1,0:T(8,128)(2,1)S(1)} %get-tuple-element.61.refs_0_, bf16[128,256]{1,0:T(8,128)(2,1)S(1)} %get-tuple-element.62.refs_1_, s32[2,96]{1,0:T(2,128)S(1)} %copy-done.1, s32[2,96]{1,0:T(2,128)S(1)} %copy-done.2, bf16[1,96,64,64]{3,2,1,0:T(8,128)(2,1)S(1)} %copy.22.refs_4_), custom_call_target="tpu_custom_call" | custom-call | flops 700000000 | bytes 2100000 | tf_op jit(solution)/shard_map/remap_step/pallas_call | solution.py:483
  52.6 2.3 %remap_step.10.refs_0_ = bf16[48,2176]{1,0:T(8,128)(2,1)S(1)} custom-call(bf16[256,2048]{1,0:T(8,128)(2,1)S(1)} %get-tuple-element.61.refs_0_, bf16[128,256]{1,0:T(8,128)(2,1)S(1)} %get-tuple-element.62.refs_1_, s32[2,96]{1,0:T(2,128)S(1)} %copy-done.1, s32[2,96]{1,0:T(2,128)S(1)} %copy-done.2, bf16[1,96,64,64]{3,2,1,0:T(8,128)(2,1)S(1)} %copy.22.refs_4_), custom_call_target="tpu_custom_call" | custom-call | flops 700000000 | bytes 2100000 | tf_op jit(solution)/shard_map/remap_step/pallas_call | solution.py:483
  54.9 1.7 %collective-permute-start.8 = (bf16[48,2176]{1,0:T(8,128)(2,1)S(1)}, bf16[48,2176]{1,0:T(8,128)(2,1)S(1)}, u32[]{:S(2)}, u32[]{:S(2)}) collective-permute-start(bf16[48,2176]{1,0:T(8,128)(2,1)S(1)} %fold_edges.5), channel_id=1, source_target_pairs={{0,8},{8,16},{16,24},{24,32},{32,40},{40,48},{48,56},{56,64},{64,7... | collective-permute-start | bytes 626696 | tf_op jit(solution)/shard_map/ppermute | solution.py:35
  56.7 1.3 %update_nodes.1 = (f32[3,4,4,1024]{3,2,1,0:T(4,128)}, f32[3,4,4,1024]{3,2,1,0:T(4,128)}) custom-call(f32[3,4,4,1024]{3,2,1,0:T(4,128)S(1)} %copy-done.3, f32[3,4,4,1024]{3,2,1,0:T(4,128)S(1)} %copy-done.4, f32[4,4,1024]{2,1,0:T(4,128)S(1)} %copy-done.5, f32[3,32,1024]{2,1,0:T(8,128)S(1)} %get-tuple-element.50.first_ref, ...), custom_call_target="tpu_custom_call" | custom-call | flops 2500000000 | bytes 7500000 | tf_op jit(solution)/shard_map/update_nodes/pallas_call | solution.py:595
  58.0 2.2 %remap_step.11.middle_ref = bf16[32,2176]{1,0:T(8,128)(2,1)S(1)} custom-call(bf16[256,2048]{1,0:T(8,128)(2,1)S(1)} %get-tuple-element.61.refs_0_, bf16[128,256]{1,0:T(8,128)(2,1)S(1)} %get-tuple-element.62.refs_1_, s32[2,96]{1,0:T(2,128)S(1)} %copy-done.1, s32[2,96]{1,0:T(2,128)S(1)} %copy-done.2, bf16[1,96,64,64]{3,2,1,0:T(8,128)(2,1)S(1)} %copy.22.refs_4_), custom_call_target="tpu_custom_call" | custom-call | flops 700000000 | bytes 2100000 | tf_op jit(solution)/shard_map/remap_step/pallas_call | solution.py:483
  60.3 4.9 %collective-permute-done.8.in_low_ref = bf16[48,2176]{1,0:T(8,128)(2,1)S(1)} collective-permute-done((bf16[48,2176]{1,0:T(8,128)(2,1)S(1)}, bf16[48,2176]{1,0:T(8,128)(2,1)S(1)}, u32[]{:S(2)}, u32[]{:S(2)}) %collective-permute-start.8) | collective-permute-done | bytes 208928 | tf_op jit(solution)/shard_map/ppermute | solution.py:35
  65.1 2.4 %finish_step.1 = (bf16[256,2048]{1,0:T(8,128)(2,1)}, f32[3,4,4,1024]{3,2,1,0:T(4,128)}, f32[3,4,4,1024]{3,2,1,0:T(4,128)}) custom-call(f32[3,4,4,1024]{3,2,1,0:T(4,128)} %get-tuple-element.53.velocity_ref, f32[3,4,4,1024]{3,2,1,0:T(4,128)} %get-tuple-element.54.displacement_ref, ...), custom_call_target="tpu_custom_call", output_to_operand_aliasing={{1}: (0, {}), {2}: (1, {})} | custom-call | flops 3000000000 | bytes 9000000 | tf_op jit(solution)/shard_map/finish_step/pallas_call | solution.py:604
  (35 shorter events, 1.2 us)
Async XLA Ops:
  0.6 14.1 %copy-start.10 = (bf16[2,96,64,64]{1,3,2,0:T(8,128)(2,1)S(1)}, bf16[2,96,64,64]{1,3,2,0:T(8,128)(2,1)}, u32[]{:S(2)}) copy-start(bf16[2,96,64,64]{1,3,2,0:T(8,128)(2,1)} %param.15) | copy-start | bytes 4718596
  2.4 19.2 %collective-permute-start.2 = (f32[4,1,1024]{2,1,0:T(1,128)}, f32[4,1,1024]{2,1,0:T(1,128)S(1)}, u32[]{:S(2)}, u32[]{:S(2)}) collective-permute-start(f32[4,1,1024]{2,1,0:T(1,128)} %get-tuple-element.36), channel_id=1, source_target_pairs={{9,0},{10,1},{11,2},{12,3},{13,4},{14,5},{15,6},{8,7},{17,8},{18,9... | collective-permute-start | bytes 49160 | tf_op jit(solution)/shard_map/ppermute | solution.py:545
  11.9 9.7 %collective-permute-start = (f32[4,4,1024]{2,1,0:T(4,128)}, f32[4,4,1024]{2,1,0:T(4,128)S(1)}, u32[]{:S(2)}, u32[]{:S(2)}) collective-permute-start(f32[4,4,1024]{2,1,0:T(4,128)} %get-tuple-element.34), channel_id=1, source_target_pairs={{0,248},{8,0},{16,8},{24,16},{32,24},{40,32},{48,40},{56,48},{64,5... | collective-permute-start | bytes 196616 | tf_op jit(solution)/shard_map/ppermute | solution.py:35
  12.4 9.2 %collective-permute-start.1 = (f32[4,4,1024]{2,1,0:T(4,128)}, f32[4,4,1024]{2,1,0:T(4,128)S(1)}, u32[]{:S(2)}, u32[]{:S(2)}) collective-permute-start(f32[4,4,1024]{2,1,0:T(4,128)} %get-tuple-element.35), channel_id=1, source_target_pairs={{0,7},{1,0},{2,1},{3,2},{4,3},{5,4},{6,5},{7,6},{8,15},{9,8},{10,9... | collective-permute-start | bytes 196616 | tf_op jit(solution)/shard_map/ppermute | solution.py:35
  18.2 3.4 %copy-start.3 = (f32[3,4,4,1024]{3,2,1,0:T(4,128)S(1)}, f32[3,4,4,1024]{3,2,1,0:T(4,128)}, u32[]{:S(2)}) copy-start(f32[3,4,4,1024]{3,2,1,0:T(4,128)} %velocity_ref.3) | copy-start | bytes 589828
  18.2 3.4 %copy-start.5 = (f32[4,4,1024]{2,1,0:T(4,128)S(1)}, f32[4,4,1024]{2,1,0:T(4,128)}, u32[]{:S(2)}) copy-start(f32[4,4,1024]{2,1,0:T(4,128)} %mass_ref.5) | copy-start | bytes 196612
  21.6 6.9 %copy-start = (bf16[256,2048]{1,0:T(8,128)(2,1)S(1)}, bf16[256,2048]{1,0:T(8,128)(2,1)}, u32[]{:S(2)}) copy-start(bf16[256,2048]{1,0:T(8,128)(2,1)} %refs_0_.3) | copy-start | bytes 3145732
  21.6 6.9 %copy-start.1 = (s32[2,96]{1,0:T(2,128)S(1)}, s32[2,96]{1,0:T(2,128)}, u32[]{:S(2)}) copy-start(s32[2,96]{1,0:T(2,128)} %refs_2_.11) | copy-start | bytes 2308
  21.6 6.9 %copy-start.2 = (s32[2,96]{1,0:T(2,128)S(1)}, s32[2,96]{1,0:T(2,128)}, u32[]{:S(2)}) copy-start(s32[2,96]{1,0:T(2,128)} %refs_3_.11) | copy-start | bytes 2308
  27.8 2.9 %collective-permute-start.3 = (f32[15,1024]{1,0:T(8,128)S(1)}, f32[15,1024]{1,0:T(8,128)S(1)}, u32[]{:S(2)}, u32[]{:S(2)}) collective-permute-start(f32[15,1024]{1,0:T(8,128)S(1)} %get-tuple-element.39), channel_id=1, source_target_pairs={{0,1},{1,2},{2,3},{3,4},{4,5},{5,6},{6,7},{7,0},{8,9},{9,10},{10,1... | collective-permute-start | bytes 184328 | tf_op jit(solution)/shard_map/ppermute | solution.py:35
  27.9 3.7 %collective-permute-start.4 = (f32[15,1024]{1,0:T(8,128)S(1)}, f32[15,1024]{1,0:T(8,128)S(1)}, u32[]{:S(2)}, u32[]{:S(2)}) collective-permute-start(f32[15,1024]{1,0:T(8,128)S(1)} %get-tuple-element.40), channel_id=1, source_target_pairs={{0,7},{1,0},{2,1},{3,2},{4,3},{5,4},{6,5},{7,6},{8,15},{9,8},{10,9... | collective-permute-start | bytes 184328 | tf_op jit(solution)/shard_map/ppermute | solution.py:35
  33.8 8.5 %copy-start.6 = (bf16[1536,480]{1,0:T(8,128)(2,1)S(1)}, bf16[1536,480]{1,0:T(8,128)(2,1)}, u32[]{:S(2)}) copy-start(bf16[1536,480]{1,0:T(8,128)(2,1)} %constant.8.clone.grad_hbm.grad_ref) | copy-start | bytes 4423684
  33.9 8.4 %copy-start.7 = (bf16[320,1536]{1,0:T(8,128)(2,1)S(1)}, bf16[320,1536]{1,0:T(8,128)(2,1)}, u32[]{:S(2)}) copy-start(bf16[320,1536]{1,0:T(8,128)(2,1)} %constant.9.clone.force_hbm.force_ref) | copy-start | bytes 2949124
  33.9 8.4 %copy-start.8 = (bf16[128,512]{1,0:T(8,128)(2,1)S(1)}, bf16[128,512]{1,0:T(8,128)(2,1)}, u32[]{:S(2)}) copy-start(bf16[128,512]{1,0:T(8,128)(2,1)} %constant.11.clone.proj_hbm.proj_ref) | copy-start | bytes 393220
  33.9 8.4 %copy-start.9 = (bf16[512,128]{1,0:T(8,128)(2,1)S(1)}, bf16[512,128]{1,0:T(8,128)(2,1)}, u32[]{:S(2)}) copy-start(bf16[512,128]{1,0:T(8,128)(2,1)} %constant.10.clone.inter_hbm.inter_ref) | copy-start | bytes 393220
  33.9 4.9 %collective-permute-start.6 = (bf16[48,2176]{1,0:T(8,128)(2,1)S(1)}, bf16[48,2176]{1,0:T(8,128)(2,1)S(1)}, u32[]{:S(2)}, u32[]{:S(2)}) collective-permute-start(bf16[48,2176]{1,0:T(8,128)(2,1)S(1)} %fold_edges.4), channel_id=1, source_target_pairs={{0,248},{8,0},{16,8},{24,16},{32,24},{40,32},{48,40},{56,48},{64,5... | collective-permute-start | bytes 626696 | tf_op jit(solution)/shard_map/ppermute | solution.py:35
  34.3 8.0 %collective-permute-start.5 = (bf16[48,2176]{1,0:T(8,128)(2,1)S(1)}, bf16[48,2176]{1,0:T(8,128)(2,1)S(1)}, u32[]{:S(2)}, u32[]{:S(2)}) collective-permute-start(bf16[48,2176]{1,0:T(8,128)(2,1)S(1)} %fold_edges.3), channel_id=1, source_target_pairs={{0,8},{8,16},{16,24},{24,32},{32,40},{40,48},{48,56},{56,64},{64,7... | collective-permute-start | bytes 626696 | tf_op jit(solution)/shard_map/ppermute | solution.py:35
  46.6 8.3 %collective-permute-start.7 = (f32[15,1024]{1,0:T(8,128)S(1)}, f32[15,1024]{1,0:T(8,128)S(1)}, u32[]{:S(2)}, u32[]{:S(2)}) collective-permute-start(f32[15,1024]{1,0:T(8,128)S(1)} %get-tuple-element.52), channel_id=1, source_target_pairs={{0,1},{1,2},{2,3},{3,4},{4,5},{5,6},{6,7},{7,0},{8,9},{9,10},{10,1... | collective-permute-start | bytes 184328 | tf_op jit(solution)/shard_map/ppermute | solution.py:35
  52.5 7.7 %collective-permute-start.9 = (bf16[32,2176]{1,0:T(8,128)(2,1)S(1)}, bf16[32,2176]{1,0:T(8,128)(2,1)S(1)}, u32[]{:S(2)}, u32[]{:S(2)}) collective-permute-start(bf16[32,2176]{1,0:T(8,128)(2,1)S(1)} %remap_step.9), channel_id=1, source_target_pairs={{0,248},{8,0},{16,8},{24,16},{32,24},{40,32},{48,40},{56,48},{64,5... | collective-permute-start | bytes 417800 | tf_op jit(solution)/shard_map/ppermute | solution.py:35
  54.9 1.8 %copy-start.4 = (f32[3,4,4,1024]{3,2,1,0:T(4,128)S(1)}, f32[3,4,4,1024]{3,2,1,0:T(4,128)}, u32[]{:S(2)}) copy-start(f32[3,4,4,1024]{3,2,1,0:T(4,128)} %displacement_ref.1) | copy-start | bytes 589828
  54.9 10.2 %collective-permute-start.8 = (bf16[48,2176]{1,0:T(8,128)(2,1)S(1)}, bf16[48,2176]{1,0:T(8,128)(2,1)S(1)}, u32[]{:S(2)}, u32[]{:S(2)}) collective-permute-start(bf16[48,2176]{1,0:T(8,128)(2,1)S(1)} %fold_edges.5), channel_id=1, source_target_pairs={{0,8},{8,16},{16,24},{24,32},{32,40},{40,48},{48,56},{56,64},{64,7... | collective-permute-start | bytes 626696 | tf_op jit(solution)/shard_map/ppermute | solution.py:35

commit v5 on v4

--- a/solution.py
+++ b/solution.py
@@ -5,6 +5,7 @@
 import numpy as np
 from jax import lax
 from jax.experimental import pallas as pl
+from jax.experimental.layout import Layout, with_layout_constraint
 from jax.experimental.pallas import tpu as pltpu
 from jax.sharding import PartitionSpec as P
 
@@ -563,7 +564,7 @@
     from_up = from_behind(down, "gz", -1)
     index = (remap_source, remap_target)
     matrix = remap_matrix[0:1]
-    matrix_late = remap_matrix[1:2]
+    matrix_late = jnp.transpose(remap_matrix[1], (1, 2, 0))
     (upper,) = remap_call(0, (2,), (FOLDED,), fields, modes, matrix, *index)
     upper = fold_call(4, upper, edge_up, from_low, from_up)
     fields, modes, upper = lax.optimization_barrier((fields, modes, upper))
@@ -582,7 +583,8 @@
         name="zone_second",
     )(state, partial, *near(from_low, from_up), middle, *near(in_low, in_upper, *tables))
     from_low = from_behind(up, "gz", 1)
-    matrix = matrix_late
+    matrix_late = with_layout_constraint(matrix_late, Layout(major_to_minor=(0, 1, 2)))
+    matrix = jnp.transpose(matrix_late, (2, 0, 1))[None]
     (low,) = remap_call(1, (0,), (CAPACITY,), fields, modes, matrix, *index)
     fields, modes, low = lax.optimization_barrier((fields, modes, low))
     in_upper = from_behind(low, lines, -1)

time: 67.7 us -> 73.7 us (1.089)
  the two profiles are of different devices: /device:TPU:1 before, /device:TPU:7 now
where the time goes in v5:
time: 73.7 us; the launch traced here: 73.3 us
  Pallas kernels  30.7 us (42%)
  starting transfers between devices  18.9 us (26%)
  local copies, waits for them, and re-layouts  11.7 us (16%)
  waiting for transfers between devices  11.1 us (15%)
  between operations  0.93 us (1%)
    pallas_call x6, Pallas kernels, remap_call(): pl.pallas_call(lambda *refs: remap_kernel(step, blocks, *refs), grid=(1,)...  14 us
    ppermute x9, waiting for transfers between devices, from_behind(): lax.ppermute(shard, axis, [(i, (i + by) % size) for i in range(size)])  11.1 us
    ppermute x9, starting transfers between devices, from_behind(): lax.ppermute(shard, axis, [(i, (i + by) % size) for i in range(size)])  10.2 us
    ppermute x1, starting transfers between devices, body(): halo_c = lax.ppermute(send_c, ('gx', 'gy', 'gz'), corner)  8.66 us
    unnamed x43, local copies, waits for them, and re-layouts  7.22 us
    pallas_call x1, Pallas kernels, body(): pl.pallas_call(zone_first_kernel, in_specs=[pl.BlockSpec(memory_space=plt...  6.02 us
    pallas_call x1, Pallas kernels, body(): pl.pallas_call(zone_second_kernel, out_shape=[shape(ZONE_COUNT, WIDTH, dt...  5.14 us
    another operation x1, local copies, waits for them, and re-layouts, body(): with_layout_constraint(matrix_late, Layout(major_to_minor=(0, 1, 2)))  3.3 us
  transfers between devices with their start and end apart: 10, of which 4 were waited for; matrix products, arithmetic and copies ran while one was open for 9% of the time, Pallas kernels for 17%

profile of v5, /device:TPU:7, one launch (start us, length us, event | category | flops | bytes accessed | tf_op | source)
XLA Modules:
  0.0 73.3 jit_solution(439655636093908328)
XLA Ops:
  0.6 1.1 %pack_halo.1 = (f32[4,4,1024]{2,1,0:T(4,128)S(1)}, f32[4,4,1024]{2,1,0:T(4,128)S(1)}, f32[4,1,1024]{2,1,0:T(1,128)S(1)}) custom-call(f32[3,4,4,1024]{3,2,1,0:T(4,128)} %velocity_ref.3, f32[4,4,1024]{2,1,0:T(4,128)} %mass_ref.5), custom_call_target="tpu_custom_call" | custom-call | flops 1000000000 | bytes 3000000 | tf_op jit(solution)/shard_map/pack_halo/pallas_call | solution.py:524
  1.8 8.7 %collective-permute-start.2 = (f32[4,1,1024]{2,1,0:T(1,128)S(1)}, f32[4,1,1024]{2,1,0:T(1,128)S(1)}, u32[]{:S(2)}, u32[]{:S(2)}) collective-permute-start(f32[4,1,1024]{2,1,0:T(1,128)S(1)} %get-tuple-element.36), channel_id=1, source_target_pairs={{9,0},{10,1},{11,2},{12,3},{13,4},{14,5},{15,6},{8,7},{17,8},{18,9... | collective-permute-start | bytes 49160 | tf_op jit(solution)/shard_map/ppermute | solution.py:546
  11.3 1.1 %slice_bitcast_fusion = (bf16[64,64,96]{2,1,0:T(8,128)(2,1)}, bf16[1,96,64,64]{1,3,2,0:T(8,128)(2,1)S(1)}) fusion(bf16[2,96,64,64]{1,3,2,0:T(8,128)(2,1)S(1)} %copy-done.20), kind=kLoop, calls=%fused_computation | loop fusion | bytes 3145728 | tf_op jit(solution)/shard_map/transpose | solution.py:567
  12.4 2.3 %copy.21.refs_4_ = bf16[1,96,64,64]{3,2,1,0:T(8,128)(2,1)S(1)} copy(bf16[1,96,64,64]{1,3,2,0:T(8,128)(2,1)S(1)} %get-tuple-element.66) | data formatting | bytes 1572864
  15.8 6.0 %zone_first.1 = (f32[4,32,1024]{2,1,0:T(8,128)S(1)}, f32[3,32,1024]{2,1,0:T(8,128)S(1)}, f32[15,1024]{1,0:T(8,128)S(1)}, f32[15,1024]{1,0:T(8,128)S(1)}, f32[15,...) custom-call(f32[3,4,4,1024]{3,2,1,0:T(4,128)S(1)} %copy-done.4, ...), custom_call_target="tpu_custom_call" | custom-call | flops 7000000000 | bytes 21000000 | tf_op jit(solution)/shard_map/zone_first/pallas_call | solution.py:551
  21.9 1.8 %collective-permute-start.3 = (f32[15,1024]{1,0:T(8,128)S(1)}, f32[15,1024]{1,0:T(8,128)S(1)}, u32[]{:S(2)}, u32[]{:S(2)}) collective-permute-start(f32[15,1024]{1,0:T(8,128)S(1)} %get-tuple-element.39), channel_id=1, source_target_pairs={{0,1},{1,2},{2,3},{3,4},{4,5},{5,6},{6,7},{7,0},{8,9},{9,10},{10,1... | collective-permute-start | bytes 184328 | tf_op jit(solution)/shard_map/ppermute | solution.py:36
  23.7 2.3 %remap_step.6.refs_0_ = bf16[48,2176]{1,0:T(8,128)(2,1)S(1)} custom-call(bf16[256,2048]{1,0:T(8,128)(2,1)S(1)} %copy-done, bf16[128,256]{1,0:T(8,128)(2,1)S(1)} %get-tuple-element.47.refs_1_, s32[2,96]{1,0:T(2,128)S(1)} %copy-done.2, s32[2,96]{1,0:T(2,128)S(1)} %copy-done.3, bf16[1,96,64,64]{3,2,1,0:T(8,128)(2,1)S(1)} %copy.21.refs_4_), custom_call_target="tpu_custom_call" | custom-call | flops 700000000 | bytes 2100000 | tf_op jit(solution)/shard_map/remap_step/pallas_call | solution.py:484
  26.0 2.6 %collective-permute-done.4.refs_3_.upper_ref = f32[15,1024]{1,0:T(8,128)S(1)} collective-permute-done((f32[15,1024]{1,0:T(8,128)S(1)}, f32[15,1024]{1,0:T(8,128)S(1)}, u32[]{:S(2)}, u32[]{:S(2)}) %collective-permute-start.4) | collective-permute-done | bytes 61472 | tf_op jit(solution)/shard_map/ppermute | solution.py:36
  28.7 2.8 %remap_step.7.refs_0_ = bf16[48,2176]{1,0:T(8,128)(2,1)} custom-call(bf16[256,2048]{1,0:T(8,128)(2,1)S(1)} %copy-done, bf16[128,256]{1,0:T(8,128)(2,1)S(1)} %get-tuple-element.47.refs_1_, s32[2,96]{1,0:T(2,128)S(1)} %copy-done.2, s32[2,96]{1,0:T(2,128)S(1)} %copy-done.3, bf16[1,96,64,64]{3,2,1,0:T(8,128)(2,1)S(1)} %copy.21.refs_4_), custom_call_target="tpu_custom_call" | custom-call | flops 700000000 | bytes 2100000 | tf_op jit(solution)/shard_map/remap_step/pallas_call | solution.py:484
  32.2 3.0 %collective-permute-start.6 = (bf16[48,2176]{1,0:T(8,128)(2,1)}, bf16[48,2176]{1,0:T(8,128)(2,1)}, u32[]{:S(2)}, u32[]{:S(2)}) collective-permute-start(bf16[48,2176]{1,0:T(8,128)(2,1)} %fold_edges.4), channel_id=1, source_target_pairs={{0,248},{8,0},{16,8},{24,16},{32,24},{40,32},{48,40},{56,48},{64,5... | collective-permute-start | bytes 626696 | tf_op jit(solution)/shard_map/ppermute | solution.py:36
  35.1 3.3 %copy.20 = bf16[64,64,96]{1,0,2:T(8,128)(2,1)S(1)} copy(bf16[64,64,96]{2,1,0:T(8,128)(2,1)} %get-tuple-element.57) | data formatting | bytes 1572864 | tf_op jit(solution)/shard_map/layout_constraint | solution.py:586
  38.5 1.2 %copy-done.1 = bf16[256,2048]{1,0:T(8,128)(2,1)S(1)} copy-done((bf16[256,2048]{1,0:T(8,128)(2,1)S(1)}, bf16[256,2048]{1,0:T(8,128)(2,1)}, u32[]{:S(2)}) %copy-start.1) | copy-done | bytes 1048600
  39.7 2.2 %remap_step.8.middle_ref = bf16[32,2176]{1,0:T(8,128)(2,1)S(1)} custom-call(bf16[256,2048]{1,0:T(8,128)(2,1)S(1)} %copy-done.1, bf16[128,256]{1,0:T(8,128)(2,1)S(1)} %get-tuple-element.47.refs_1_, s32[2,96]{1,0:T(2,128)S(1)} %copy-done.2, s32[2,96]{1,0:T(2,128)S(1)} %copy-done.3, bf16[1,96,64,64]{3,2,1,0:T(8,128)(2,1)S(1)} %copy.21.refs_4_), custom_call_target="tpu_custom_call" | custom-call | flops 700000000 | bytes 2100000 | tf_op jit(solution)/shard_map/remap_step/pallas_call | solution.py:484
  42.0 1.5 %collective-permute-done.5.in_low_ref = bf16[48,2176]{1,0:T(8,128)(2,1)} collective-permute-done((bf16[48,2176]{1,0:T(8,128)(2,1)S(1)}, bf16[48,2176]{1,0:T(8,128)(2,1)}, u32[]{:S(2)}, u32[]{:S(2)}) %collective-permute-start.5) | collective-permute-done | bytes 208928 | tf_op jit(solution)/shard_map/ppermute | solution.py:36
  44.4 1.0 %copy-done.17 = f32[4,32,1024]{2,1,0:T(8,128)S(1)} copy-done((f32[4,32,1024]{2,1,0:T(8,128)S(1)}, f32[4,32,1024]{2,1,0:T(8,128)}, u32[]{:S(2)}) %copy-start.17) | copy-done | bytes 524312
  46.5 5.1 %zone_second.1 = (bf16[256,2048]{1,0:T(8,128)(2,1)S(1)}, f32[3,32,1024]{2,1,0:T(8,128)S(1)}, f32[3,32,1024]{2,1,0:T(8,128)S(1)}, f32[15,1024]{1,0:T(8,128)S(1)},...) custom-call(f32[4,32,1024]{2,1,0:T(8,128)S(1)} %copy-done.17, f32[3,32,1024]{2,1,0:T(8,128)S(1)} %copy-done.19, ...), custom_call_target="tpu_custom_call" | custom-call | flops 7000000000 | bytes 21000000 | tf_op jit(solution)/shard_map/zone_second/pallas_call | solution.py:577
  51.6 1.5 %collective-permute-start.7 = (f32[15,1024]{1,0:T(8,128)S(1)}, f32[15,1024]{1,0:T(8,128)S(1)}, u32[]{:S(2)}, u32[]{:S(2)}) collective-permute-start(f32[15,1024]{1,0:T(8,128)S(1)} %get-tuple-element.52), channel_id=1, source_target_pairs={{0,1},{1,2},{2,3},{3,4},{4,5},{5,6},{6,7},{7,0},{8,9},{9,10},{10,1... | collective-permute-start | bytes 184328 | tf_op jit(solution)/shard_map/ppermute | solution.py:36
  53.2 2.2 %remap_step.9 = bf16[32,2176]{1,0:T(8,128)(2,1)S(1)} custom-call(bf16[256,2048]{1,0:T(8,128)(2,1)S(1)} %get-tuple-element.61.refs_0_, bf16[128,256]{1,0:T(8,128)(2,1)S(1)} %get-tuple-element.62.refs_1_, s32[2,96]{1,0:T(2,128)S(1)} %copy-done.2, s32[2,96]{1,0:T(2,128)S(1)} %copy-done.3, bf16[1,96,64,64]{3,2,1,0:T(8,128)(2,1)S(1)} %bitcast.7), custom_call_target="tpu_custom_call" | custom-call | flops 700000000 | bytes 2100000 | tf_op jit(solution)/shard_map/remap_step/pallas_call | solution.py:484
  55.3 2.8 %collective-permute-start.9 = (bf16[32,2176]{1,0:T(8,128)(2,1)S(1)}, bf16[32,2176]{1,0:T(8,128)(2,1)S(1)}, u32[]{:S(2)}, u32[]{:S(2)}) collective-permute-start(bf16[32,2176]{1,0:T(8,128)(2,1)S(1)} %remap_step.9), channel_id=1, source_target_pairs={{0,248},{8,0},{16,8},{24,16},{32,24},{40,32},{48,40},{56,48},{64,5... | collective-permute-start | bytes 417800 | tf_op jit(solution)/shard_map/ppermute | solution.py:36
  58.1 2.3 %remap_step.10.refs_0_ = bf16[48,2176]{1,0:T(8,128)(2,1)S(1)} custom-call(bf16[256,2048]{1,0:T(8,128)(2,1)S(1)} %get-tuple-element.61.refs_0_, bf16[128,256]{1,0:T(8,128)(2,1)S(1)} %get-tuple-element.62.refs_1_, s32[2,96]{1,0:T(2,128)S(1)} %copy-done.2, s32[2,96]{1,0:T(2,128)S(1)} %copy-done.3, bf16[1,96,64,64]{3,2,1,0:T(8,128)(2,1)S(1)} %bitcast.8), custom_call_target="tpu_custom_call" | custom-call | flops 700000000 | bytes 2100000 | tf_op jit(solution)/shard_map/remap_step/pallas_call | solution.py:484
  61.4 1.3 %update_nodes.1 = (f32[3,4,4,1024]{3,2,1,0:T(4,128)}, f32[3,4,4,1024]{3,2,1,0:T(4,128)}) custom-call(f32[3,4,4,1024]{3,2,1,0:T(4,128)S(1)} %copy-done.5, f32[3,4,4,1024]{3,2,1,0:T(4,128)S(1)} %copy-done.6, f32[4,4,1024]{2,1,0:T(4,128)S(1)} %copy-done.7, f32[3,32,1024]{2,1,0:T(8,128)S(1)} %get-tuple-element.50.first_ref, ...), custom_call_target="tpu_custom_call" | custom-call | flops 2500000000 | bytes 7500000 | tf_op jit(solution)/shard_map/update_nodes/pallas_call | solution.py:597
  62.7 2.2 %remap_step.11.middle_ref = bf16[32,2176]{1,0:T(8,128)(2,1)S(1)} custom-call(bf16[256,2048]{1,0:T(8,128)(2,1)S(1)} %get-tuple-element.61.refs_0_, bf16[128,256]{1,0:T(8,128)(2,1)S(1)} %get-tuple-element.62.refs_1_, s32[2,96]{1,0:T(2,128)S(1)} %copy-done.2, s32[2,96]{1,0:T(2,128)S(1)} %copy-done.3, bf16[1,96,64,64]{3,2,1,0:T(8,128)(2,1)S(1)} %bitcast.9), custom_call_target="tpu_custom_call" | custom-call | flops 700000000 | bytes 2100000 | tf_op jit(solution)/shard_map/remap_step/pallas_call | solution.py:484
  65.0 5.9 %collective-permute-done.8.in_low_ref = bf16[48,2176]{1,0:T(8,128)(2,1)S(1)} collective-permute-done((bf16[48,2176]{1,0:T(8,128)(2,1)S(1)}, bf16[48,2176]{1,0:T(8,128)(2,1)S(1)}, u32[]{:S(2)}, u32[]{:S(2)}) %collective-permute-start.8) | collective-permute-done | bytes 208928 | tf_op jit(solution)/shard_map/ppermute | solution.py:36
  70.9 2.4 %finish_step.1 = (bf16[256,2048]{1,0:T(8,128)(2,1)}, f32[3,4,4,1024]{3,2,1,0:T(4,128)}, f32[3,4,4,1024]{3,2,1,0:T(4,128)}) custom-call(f32[3,4,4,1024]{3,2,1,0:T(4,128)} %get-tuple-element.53.velocity_ref, f32[3,4,4,1024]{3,2,1,0:T(4,128)} %get-tuple-element.54.displacement_ref, ...), custom_call_target="tpu_custom_call", output_to_operand_aliasing={{1}: (0, {}), {2}: (1, {})} | custom-call | flops 3000000000 | bytes 9000000 | tf_op jit(solution)/shard_map/finish_step/pallas_call | solution.py:606
  (55 shorter events, 5.5 us)
Async XLA Ops:
  0.6 10.7 %copy-start.20 = (bf16[2,96,64,64]{1,3,2,0:T(8,128)(2,1)S(1)}, bf16[2,96,64,64]{1,3,2,0:T(8,128)(2,1)}, u32[]{:S(2)}) copy-start(bf16[2,96,64,64]{1,3,2,0:T(8,128)(2,1)} %param.15) | copy-start | bytes 4718596
  1.8 13.0 %collective-permute-start.2 = (f32[4,1,1024]{2,1,0:T(1,128)S(1)}, f32[4,1,1024]{2,1,0:T(1,128)S(1)}, u32[]{:S(2)}, u32[]{:S(2)}) collective-permute-start(f32[4,1,1024]{2,1,0:T(1,128)S(1)} %get-tuple-element.36), channel_id=1, source_target_pairs={{9,0},{10,1},{11,2},{12,3},{13,4},{14,5},{15,6},{8,7},{17,8},{18,9... | collective-permute-start | bytes 49160 | tf_op jit(solution)/shard_map/ppermute | solution.py:546
  10.4 4.4 %collective-permute-start = (f32[4,4,1024]{2,1,0:T(4,128)S(1)}, f32[4,4,1024]{2,1,0:T(4,128)S(1)}, u32[]{:S(2)}, u32[]{:S(2)}) collective-permute-start(f32[4,4,1024]{2,1,0:T(4,128)S(1)} %get-tuple-element.34), channel_id=1, source_target_pairs={{0,248},{8,0},{16,8},{24,16},{32,24},{40,32},{48,40},{56,48},{64,5... | collective-permute-start | bytes 196616 | tf_op jit(solution)/shard_map/ppermute | solution.py:36
  10.9 4.9 %collective-permute-start.1 = (f32[4,4,1024]{2,1,0:T(4,128)S(1)}, f32[4,4,1024]{2,1,0:T(4,128)S(1)}, u32[]{:S(2)}, u32[]{:S(2)}) collective-permute-start(f32[4,4,1024]{2,1,0:T(4,128)S(1)} %get-tuple-element.35), channel_id=1, source_target_pairs={{0,7},{1,0},{2,1},{3,2},{4,3},{5,4},{6,5},{7,6},{8,15},{9,8},{10,9... | collective-permute-start | bytes 196616 | tf_op jit(solution)/shard_map/ppermute | solution.py:36
  12.4 3.4 %copy-start.4 = (f32[3,4,4,1024]{3,2,1,0:T(4,128)S(1)}, f32[3,4,4,1024]{3,2,1,0:T(4,128)}, u32[]{:S(2)}) copy-start(f32[3,4,4,1024]{3,2,1,0:T(4,128)} %velocity_ref.3) | copy-start | bytes 589828
  12.4 3.4 %copy-start.7 = (f32[4,4,1024]{2,1,0:T(4,128)S(1)}, f32[4,4,1024]{2,1,0:T(4,128)}, u32[]{:S(2)}) copy-start(f32[4,4,1024]{2,1,0:T(4,128)} %mass_ref.5) | copy-start | bytes 196612
  14.8 8.9 %copy-start = (bf16[256,2048]{1,0:T(8,128)(2,1)S(1)}, bf16[256,2048]{1,0:T(8,128)(2,1)}, u32[]{:S(2)}) copy-start(bf16[256,2048]{1,0:T(8,128)(2,1)} %refs_0_.3) | copy-start | bytes 3145732
  14.8 8.9 %copy-start.2 = (s32[2,96]{1,0:T(2,128)S(1)}, s32[2,96]{1,0:T(2,128)}, u32[]{:S(2)}) copy-start(s32[2,96]{1,0:T(2,128)} %refs_2_.11) | copy-start | bytes 2308
  14.8 8.9 %copy-start.3 = (s32[2,96]{1,0:T(2,128)S(1)}, s32[2,96]{1,0:T(2,128)}, u32[]{:S(2)}) copy-start(s32[2,96]{1,0:T(2,128)} %refs_3_.11) | copy-start | bytes 2308
  21.9 6.8 %copy-start.16 = (f32[4,32,1024]{2,1,0:T(8,128)}, f32[4,32,1024]{2,1,0:T(8,128)S(1)}, u32[]{:S(2)}) copy-start(f32[4,32,1024]{2,1,0:T(8,128)S(1)} %get-tuple-element.37.state_ref) | copy-start | bytes 1572868
  21.9 6.8 %copy-start.18 = (f32[3,32,1024]{2,1,0:T(8,128)}, f32[3,32,1024]{2,1,0:T(8,128)S(1)}, u32[]{:S(2)}) copy-start(f32[3,32,1024]{2,1,0:T(8,128)S(1)} %get-tuple-element.38.first_ref) | copy-start | bytes 1179652
  21.9 4.1 %collective-permute-start.3 = (f32[15,1024]{1,0:T(8,128)S(1)}, f32[15,1024]{1,0:T(8,128)S(1)}, u32[]{:S(2)}, u32[]{:S(2)}) collective-permute-start(f32[15,1024]{1,0:T(8,128)S(1)} %get-tuple-element.39), channel_id=1, source_target_pairs={{0,1},{1,2},{2,3},{3,4},{4,5},{5,6},{6,7},{7,0},{8,9},{9,10},{10,1... | collective-permute-start | bytes 184328 | tf_op jit(solution)/shard_map/ppermute | solution.py:36
  23.7 4.9 %collective-permute-start.4 = (f32[15,1024]{1,0:T(8,128)S(1)}, f32[15,1024]{1,0:T(8,128)S(1)}, u32[]{:S(2)}, u32[]{:S(2)}) collective-permute-start(f32[15,1024]{1,0:T(8,128)S(1)} %get-tuple-element.40), channel_id=1, source_target_pairs={{0,7},{1,0},{2,1},{3,2},{4,3},{5,4},{6,5},{7,6},{8,15},{9,8},{10,9... | collective-permute-start | bytes 184328 | tf_op jit(solution)/shard_map/ppermute | solution.py:36
  26.0 5.5 %copy-start.8 = (f32[15,1024]{1,0:T(8,128)}, f32[15,1024]{1,0:T(8,128)S(1)}, u32[]{:S(2)}) copy-start(f32[15,1024]{1,0:T(8,128)S(1)} %collective-permute-done.3.refs_2_.low_ref) | copy-start | bytes 184324
  32.2 9.8 %collective-permute-start.6 = (bf16[48,2176]{1,0:T(8,128)(2,1)}, bf16[48,2176]{1,0:T(8,128)(2,1)}, u32[]{:S(2)}, u32[]{:S(2)}) collective-permute-start(bf16[48,2176]{1,0:T(8,128)(2,1)} %fold_edges.4), channel_id=1, source_target_pairs={{0,248},{8,0},{16,8},{24,16},{32,24},{40,32},{48,40},{56,48},{64,5... | collective-permute-start | bytes 626696 | tf_op jit(solution)/shard_map/ppermute | solution.py:36
  35.1 8.4 %collective-permute-start.5 = (bf16[48,2176]{1,0:T(8,128)(2,1)S(1)}, bf16[48,2176]{1,0:T(8,128)(2,1)}, u32[]{:S(2)}, u32[]{:S(2)}) collective-permute-start(bf16[48,2176]{1,0:T(8,128)(2,1)S(1)} %fold_edges.3), channel_id=1, source_target_pairs={{0,8},{8,16},{16,24},{24,32},{32,40},{40,48},{48,56},{56,64},{64,7... | collective-permute-start | bytes 626696 | tf_op jit(solution)/shard_map/ppermute | solution.py:36
  39.7 3.8 %copy-start.9 = (f32[15,1024]{1,0:T(8,128)S(1)}, f32[15,1024]{1,0:T(8,128)}, u32[]{:S(2)}) copy-start(f32[15,1024]{1,0:T(8,128)} %copy-done.8) | copy-start | bytes 184324
  39.7 3.8 %copy-start.11 = (f32[15,1024]{1,0:T(8,128)S(1)}, f32[15,1024]{1,0:T(8,128)}, u32[]{:S(2)}) copy-start(f32[15,1024]{1,0:T(8,128)} %copy-done.10) | copy-start | bytes 184324
  39.7 3.8 %copy-start.12 = (bf16[1536,480]{1,0:T(8,128)(2,1)S(1)}, bf16[1536,480]{1,0:T(8,128)(2,1)}, u32[]{:S(2)}) copy-start(bf16[1536,480]{1,0:T(8,128)(2,1)} %constant.8.clone.grad_hbm.grad_ref) | copy-start | bytes 4423684
  39.7 3.8 %copy-start.13 = (bf16[320,1536]{1,0:T(8,128)(2,1)S(1)}, bf16[320,1536]{1,0:T(8,128)(2,1)}, u32[]{:S(2)}) copy-start(bf16[320,1536]{1,0:T(8,128)(2,1)} %constant.9.clone.force_hbm.force_ref) | copy-start | bytes 2949124
  39.7 3.8 %copy-start.14 = (bf16[128,512]{1,0:T(8,128)(2,1)S(1)}, bf16[128,512]{1,0:T(8,128)(2,1)}, u32[]{:S(2)}) copy-start(bf16[128,512]{1,0:T(8,128)(2,1)} %constant.11.clone.proj_hbm.proj_ref) | copy-start | bytes 393220
  51.6 8.8 %collective-permute-start.7 = (f32[15,1024]{1,0:T(8,128)S(1)}, f32[15,1024]{1,0:T(8,128)S(1)}, u32[]{:S(2)}, u32[]{:S(2)}) collective-permute-start(f32[15,1024]{1,0:T(8,128)S(1)} %get-tuple-element.52), channel_id=1, source_target_pairs={{0,1},{1,2},{2,3},{3,4},{4,5},{5,6},{6,7},{7,0},{8,9},{9,10},{10,1... | collective-permute-start | bytes 184328 | tf_op jit(solution)/shard_map/ppermute | solution.py:36
  55.3 9.6 %collective-permute-start.9 = (bf16[32,2176]{1,0:T(8,128)(2,1)S(1)}, bf16[32,2176]{1,0:T(8,128)(2,1)S(1)}, u32[]{:S(2)}, u32[]{:S(2)}) collective-permute-start(bf16[32,2176]{1,0:T(8,128)(2,1)S(1)} %remap_step.9), channel_id=1, source_target_pairs={{0,248},{8,0},{16,8},{24,16},{32,24},{40,32},{48,40},{56,48},{64,5... | collective-permute-start | bytes 417800 | tf_op jit(solution)/shard_map/ppermute | solution.py:36
  60.4 10.5 %collective-permute-start.8 = (bf16[48,2176]{1,0:T(8,128)(2,1)S(1)}, bf16[48,2176]{1,0:T(8,128)(2,1)S(1)}, u32[]{:S(2)}, u32[]{:S(2)}) collective-permute-start(bf16[48,2176]{1,0:T(8,128)(2,1)S(1)} %fold_edges.5), channel_id=1, source_target_pairs={{0,8},{8,16},{16,24},{24,32},{32,40},{40,48},{48,56},{56,64},{64,7... | collective-permute-start | bytes 626696 | tf_op jit(solution)/shard_map/ppermute | solution.py:36
  (7 other events, 9.0 us)

commit v6 on v4

--- a/solution.py
+++ b/solution.py
@@ -564,12 +564,10 @@
     index = (remap_source, remap_target)
     matrix = remap_matrix[0:1]
     matrix_late = remap_matrix[1:2]
-    (upper,) = remap_call(0, (2,), (FOLDED,), fields, modes, matrix, *index)
+    low, upper = remap_call(0, (0, 2), (FOLDED, FOLDED), fields, modes, matrix, *index)
     upper = fold_call(4, upper, edge_up, from_low, from_up)
-    fields, modes, upper = lax.optimization_barrier((fields, modes, upper))
+    low = fold_call(0, low, edge_down, from_low, from_up)
     in_low = from_behind(upper, lines, 1)
-    (low,) = remap_call(0, (0,), (FOLDED,), fields, modes, matrix, *index)
-    low = fold_call(0, low, edge_down, from_low, from_up)
     fields, modes, low, matrix_late = lax.optimization_barrier((fields, modes, low, matrix_late))
     in_upper = from_behind(low, lines, -1)
     (middle,) = remap_call(0, (1,), (CAPACITY,), fields, modes, matrix, *index)

time: 67.7 us -> 70.7 us (1.044)
  the two profiles are of different devices: /device:TPU:1 before, /device:TPU:7 now
where the time goes in v6:
time: 70.7 us; the launch traced here: 70.5 us
  Pallas kernels  28.9 us (41%)
  starting transfers between devices  24.3 us (34%)
  waiting for transfers between devices  8.99 us (13%)
  local copies, waits for them, and re-layouts  7.46 us (11%)
  between operations  0.91 us (1%)
    ppermute x9, starting transfers between devices, from_behind(): lax.ppermute(shard, axis, [(i, (i + by) % size) for i in range(size)])  15.6 us
    pallas_call x5, Pallas kernels, remap_call(): pl.pallas_call(lambda *refs: remap_kernel(step, blocks, *refs), grid=(1,)...  12.8 us
    ppermute x9, waiting for transfers between devices, from_behind(): lax.ppermute(shard, axis, [(i, (i + by) % size) for i in range(size)])  8.99 us
    ppermute x1, starting transfers between devices, body(): halo_c = lax.ppermute(send_c, ('gx', 'gy', 'gz'), corner)  8.66 us
    pallas_call x1, Pallas kernels, body(): pl.pallas_call(zone_first_kernel, in_specs=[pl.BlockSpec(memory_space=plt...  6.18 us
    pallas_call x1, Pallas kernels, body(): pl.pallas_call(zone_second_kernel, out_shape=[shape(ZONE_COUNT, WIDTH, dt...  4.28 us
    unnamed x23, local copies, waits for them, and re-layouts  3.98 us
    pallas_call x1, Pallas kernels, body(): pl.pallas_call(finish_kernel, grid=(1,), in_specs=[bottom, bottom, whole(...  2.36 us
  transfers between devices with their start and end apart: 10, of which 3 were waited for; matrix products, arithmetic and copies ran while one was open for 10% of the time, Pallas kernels for 20%

profile of v6, /device:TPU:7, one launch (start us, length us, event | category | flops | bytes accessed | tf_op | source)
XLA Modules:
  0.0 70.5 jit_solution(4323968953769546829)
XLA Ops:
  0.6 1.8 %pack_halo.1 = (f32[4,4,1024]{2,1,0:T(4,128)}, f32[4,4,1024]{2,1,0:T(4,128)}, f32[4,1,1024]{2,1,0:T(1,128)}) custom-call(f32[3,4,4,1024]{3,2,1,0:T(4,128)} %velocity_ref.3, f32[4,4,1024]{2,1,0:T(4,128)} %mass_ref.5), custom_call_target="tpu_custom_call" | custom-call | flops 1000000000 | bytes 3000000 | tf_op jit(solution)/shard_map/pack_halo/pallas_call | solution.py:523
  2.4 8.7 %collective-permute-start.2 = (f32[4,1,1024]{2,1,0:T(1,128)}, f32[4,1,1024]{2,1,0:T(1,128)S(1)}, u32[]{:S(2)}, u32[]{:S(2)}) collective-permute-start(f32[4,1,1024]{2,1,0:T(1,128)} %get-tuple-element.35), channel_id=1, source_target_pairs={{9,0},{10,1},{11,2},{12,3},{13,4},{14,5},{15,6},{8,7},{17,8},{18,9... | collective-permute-start | bytes 49160 | tf_op jit(solution)/shard_map/ppermute | solution.py:545
  11.1 0.5 collective-permute-start
  11.9 1.1 %fusion = (bf16[1,96,64,64]{1,3,2,0:T(8,128)(2,1)S(1)}, bf16[1,96,64,64]{1,3,2,0:T(8,128)(2,1)}) fusion(bf16[2,96,64,64]{1,3,2,0:T(8,128)(2,1)S(1)} %copy-done.10), kind=kLoop, calls=%fused_computation | loop fusion | bytes 3145728 | tf_op jit(solution)/shard_map/slice | solution.py:566
  13.1 2.3 %copy.22.refs_4_ = bf16[1,96,64,64]{3,2,1,0:T(8,128)(2,1)S(1)} copy(bf16[1,96,64,64]{1,3,2,0:T(8,128)(2,1)S(1)} %get-tuple-element.63) | data formatting | bytes 1572864 | tf_op jit(solution)/shard_map/optimization_barrier | solution.py:571
  15.4 3.3 %copy.21.refs_4_.refs_5_ = bf16[1,96,64,64]{3,2,1,0:T(8,128)(2,1)S(1)} copy(bf16[1,96,64,64]{1,3,2,0:T(8,128)(2,1)} %get-tuple-element.64) | data formatting | bytes 1572864
  18.9 6.2 %zone_first.1 = (f32[4,32,1024]{2,1,0:T(8,128)S(1)}, f32[3,32,1024]{2,1,0:T(8,128)S(1)}, f32[15,1024]{1,0:T(8,128)S(1)}, f32[15,1024]{1,0:T(8,128)S(1)}, f32[15,...) custom-call(f32[3,4,4,1024]{3,2,1,0:T(4,128)S(1)} %copy-done.3, ...), custom_call_target="tpu_custom_call" | custom-call | flops 7000000000 | bytes 21000000 | tf_op jit(solution)/shard_map/zone_first/pallas_call | solution.py:550
  25.1 2.6 %collective-permute-start.3 = (f32[15,1024]{1,0:T(8,128)S(1)}, f32[15,1024]{1,0:T(8,128)S(1)}, u32[]{:S(2)}, u32[]{:S(2)}) collective-permute-start(f32[15,1024]{1,0:T(8,128)S(1)} %get-tuple-element.38), channel_id=1, source_target_pairs={{0,1},{1,2},{2,3},{3,4},{4,5},{5,6},{6,7},{7,0},{8,9},{9,10},{10,1... | collective-permute-start | bytes 184328 | tf_op jit(solution)/shard_map/ppermute | solution.py:35
  27.7 3.9 %remap_step.5 = (bf16[48,2176]{1,0:T(8,128)(2,1)S(1)}, bf16[48,2176]{1,0:T(8,128)(2,1)S(1)}) custom-call(bf16[256,2048]{1,0:T(8,128)(2,1)S(1)} %copy-done, bf16[128,256]{1,0:T(8,128)(2,1)S(1)} %get-tuple-element.44.refs_1_, s32[2,96]{1,0:T(2,128)S(1)} %copy-done.1, s32[2,96]{1,0:T(2,128)S(1)} %copy-done.2, bf16[1,96,64,64]{3,2,1,0:T(8,128)(2,1)S(1)} %copy.21.refs_4_.refs_5_, ...), custom_call_target="tpu_custom_call" | custom-call | flops 700000000 | bytes 2100000 | tf_op jit(solution)/shard_map/remap_step/pallas_call | solution.py:483
  31.7 0.9 %collective-permute-done.4.refs_3_.upper_ref = f32[15,1024]{1,0:T(8,128)S(1)} collective-permute-done((f32[15,1024]{1,0:T(8,128)S(1)}, f32[15,1024]{1,0:T(8,128)S(1)}, u32[]{:S(2)}, u32[]{:S(2)}) %collective-permute-start.4) | collective-permute-done | bytes 61472 | tf_op jit(solution)/shard_map/ppermute | solution.py:35
  32.7 1.3 %collective-permute-start.5 = (bf16[48,2176]{1,0:T(8,128)(2,1)S(1)}, bf16[48,2176]{1,0:T(8,128)(2,1)S(1)}, u32[]{:S(2)}, u32[]{:S(2)}) collective-permute-start(bf16[48,2176]{1,0:T(8,128)(2,1)S(1)} %fold_edges.4), channel_id=1, source_target_pairs={{0,8},{8,16},{16,24},{24,32},{32,40},{40,48},{48,56},{56,64},{64,7... | collective-permute-start | bytes 626696 | tf_op jit(solution)/shard_map/ppermute | solution.py:35
  34.0 3.8 %collective-permute-start.6 = (bf16[48,2176]{1,0:T(8,128)(2,1)S(1)}, bf16[48,2176]{1,0:T(8,128)(2,1)S(1)}, u32[]{:S(2)}, u32[]{:S(2)}) collective-permute-start(bf16[48,2176]{1,0:T(8,128)(2,1)S(1)} %fold_edges.3), channel_id=1, source_target_pairs={{0,248},{8,0},{16,8},{24,16},{32,24},{40,32},{48,40},{56,48},{64,5... | collective-permute-start | bytes 626696 | tf_op jit(solution)/shard_map/ppermute | solution.py:35
  37.8 2.2 %remap_step.6.middle_ref = bf16[32,2176]{1,0:T(8,128)(2,1)S(1)} custom-call(bf16[256,2048]{1,0:T(8,128)(2,1)S(1)} %copy-done, bf16[128,256]{1,0:T(8,128)(2,1)S(1)} %get-tuple-element.44.refs_1_, s32[2,96]{1,0:T(2,128)S(1)} %copy-done.1, s32[2,96]{1,0:T(2,128)S(1)} %copy-done.2, bf16[1,96,64,64]{3,2,1,0:T(8,128)(2,1)S(1)} %copy.21.refs_4_.refs_5_), custom_call_target="tpu_custom_call" | custom-call | flops 700000000 | bytes 2100000 | tf_op jit(solution)/shard_map/remap_step/pallas_call | solution.py:483
  40.0 2.4 %collective-permute-done.5.in_low_ref = bf16[48,2176]{1,0:T(8,128)(2,1)S(1)} collective-permute-done((bf16[48,2176]{1,0:T(8,128)(2,1)S(1)}, bf16[48,2176]{1,0:T(8,128)(2,1)S(1)}, u32[]{:S(2)}, u32[]{:S(2)}) %collective-permute-start.5) | collective-permute-done | bytes 208928 | tf_op jit(solution)/shard_map/ppermute | solution.py:35
  42.5 4.3 %zone_second.1 = (bf16[256,2048]{1,0:T(8,128)(2,1)S(1)}, f32[3,32,1024]{2,1,0:T(8,128)S(1)}, f32[3,32,1024]{2,1,0:T(8,128)S(1)}, f32[15,1024]{1,0:T(8,128)S(1)},...) custom-call(f32[4,32,1024]{2,1,0:T(8,128)S(1)} %get-tuple-element.36.state_ref, ...), custom_call_target="tpu_custom_call" | custom-call | flops 7000000000 | bytes 21000000 | tf_op jit(solution)/shard_map/zone_second/pallas_call | solution.py:574
  46.8 1.7 %collective-permute-start.7 = (f32[15,1024]{1,0:T(8,128)S(1)}, f32[15,1024]{1,0:T(8,128)S(1)}, u32[]{:S(2)}, u32[]{:S(2)}) collective-permute-start(f32[15,1024]{1,0:T(8,128)S(1)} %get-tuple-element.50), channel_id=1, source_target_pairs={{0,1},{1,2},{2,3},{3,4},{4,5},{5,6},{6,7},{7,0},{8,9},{9,10},{10,1... | collective-permute-start | bytes 184328 | tf_op jit(solution)/shard_map/ppermute | solution.py:35
  48.5 2.2 %remap_step.7 = bf16[32,2176]{1,0:T(8,128)(2,1)S(1)} custom-call(bf16[256,2048]{1,0:T(8,128)(2,1)S(1)} %get-tuple-element.59.refs_0_, bf16[128,256]{1,0:T(8,128)(2,1)S(1)} %get-tuple-element.60.refs_1_, s32[2,96]{1,0:T(2,128)S(1)} %copy-done.1, s32[2,96]{1,0:T(2,128)S(1)} %copy-done.2, bf16[1,96,64,64]{3,2,1,0:T(8,128)(2,1)S(1)} %copy.22.refs_4_), custom_call_target="tpu_custom_call" | custom-call | flops 700000000 | bytes 2100000 | tf_op jit(solution)/shard_map/remap_step/pallas_call | solution.py:483
  50.6 5.1 %collective-permute-start.9 = (bf16[32,2176]{1,0:T(8,128)(2,1)S(1)}, bf16[32,2176]{1,0:T(8,128)(2,1)S(1)}, u32[]{:S(2)}, u32[]{:S(2)}) collective-permute-start(bf16[32,2176]{1,0:T(8,128)(2,1)S(1)} %remap_step.7), channel_id=1, source_target_pairs={{0,248},{8,0},{16,8},{24,16},{32,24},{40,32},{48,40},{56,48},{64,5... | collective-permute-start | bytes 417800 | tf_op jit(solution)/shard_map/ppermute | solution.py:35
  55.8 2.3 %remap_step.8.refs_0_ = bf16[48,2176]{1,0:T(8,128)(2,1)S(1)} custom-call(bf16[256,2048]{1,0:T(8,128)(2,1)S(1)} %get-tuple-element.59.refs_0_, bf16[128,256]{1,0:T(8,128)(2,1)S(1)} %get-tuple-element.60.refs_1_, s32[2,96]{1,0:T(2,128)S(1)} %copy-done.1, s32[2,96]{1,0:T(2,128)S(1)} %copy-done.2, bf16[1,96,64,64]{3,2,1,0:T(8,128)(2,1)S(1)} %copy.22.refs_4_), custom_call_target="tpu_custom_call" | custom-call | flops 700000000 | bytes 2100000 | tf_op jit(solution)/shard_map/remap_step/pallas_call | solution.py:483
  58.4 0.6 copy-done.4
  59.0 1.3 %update_nodes.1 = (f32[3,4,4,1024]{3,2,1,0:T(4,128)}, f32[3,4,4,1024]{3,2,1,0:T(4,128)}) custom-call(f32[3,4,4,1024]{3,2,1,0:T(4,128)S(1)} %copy-done.3, f32[3,4,4,1024]{3,2,1,0:T(4,128)S(1)} %copy-done.4, f32[4,4,1024]{2,1,0:T(4,128)S(1)} %copy-done.5, f32[3,32,1024]{2,1,0:T(8,128)S(1)} %get-tuple-element.48.first_ref, ...), custom_call_target="tpu_custom_call" | custom-call | flops 2500000000 | bytes 7500000 | tf_op jit(solution)/shard_map/update_nodes/pallas_call | solution.py:593
  60.3 2.2 %remap_step.9.middle_ref = bf16[32,2176]{1,0:T(8,128)(2,1)S(1)} custom-call(bf16[256,2048]{1,0:T(8,128)(2,1)S(1)} %get-tuple-element.59.refs_0_, bf16[128,256]{1,0:T(8,128)(2,1)S(1)} %get-tuple-element.60.refs_1_, s32[2,96]{1,0:T(2,128)S(1)} %copy-done.1, s32[2,96]{1,0:T(2,128)S(1)} %copy-done.2, bf16[1,96,64,64]{3,2,1,0:T(8,128)(2,1)S(1)} %copy.22.refs_4_), custom_call_target="tpu_custom_call" | custom-call | flops 700000000 | bytes 2100000 | tf_op jit(solution)/shard_map/remap_step/pallas_call | solution.py:483
  62.5 5.6 %collective-permute-done.8.in_low_ref = bf16[48,2176]{1,0:T(8,128)(2,1)S(1)} collective-permute-done((bf16[48,2176]{1,0:T(8,128)(2,1)S(1)}, bf16[48,2176]{1,0:T(8,128)(2,1)S(1)}, u32[]{:S(2)}, u32[]{:S(2)}) %collective-permute-start.8) | collective-permute-done | bytes 208928 | tf_op jit(solution)/shard_map/ppermute | solution.py:35
  68.2 2.4 %finish_step.1 = (bf16[256,2048]{1,0:T(8,128)(2,1)}, f32[3,4,4,1024]{3,2,1,0:T(4,128)}, f32[3,4,4,1024]{3,2,1,0:T(4,128)}) custom-call(f32[3,4,4,1024]{3,2,1,0:T(4,128)} %get-tuple-element.51.velocity_ref, f32[3,4,4,1024]{3,2,1,0:T(4,128)} %get-tuple-element.52.displacement_ref, ...), custom_call_target="tpu_custom_call", output_to_operand_aliasing={{1}: (0, {}), {2}: (1, {})} | custom-call | flops 3000000000 | bytes 9000000 | tf_op jit(solution)/shard_map/finish_step/pallas_call | solution.py:602
  (34 shorter events, 0.9 us)
Async XLA Ops:
  0.6 11.3 %copy-start.10 = (bf16[2,96,64,64]{1,3,2,0:T(8,128)(2,1)S(1)}, bf16[2,96,64,64]{1,3,2,0:T(8,128)(2,1)}, u32[]{:S(2)}) copy-start(bf16[2,96,64,64]{1,3,2,0:T(8,128)(2,1)} %param.15) | copy-start | bytes 4718596
  2.4 16.4 %collective-permute-start.2 = (f32[4,1,1024]{2,1,0:T(1,128)}, f32[4,1,1024]{2,1,0:T(1,128)S(1)}, u32[]{:S(2)}, u32[]{:S(2)}) collective-permute-start(f32[4,1,1024]{2,1,0:T(1,128)} %get-tuple-element.35), channel_id=1, source_target_pairs={{9,0},{10,1},{11,2},{12,3},{13,4},{14,5},{15,6},{8,7},{17,8},{18,9... | collective-permute-start | bytes 49160 | tf_op jit(solution)/shard_map/ppermute | solution.py:545
  11.1 7.8 %collective-permute-start = (f32[4,4,1024]{2,1,0:T(4,128)}, f32[4,4,1024]{2,1,0:T(4,128)S(1)}, u32[]{:S(2)}, u32[]{:S(2)}) collective-permute-start(f32[4,4,1024]{2,1,0:T(4,128)} %get-tuple-element.33), channel_id=1, source_target_pairs={{0,248},{8,0},{16,8},{24,16},{32,24},{40,32},{48,40},{56,48},{64,5... | collective-permute-start | bytes 196616 | tf_op jit(solution)/shard_map/ppermute | solution.py:35
  11.6 7.3 %collective-permute-start.1 = (f32[4,4,1024]{2,1,0:T(4,128)}, f32[4,4,1024]{2,1,0:T(4,128)S(1)}, u32[]{:S(2)}, u32[]{:S(2)}) collective-permute-start(f32[4,4,1024]{2,1,0:T(4,128)} %get-tuple-element.34), channel_id=1, source_target_pairs={{0,7},{1,0},{2,1},{3,2},{4,3},{5,4},{6,5},{7,6},{8,15},{9,8},{10,9... | collective-permute-start | bytes 196616 | tf_op jit(solution)/shard_map/ppermute | solution.py:35
  15.4 3.4 %copy-start.3 = (f32[3,4,4,1024]{3,2,1,0:T(4,128)S(1)}, f32[3,4,4,1024]{3,2,1,0:T(4,128)}, u32[]{:S(2)}) copy-start(f32[3,4,4,1024]{3,2,1,0:T(4,128)} %velocity_ref.3) | copy-start | bytes 589828
  15.4 3.4 %copy-start.5 = (f32[4,4,1024]{2,1,0:T(4,128)S(1)}, f32[4,4,1024]{2,1,0:T(4,128)}, u32[]{:S(2)}) copy-start(f32[4,4,1024]{2,1,0:T(4,128)} %mass_ref.5) | copy-start | bytes 196612
  18.8 8.9 %copy-start = (bf16[256,2048]{1,0:T(8,128)(2,1)S(1)}, bf16[256,2048]{1,0:T(8,128)(2,1)}, u32[]{:S(2)}) copy-start(bf16[256,2048]{1,0:T(8,128)(2,1)} %refs_0_.2) | copy-start | bytes 3145732
  18.8 8.9 %copy-start.1 = (s32[2,96]{1,0:T(2,128)S(1)}, s32[2,96]{1,0:T(2,128)}, u32[]{:S(2)}) copy-start(s32[2,96]{1,0:T(2,128)} %refs_2_.9) | copy-start | bytes 2308
  18.8 8.9 %copy-start.2 = (s32[2,96]{1,0:T(2,128)S(1)}, s32[2,96]{1,0:T(2,128)}, u32[]{:S(2)}) copy-start(s32[2,96]{1,0:T(2,128)} %refs_3_.9) | copy-start | bytes 2308
  25.1 6.6 %collective-permute-start.3 = (f32[15,1024]{1,0:T(8,128)S(1)}, f32[15,1024]{1,0:T(8,128)S(1)}, u32[]{:S(2)}, u32[]{:S(2)}) collective-permute-start(f32[15,1024]{1,0:T(8,128)S(1)} %get-tuple-element.38), channel_id=1, source_target_pairs={{0,1},{1,2},{2,3},{3,4},{4,5},{5,6},{6,7},{7,0},{8,9},{9,10},{10,1... | collective-permute-start | bytes 184328 | tf_op jit(solution)/shard_map/ppermute | solution.py:35
  27.7 4.9 %collective-permute-start.4 = (f32[15,1024]{1,0:T(8,128)S(1)}, f32[15,1024]{1,0:T(8,128)S(1)}, u32[]{:S(2)}, u32[]{:S(2)}) collective-permute-start(f32[15,1024]{1,0:T(8,128)S(1)} %get-tuple-element.39), channel_id=1, source_target_pairs={{0,7},{1,0},{2,1},{3,2},{4,3},{5,4},{6,5},{7,6},{8,15},{9,8},{10,9... | collective-permute-start | bytes 184328 | tf_op jit(solution)/shard_map/ppermute | solution.py:35
  32.7 9.8 %copy-start.6 = (bf16[1536,480]{1,0:T(8,128)(2,1)S(1)}, bf16[1536,480]{1,0:T(8,128)(2,1)}, u32[]{:S(2)}) copy-start(bf16[1536,480]{1,0:T(8,128)(2,1)} %constant.8.clone.grad_hbm.grad_ref) | copy-start | bytes 4423684
  32.7 9.8 %copy-start.7 = (bf16[320,1536]{1,0:T(8,128)(2,1)S(1)}, bf16[320,1536]{1,0:T(8,128)(2,1)}, u32[]{:S(2)}) copy-start(bf16[320,1536]{1,0:T(8,128)(2,1)} %constant.9.clone.force_hbm.force_ref) | copy-start | bytes 2949124
  32.7 9.8 %copy-start.8 = (bf16[128,512]{1,0:T(8,128)(2,1)S(1)}, bf16[128,512]{1,0:T(8,128)(2,1)}, u32[]{:S(2)}) copy-start(bf16[128,512]{1,0:T(8,128)(2,1)} %constant.11.clone.proj_hbm.proj_ref) | copy-start | bytes 393220
  32.7 9.8 %copy-start.9 = (bf16[512,128]{1,0:T(8,128)(2,1)S(1)}, bf16[512,128]{1,0:T(8,128)(2,1)}, u32[]{:S(2)}) copy-start(bf16[512,128]{1,0:T(8,128)(2,1)} %constant.10.clone.inter_hbm.inter_ref) | copy-start | bytes 393220
  32.7 9.7 %collective-permute-start.5 = (bf16[48,2176]{1,0:T(8,128)(2,1)S(1)}, bf16[48,2176]{1,0:T(8,128)(2,1)S(1)}, u32[]{:S(2)}, u32[]{:S(2)}) collective-permute-start(bf16[48,2176]{1,0:T(8,128)(2,1)S(1)} %fold_edges.4), channel_id=1, source_target_pairs={{0,8},{8,16},{16,24},{24,32},{32,40},{40,48},{48,56},{56,64},{64,7... | collective-permute-start | bytes 626696 | tf_op jit(solution)/shard_map/ppermute | solution.py:35
  34.0 8.5 %collective-permute-start.6 = (bf16[48,2176]{1,0:T(8,128)(2,1)S(1)}, bf16[48,2176]{1,0:T(8,128)(2,1)S(1)}, u32[]{:S(2)}, u32[]{:S(2)}) collective-permute-start(bf16[48,2176]{1,0:T(8,128)(2,1)S(1)} %fold_edges.3), channel_id=1, source_target_pairs={{0,248},{8,0},{16,8},{24,16},{32,24},{40,32},{48,40},{56,48},{64,5... | collective-permute-start | bytes 626696 | tf_op jit(solution)/shard_map/ppermute | solution.py:35
  46.8 11.3 %collective-permute-start.7 = (f32[15,1024]{1,0:T(8,128)S(1)}, f32[15,1024]{1,0:T(8,128)S(1)}, u32[]{:S(2)}, u32[]{:S(2)}) collective-permute-start(f32[15,1024]{1,0:T(8,128)S(1)} %get-tuple-element.50), channel_id=1, source_target_pairs={{0,1},{1,2},{2,3},{3,4},{4,5},{5,6},{6,7},{7,0},{8,9},{9,10},{10,1... | collective-permute-start | bytes 184328 | tf_op jit(solution)/shard_map/ppermute | solution.py:35
  50.6 11.9 %collective-permute-start.9 = (bf16[32,2176]{1,0:T(8,128)(2,1)S(1)}, bf16[32,2176]{1,0:T(8,128)(2,1)S(1)}, u32[]{:S(2)}, u32[]{:S(2)}) collective-permute-start(bf16[32,2176]{1,0:T(8,128)(2,1)S(1)} %remap_step.7), channel_id=1, source_target_pairs={{0,248},{8,0},{16,8},{24,16},{32,24},{40,32},{48,40},{56,48},{64,5... | collective-permute-start | bytes 417800 | tf_op jit(solution)/shard_map/ppermute | solution.py:35
  58.0 0.9 %copy-start.4 = (f32[3,4,4,1024]{3,2,1,0:T(4,128)S(1)}, f32[3,4,4,1024]{3,2,1,0:T(4,128)}, u32[]{:S(2)}) copy-start(f32[3,4,4,1024]{3,2,1,0:T(4,128)} %displacement_ref.1) | copy-start | bytes 589828
  58.1 10.1 %collective-permute-start.8 = (bf16[48,2176]{1,0:T(8,128)(2,1)S(1)}, bf16[48,2176]{1,0:T(8,128)(2,1)S(1)}, u32[]{:S(2)}, u32[]{:S(2)}) collective-permute-start(bf16[48,2176]{1,0:T(8,128)(2,1)S(1)} %fold_edges.5), channel_id=1, source_target_pairs={{0,8},{8,16},{16,24},{24,32},{32,40},{40,48},{48,56},{56,64},{64,7... | collective-permute-start | bytes 626696 | tf_op jit(solution)/shard_map/ppermute | solution.py:35
